TPU v7x, 32 devices: a whole 2x2x4 slice. The times are simulated.
32 devices in a mesh: row: 4 (over z), col: 8 (over y, x, core).
Axes of the slice: x: 2, y: 2, z: 4, core: 2. Of those that a mesh axis runs over, the one named last changes fastest.
Arguments:
- hidden: bfloat16 [4096, 2048], P(('row', 'col')), may hold values from -6 to 6
- cached_lengths: int32 [4], replicated, may hold values from 1024 to 4096, as said below
- request_order: int32 [4], replicated, may hold values from 0 to 3, each once
- cache_keys: bfloat16 [4, 4096, 2048], P('row', None, 'col'), may hold values from -480 to 480
- cache_values: bfloat16 [4, 4096, 2048], P('row', None, 'col'), may hold values from -6 to 6
- attn_gain: bfloat16 [2048], replicated, may hold values from 0.5 to 1.5
- w_qkv: bfloat16 [2048, 16, 384], P(None, 'col'), may hold values from -0.125 to 0.125
- w_out: bfloat16 [2048, 2048], P('col'), may hold values from -0.125 to 0.125
- moe_gain: bfloat16 [2048], replicated, may hold values from 0.5 to 1.5
- expert_ids: int32 [4096, 6], P(('row', 'col')), may hold values from 0 to 63, all different within a row; in each aligned block of 128 rows (0 to 127, 128 to 255, ...) at most 16 rows name the same one
- gate_weights: bfloat16 [4096, 6], P(('row', 'col')), may hold values from 0.049804688 to 0.3984375
- w_in: bfloat16 [128, 2048, 1408], P(('row', 'col')), may hold values from -0.125 to 0.125
- w_down: bfloat16 [128, 704, 2048], P(('row', 'col')), may hold values from -0.15625 to 0.15625
Outputs:
- new_hidden: bfloat16 [4096, 2048], P(('row', 'col'))
- new_keys: bfloat16 [4096, 2048], P('row', 'col')
- new_values: bfloat16 [4096, 2048], P('row', 'col')
Inputs may be any that keep to these rules, and one draw needn't show every extreme that they name: `cached_lengths`: every request has at least a quarter of 4096 cached tokens, and some request has exactly 4096. `request_order`: each slot serves a different request. `expert_ids`: among the rows of one device (aligned blocks of 128 tokens) no expert is named by more than 16 rows, a bound that some block reaches.
All inputs are finite; a program needn't handle non-finite values.
Results may differ from a plain program's by a relative error of at most 0.015.
Values may be sent and summed in bfloat16 or wider, within the bound.
No kernel may reach another device: no remote copies, remote signals or barrier semaphores. Data moves between devices by JAX's collectives and lax.ppermute only.
A program may use at most 192 MiB of HBM per device.

v0:
```python
import jax
import jax.numpy as jnp
from jax import lax
from jax.sharding import PartitionSpec as P

EXPERTS = 64
WINDOW = 4096
SINKS = 4
CAP = 16


EPS = 1e-06
THETA = 10000.0


def rms_scale(matrix, scaling):
    values = matrix.astype(jnp.float32)
    factor = lax.rsqrt(jnp.mean(values * values, axis=-1, keepdims=True) + EPS)
    return values * factor * scaling.astype(jnp.float32)


def rotate(vectors, positions):
    half_width = vectors.shape[-1] // 2
    frequency = THETA ** (-2.0 * jnp.arange(half_width, dtype=jnp.float32) / vectors.shape[-1])
    angles = positions.astype(jnp.float32)[..., None] * frequency
    cosine = jnp.cos(angles)[..., None, :]
    sine_part = jnp.sin(angles)[..., None, :]
    leading = vectors[..., :half_width]
    trailing = vectors[..., half_width:]
    return jnp.concatenate(
        [leading * cosine - trailing * sine_part, trailing * cosine + leading * sine_part], axis=-1
    )


def attend(queries, key_rows, value_rows, key_places, key_valid, query_places):
    scores = jnp.einsum(
        "nhe,mhe->hnm", queries, key_rows, preferred_element_type=jnp.float32
    ) * queries.shape[-1] ** (-0.5)
    distance = query_places[:, None] - key_places[None, :]
    allowed = (
        key_valid[None, :] & (distance >= 0) & ((distance < WINDOW) | (key_places[None, :] < SINKS))
    )
    scores = jnp.where(allowed[None], scores, -1e30)
    highest = jnp.max(scores, axis=-1, keepdims=True)
    weights = jnp.exp(scores - highest)
    shares = (weights / jnp.sum(weights, axis=-1, keepdims=True)).astype(jnp.bfloat16)
    return jnp.einsum(
        "hnm,mhe->nhe", shares, value_rows, preferred_element_type=jnp.float32
    ).astype(jnp.bfloat16)


def body(
    hidden,
    cached_lengths,
    request_order,
    cache_keys,
    cache_values,
    attn_gain,
    w_qkv,
    w_out,
    moe_gain,
    expert_ids,
    gate_weights,
    w_in,
    w_down,
):
    tok_rows, model_width = hidden.shape
    heads_here = w_qkv.shape[1]
    head_width = w_qkv.shape[2] // 3
    normed = rms_scale(hidden, attn_gain).astype(jnp.bfloat16)
    qkv_matrix = w_qkv.reshape(model_width, heads_here * 3 * head_width)
    projected = jnp.dot(
        lax.all_gather(normed, "col", axis=0, tiled=True),
        qkv_matrix,
        preferred_element_type=jnp.float32,
    )
    new_rows = projected.shape[0]
    projected = projected.reshape(new_rows, heads_here, 3, head_width)
    row_index = lax.axis_index("row")
    places = jnp.arange(request_order.shape[0], dtype=jnp.int32)
    request = jnp.sum(jnp.where(places == row_index, request_order, 0))
    length = jnp.sum(jnp.where(places == request, cached_lengths, 0))
    query_pos = length + jnp.arange(new_rows, dtype=jnp.int32)
    queries = rotate(projected[:, :, 0], query_pos).astype(jnp.bfloat16)
    fresh_keys = rotate(projected[:, :, 1], query_pos).astype(jnp.bfloat16)
    fresh_values = projected[:, :, 2].astype(jnp.bfloat16)
    cache_rows = cache_keys.shape[1]
    cache_places = jnp.arange(cache_rows, dtype=jnp.int32)
    keys_all = jnp.concatenate(
        [cache_keys[0].reshape(cache_rows, heads_here, head_width), fresh_keys], axis=0
    )
    values_all = jnp.concatenate(
        [cache_values[0].reshape(cache_rows, heads_here, head_width), fresh_values], axis=0
    )
    key_places = jnp.concatenate([cache_places, query_pos])
    key_valid = jnp.concatenate([cache_places < length, jnp.ones((new_rows,), jnp.bool_)])
    block_rows = min(512, new_rows)
    query_blocks = queries.reshape(new_rows // block_rows, block_rows, heads_here, head_width)
    position_blocks = query_pos.reshape(new_rows // block_rows, block_rows)

    def one_block(operands):
        block_queries, block_places = operands
        return attend(block_queries, keys_all, values_all, key_places, key_valid, block_places)

    context = lax.map(one_block, (query_blocks, position_blocks)).reshape(
        new_rows, heads_here * head_width
    )
    attention = lax.psum_scatter(
        jnp.dot(context, w_out, preferred_element_type=jnp.float32).astype(jnp.bfloat16),
        "col",
        scatter_dimension=0,
        tiled=True,
    ).astype(jnp.float32)
    residual = hidden.astype(jnp.float32) + attention
    moe_in = rms_scale(residual, moe_gain).astype(jnp.bfloat16)
    top_count = expert_ids.shape[1]
    flat_ids = expert_ids.reshape(-1)
    onehot = (flat_ids[:, None] == jnp.arange(EXPERTS, dtype=jnp.int32)[None, :]).astype(jnp.int32)
    slot_rank = jnp.sum((jnp.cumsum(onehot, axis=0) - onehot) * onehot, axis=1)
    slot_index = flat_ids * CAP + slot_rank
    owners = jnp.arange(flat_ids.shape[0], dtype=jnp.int32) // top_count
    slot_table = jnp.full((EXPERTS * CAP,), tok_rows, jnp.int32).at[slot_index].set(owners)
    padded = jnp.concatenate([moe_in, jnp.zeros((1, model_width), jnp.bfloat16)], axis=0)
    routed_rows = padded[slot_table]
    row_count = lax.axis_size("row")
    col_count = lax.axis_size("col")
    device_count = row_count * col_count
    per_device = w_in.shape[0]
    half_units = w_down.shape[1]
    outgoing = routed_rows.reshape(EXPERTS, 1, CAP, model_width)
    outgoing = jnp.broadcast_to(outgoing, (EXPERTS, 2, CAP, model_width))
    sending = outgoing.reshape(device_count, per_device, CAP, model_width)
    both_parts = jnp.einsum(
        "shcd,hdf->shcf",
        lax.all_to_all(sending, ("row", "col"), split_axis=0, concat_axis=0, tiled=True),
        w_in,
        preferred_element_type=jnp.float32,
    )
    activated = (jax.nn.silu(both_parts[..., :half_units]) * both_parts[..., half_units:]).astype(
        jnp.bfloat16
    )
    results = jnp.einsum("shcf,hfd->shcd", activated, w_down, preferred_element_type=jnp.float32)
    returned = lax.all_to_all(
        results.astype(jnp.bfloat16), ("row", "col"), split_axis=0, concat_axis=0, tiled=True
    ).astype(results.dtype)
    flat_returned = returned.reshape(EXPERTS * 2 * CAP, model_width)
    half_ids = jnp.arange(2, dtype=jnp.int32)
    gather_index = (flat_ids[:, None] * 2 + half_ids[None, :]) * CAP + slot_rank[:, None]
    picked = flat_returned[gather_index.reshape(-1)].reshape(tok_rows, top_count, 2, model_width)
    part_rows = (picked[:, :, 0] + picked[:, :, 1]).astype(jnp.bfloat16)
    expert_sum = jnp.einsum(
        "tk,tkd->td", gate_weights, part_rows, preferred_element_type=jnp.float32
    )
    new_hidden = (residual + expert_sum).astype(jnp.bfloat16)
    new_keys = fresh_keys.reshape(new_rows, heads_here * head_width)
    new_values = fresh_values.reshape(new_rows, heads_here * head_width)
    return (new_hidden, new_keys, new_values)


def solution(mesh):
    in_specs = (
        P(("row", "col"), None),
        P(),
        P(),
        P("row", None, "col"),
        P("row", None, "col"),
        P(),
        P(None, "col", None),
        P("col", None),
        P(),
        P(("row", "col"), None),
        P(("row", "col"), None),
        P(("row", "col"), None, None),
        P(("row", "col"), None, None),
    )
    out_specs = (P(("row", "col"), None), P("row", "col"), P("row", "col"))
    return jax.shard_map(body, mesh=mesh, in_specs=in_specs, out_specs=out_specs, check_vma=False)
```

profile of v0, /device:TPU:0, one launch (start us, length us, event | category | flops | bytes accessed | tf_op | source)
XLA Modules:
  0.0 759.2 jit_solution(14790934212152108399)
XLA Ops:
  14.3 4.1 copy.48
  18.4 4.3 copy.75
  22.7 4.7 copy.43
  33.3 17.6 %all-gather.2.cloned.1.call-done = bf16[1024,2048]{1,0:T(8,128)(2,1)} async-done(((bf16[128,2048]{1,0:T(8,128)(2,1)}), bf16[1024,2048]{1,0:T(8,128)(2,1)}) %all-gather.2.cloned.1.call-update) | async-done | bytes 4194320 | tf_op jit(solution)/shard_map/all_gather | solution.py:73
  50.9 6.2 fusion.31
  61.9 4.4 copy.50
  78.7 4.4 copy.49
  84.6 101.7 %while.10 = (s32[]{:T(128)}, bf16[2,512,2,128]{3,2,1,0:T(2,128)(2,1)}, pred[5120]{0:T(1024)(128)(4,1)S(1)}, s32[2,512]{1,0:T(2,128)S(1)}, s32[5120]{0:T(1024)S(1...) while((s32[]{:T(128)}, ...), condition=%wide.region_6.7_spmd, body=%wide.region_3.6_spmd.sunk | while | flops 2742167552 | bytes 99685544 | solution.py:105
  84.8 3.6 fusion.78
  88.4 10.3 %fusion.77 = f32[2,512,5120]{2,1,0:T(8,128)} fusion(bf16[5120,2,128]{2,0,1:T(8,128)(2,1)} %get-tuple-element.178, bf16[2,512,2,128]{3,1,2,0:T(8,128)(2,1)S(1)} %get-tuple-element.177, s32[]{:T(128)S(6)} %copy.103), kind=kOutput, calls=%fused_computation.20.clone.1 | convolution fusion | flops 1342177280 | bytes 23855108 | tf_op jit(solution)/shard_map/while/body/eval_jaxpr/nhe,mhe->hnm/dot_general | solution.py:36
  98.8 25.0 %fusion.79 = (f32[2,512]{1,0:T(2,128)S(1)}, f32[2,512,5120]{2,1,0:T(8,128)}) fusion(f32[2,512,5120]{2,1,0:T(8,128)} %fusion.77, pred[512,5120]{1,0:T(8,128)(4,1)S(1)} %fusion.78), kind=kOutput, calls=%fused_computation.113.clone.1 | output fusion | flops 31462400 | bytes 44568576 | tf_op jit(solution)/shard_map/while/body/eval_jaxpr/sub | solution.py:45
  123.8 10.7 %fusion.80 = bf16[1,512,2,128]{3,1,2,0:T(8,128)(2,1)S(1)} fusion(bf16[5120,2,128]{2,0,1:T(8,128)(2,1)} %get-tuple-element.179, f32[2,512,5120]{2,1,0:T(8,128)} %get-tuple-element.152, f32[2,512]{1,0:T(2,128)S(1)} %get-tuple-element.153), kind=kOutput, calls=%fused_computation.18.clone.1 | convolution fusion | flops 1352794112 | bytes 23859200 | tf_op jit(solution)/shard_map/while/body/eval_jaxpr/hnm,mhe->nhe/dot_general | solution.py:47
  135.6 3.6 fusion.78
  139.2 10.3 %fusion.77 = f32[2,512,5120]{2,1,0:T(8,128)} fusion(bf16[5120,2,128]{2,0,1:T(8,128)(2,1)} %get-tuple-element.178, bf16[2,512,2,128]{3,1,2,0:T(8,128)(2,1)S(1)} %get-tuple-element.177, s32[]{:T(128)S(6)} %copy.103), kind=kOutput, calls=%fused_computation.20.clone.1 | convolution fusion | flops 1342177280 | bytes 23855108 | tf_op jit(solution)/shard_map/while/body/eval_jaxpr/nhe,mhe->hnm/dot_general | solution.py:36
  149.5 25.0 %fusion.79 = (f32[2,512]{1,0:T(2,128)S(1)}, f32[2,512,5120]{2,1,0:T(8,128)}) fusion(f32[2,512,5120]{2,1,0:T(8,128)} %fusion.77, pred[512,5120]{1,0:T(8,128)(4,1)S(1)} %fusion.78), kind=kOutput, calls=%fused_computation.113.clone.1 | output fusion | flops 31462400 | bytes 44568576 | tf_op jit(solution)/shard_map/while/body/eval_jaxpr/sub | solution.py:45
  174.5 10.7 %fusion.80 = bf16[1,512,2,128]{3,1,2,0:T(8,128)(2,1)S(1)} fusion(bf16[5120,2,128]{2,0,1:T(8,128)(2,1)} %get-tuple-element.179, f32[2,512,5120]{2,1,0:T(8,128)} %get-tuple-element.152, f32[2,512]{1,0:T(2,128)S(1)} %get-tuple-element.153), kind=kOutput, calls=%fused_computation.18.clone.1 | convolution fusion | flops 1352794112 | bytes 23859200 | tf_op jit(solution)/shard_map/while/body/eval_jaxpr/hnm,mhe->nhe/dot_general | solution.py:47
  186.3 4.3 convolution_convert_fusion
  193.6 3.8 scatter_custom_fusion
  197.4 44.7 %reduce-scatter.2.cloned.1.call-done = bf16[128,2048]{1,0:T(8,128)(2,1)} async-done(((bf16[1024,2048]{1,0:T(8,128)(2,1)}), bf16[128,2048]{1,0:T(8,128)(2,1)}) %reduce-scatter.2.cloned.1.call-update) | async-done | bytes 524304 | tf_op jit(solution)/shard_map/reduce_scatter | solution.py:108
  244.8 6.1 gather_fusion
  250.8 6.8 broadcast_in_dim.43
  257.6 188.2 %all_to_all.10 = bf16[32,4,16,2048]{3,2,1,0:T(8,128)(2,1)} all-to-all(bf16[32,4,16,2048]{3,2,1,0:T(8,128)(2,1)} %bitcast.105), channel_id=1, replica_groups=mesh['row'=4,'col'=8] {'row','col'}, dimensions={0} | all-to-all | bytes 16777216 | tf_op jit(solution)/shard_map/all_to_all | solution.py:135
  445.8 21.2 %fusion.22 = f32[32,4,16,1408]{3,2,0,1:T(8,128)} fusion(bf16[4,2048,1408]{2,1,0:T(8,128)(2,1)} %param.26, bf16[32,4,16,2048]{3,2,1,0:T(8,128)(2,1)} %all_to_all.10), kind=kOutput, calls=%fused_computation.35 | convolution fusion | flops 11811160064 | bytes 42991616 | tf_op jit(solution)/shard_map/shcd,hdf->shcf/dot_general | solution.py:133
  467.0 15.5 %convert_bitcast_fusion = bf16[32,4,16,2048]{3,2,0,1:T(8,128)(2,1)} fusion(bf16[4,704,2048]{2,1,0:T(8,128)(2,1)} %param.27, f32[32,4,16,1408]{3,2,0,1:T(8,128)} %fusion.22), kind=kOutput, calls=%fused_computation.34 | convolution fusion | flops 5918425088 | bytes 32505856 | tf_op jit(solution)/shard_map/shcf,hfd->shcd/dot_general | solution.py:142
  482.5 8.3 %copy.57 = bf16[32,4,16,2048]{3,2,1,0:T(8,128)(2,1)} copy(bf16[32,4,16,2048]{3,2,0,1:T(8,128)(2,1)} %convert_bitcast_fusion) | data formatting | bytes 16777216 | tf_op jit(solution)/shard_map/convert_element_type | solution.py:144
  490.7 4.0 all-to-all-start.1
  498.8 182.0 %all-to-all-done.1 = bf16[32,4,16,2048]{3,2,1,0:T(8,128)(2,1)} async-done(((bf16[32,4,16,2048]{3,2,1,0:T(8,128)(2,1)}), bf16[32,4,16,2048]{3,2,1,0:T(8,128)(2,1)}, u32[]{:S(2)}, u32[]{:S(2)}) %all-to-all-start.1) | async-done | bytes 8388640 | tf_op jit(solution)/shard_map/all_to_all | solution.py:143
  680.8 11.2 %bitcast_convert_fusion = f32[2048,2048]{1,0:T(8,128)} fusion(bf16[32,4,16,2048]{3,2,1,0:T(8,128)(2,1)} %all-to-all-done.1), kind=kLoop, calls=%fused_computation.32 | loop fusion | flops 4194304 | bytes 25165824 | tf_op jit(solution)/shard_map/reshape | solution.py:146
  692.0 18.3 %gather_fusion.1 = f32[1536,2048]{1,0:T(8,128)} fusion(f32[2048,2048]{1,0:T(8,128)} %bitcast_convert_fusion, s32[2048]{0:T(1024)S(1)} %pad_clamp_fusion), kind=kCustom, calls=%fused_computation.1 | custom fusion | bytes 25171968 | tf_op jit(solution)/shard_map/gather | solution.py:149
  710.3 15.3 %reshape.296 = f32[128,6,2,2048]{3,2,1,0:T(2,128)} reshape(f32[1536,2048]{1,0:T(8,128)} %gather_fusion.1) | data formatting | bytes 25165824 | tf_op jit(solution)/shard_map/reshape | solution.py:149
  725.6 15.6 %fusion.61 = (f32[128,6,1,2048]{3,2,1,0:T(1,128)S(1)}, f32[128,6,1,2048]{3,2,1,0:T(1,128)S(1)}) fusion(f32[128,6,2,2048]{3,2,1,0:T(2,128)} %reshape.296), kind=kLoop, calls=%fused_computation.114 | loop fusion | bytes 25165824 | tf_op jit(solution)/shard_map/slice | solution.py:150
  741.1 7.2 fusion.35
  (100 shorter events, 47.2 us)
Async XLA Ops:
  7.2 179.1 %copy-start = (bf16[256,2048]{1,0:T(8,128)(2,1)S(1)}, bf16[256,2048]{1,0:T(8,128)(2,1)}, u32[]{:S(2)}) copy-start(bf16[256,2048]{1,0:T(8,128)(2,1)} %param.22) | copy-start | bytes 3145732
  7.2 43.7 %all-gather.2.cloned.1.call-start = ((), (), s32[]{:S(2)}) async-start(), calls=%async_computation.3 | async-start | bytes 4718592 | tf_op jit(solution)/shard_map/all_gather | solution.py:73
  11.3 230.8 %reduce-scatter.2.cloned.1.call-start = ((), (), s32[]{:S(2)}) async-start(), calls=%async_computation.4 | async-start | bytes 4718592 | tf_op jit(solution)/shard_map/reduce_scatter | solution.py:108
  18.4 9.0 %copy-start.12 = (s32[4]{0:T(128)S(1)}, s32[4]{0:T(128)}, u32[]{:S(2)}) copy-start(s32[4]{0:T(128)} %param.17) | copy-start | bytes 52
  18.4 9.6 %copy-start.13 = (s32[4]{0:T(128)S(1)}, s32[4]{0:T(128)}, u32[]{:S(2)}) copy-start(s32[4]{0:T(128)} %param.16) | copy-start | bytes 52
  57.1 1.7 copy-start.6
  57.1 3.1 copy-start.2
  76.2 0.8 copy-start.3
  123.8 10.7 %copy-start.7 = (bf16[2,512,2,128]{3,2,1,0:T(2,128)(2,1)S(1)}, bf16[2,512,2,128]{3,2,1,0:T(2,128)(2,1)}, u32[]{:S(2)}) copy-start(bf16[2,512,2,128]{3,2,1,0:T(2,128)(2,1)} %get-tuple-element.164) | copy-start | bytes 1572868 | tf_op jit(solution)/shard_map/while
  134.8 0.8 copy-start.8
  174.5 10.7 %copy-start.7 = (bf16[2,512,2,128]{3,2,1,0:T(2,128)(2,1)S(1)}, bf16[2,512,2,128]{3,2,1,0:T(2,128)(2,1)}, u32[]{:S(2)}) copy-start(bf16[2,512,2,128]{3,2,1,0:T(2,128)(2,1)} %get-tuple-element.164) | copy-start | bytes 1572868 | tf_op jit(solution)/shard_map/while
  185.5 0.8 copy-start.8
  186.3 4.3 copy-start.9
  186.3 4.7 copy-start.10
  186.3 55.8 %copy-start.1 = (bf16[128,2048]{1,0:T(8,128)(2,1)S(1)}, bf16[128,2048]{1,0:T(8,128)(2,1)}, u32[]{:S(2)}) copy-start(bf16[128,2048]{1,0:T(8,128)(2,1)} %param.15) | copy-start | bytes 1572868
  490.7 4.0 copy-start.11
  490.7 7.1 copy-start.4
  490.7 190.1 %all-to-all-start.1 = ((bf16[32,4,16,2048]{3,2,1,0:T(8,128)(2,1)}), bf16[32,4,16,2048]{3,2,1,0:T(8,128)(2,1)}, u32[]{:S(2)}, u32[]{:S(2)}) async-start(bf16[32,4,16,2048]{3,2,1,0:T(8,128)(2,1)} %copy.57), calls=%async_computation.2 | async-start | bytes 16777216 | tf_op jit(solution)/shard_map/all_to_all | solution.py:143
  748.3 2.6 copy-start.5
Sparse Core Ops, SparseCore 0:
  11.4 39.4 all-gather.1
  190.7 51.3 reduce-scatter.1
where the time goes:
time: 766 us; the launch traced here: 759 us
  waiting for transfers between devices  244 us (32%)
  blocking collectives  188 us (25%)
  local copies, waits for them, and re-layouts  114 us (15%)
  other arithmetic  102 us (13%)
  matrix products  91.8 us (12%)
  between operations  14.6 us (2%)
    all_to_all x1, blocking collectives, body(): lax.all_to_all(sending, ('row', 'col'), split_axis=0, concat_axis=0, tile...  188 us
    all_to_all x1, waiting for transfers between devices, body(): lax.all_to_all(results.astype(jnp.bfloat16), ('row', 'col'), split_axis=0...  182 us
    sub x2, other arithmetic, attend(): weights = jnp.exp(scores - highest)  49.9 us
    reduce_scatter x1, waiting for transfers between devices, body(): lax.psum_scatter(jnp.dot(context, w_out, preferred_element_type=jnp.float...  44.7 us
    dot_general x2, matrix products, attend(): jnp.einsum('hnm,mhe->nhe', shares, value_rows, preferred_element_type=jnp...  21.4 us
    dot_general x1, matrix products, body(): jnp.einsum('shcd,hdf->shcf', lax.all_to_all(sending, ('row', 'col'), spli...  21.2 us
    dot_general x2, matrix products, attend(): jnp.einsum('nhe,mhe->hnm', queries, key_rows, preferred_element_type=jnp....  20.7 us
    gather x1, local copies, waits for them, and re-layouts, body(): flat_returned[gather_index.reshape(-1)]  18.3 us
  transfers between devices with their start and end apart: 3, of which 3 were waited for; matrix products, arithmetic and copies ran while one was open for 4% of the time, Pallas kernels for 0%

commit v1 on v0

v1 whole, which is shorter than its diff:
```python
import functools

import jax
import jax.numpy as jnp
from jax import lax
from jax.experimental import pallas as pl
from jax.experimental.pallas import tpu as pltpu
from jax.sharding import PartitionSpec as P

EXPERTS = 64
WINDOW = 4096
SINKS = 4
CAP = 16
HEAD = 128

EPS = 1e-06
THETA = 10000.0
LOG2E = 1.4426950408889634
NEG = -1e30
MIB = 1 << 20


def rms_scale(matrix, scaling):
    values = matrix.astype(jnp.float32)
    factor = lax.rsqrt(jnp.mean(values * values, axis=-1, keepdims=True) + EPS)
    return values * factor * scaling.astype(jnp.float32)


def qkv_kernel(heads, x_ref, w_ref, cos_ref, sin_ref, q_ref, k_ref, v_ref):
    projected = jnp.dot(x_ref[...], w_ref[...], preferred_element_type=jnp.float32)
    cosine = cos_ref[...]
    sine = sin_ref[...]
    for h in range(heads):
        base = h * 3 * HEAD
        out = slice(h * HEAD, (h + 1) * HEAD)
        q = projected[:, base : base + HEAD]
        k = projected[:, base + HEAD : base + 2 * HEAD]
        q = q * cosine + pltpu.roll(q, HEAD // 2, 1) * sine
        k = k * cosine + pltpu.roll(k, HEAD // 2, 1) * sine
        q_ref[:, out] = (q * (LOG2E * HEAD**-0.5)).astype(jnp.bfloat16)
        k_ref[:, out] = k.astype(jnp.bfloat16)
        v_ref[:, out] = projected[:, base + 2 * HEAD : base + 3 * HEAD].astype(jnp.bfloat16)


def qkv_call(x, w, cosine, sine, heads, block=256):
    rows, width = x.shape
    out = jax.ShapeDtypeStruct((rows, heads * HEAD), jnp.bfloat16)
    out_spec = pl.BlockSpec((block, heads * HEAD), lambda i: (i, 0))
    return pl.pallas_call(
        functools.partial(qkv_kernel, heads),
        grid=(rows // block,),
        in_specs=[
            pl.BlockSpec((block, width), lambda i: (i, 0)),
            pl.BlockSpec(w.shape, lambda i: (0, 0)),
            pl.BlockSpec((block, HEAD), lambda i: (i, 0)),
            pl.BlockSpec((block, HEAD), lambda i: (i, 0)),
        ],
        out_specs=[out_spec] * 3,
        out_shape=[out] * 3,
        compiler_params=pltpu.CompilerParams(vmem_limit_bytes=32 * MIB),
        cost_estimate=pl.CostEstimate(
            flops=2 * rows * width * w.shape[1],
            bytes_accessed=2 * (rows * width + w.size + 3 * rows * heads * HEAD),
            transcendentals=0,
        ),
        name="qkv",
    )(x, w, cosine, sine)


def attention_kernel(heads, bq, bk, len_ref, q_ref, kc_ref, vc_ref, kn_ref, vn_ref, o_ref):
    q_start = pl.program_id(0) * bq
    length = len_ref[0]
    first = length + q_start
    last = first + bq - 1
    blocks = (length + bk - 1) // bk
    lowest = jnp.maximum(first - WINDOW + 1, 0) // bk
    inside = jnp.minimum((jnp.maximum(last - WINDOW + 1, 0) + bk - 1) // bk, blocks)
    whole = jnp.maximum(inside, length // bk)

    def update(state, keys, values, allowed):
        new_state = []
        for h in range(heads):
            m, l, acc = state[h]
            cols = slice(h * HEAD, (h + 1) * HEAD)
            s = lax.dot_general(
                q_ref[:, cols],
                keys[h],
                (((1,), (1,)), ((), ())),
                preferred_element_type=jnp.float32,
            )
            if allowed is not None:
                s = jnp.where(allowed, s, NEG)
            m_new = jnp.maximum(m, jnp.max(s, axis=1, keepdims=True))
            alpha = jnp.exp2(m - m_new)
            p = jnp.exp2(s - m_new)
            l = l * alpha + jnp.sum(p, axis=1, keepdims=True)
            acc = acc * alpha + jnp.dot(
                p.astype(jnp.bfloat16), values[h], preferred_element_type=jnp.float32
            )
            new_state.append((m_new, l, acc))
        return tuple(new_state)

    def cached(start, size):
        keys = [kc_ref[0, pl.ds(start, size), h * HEAD : (h + 1) * HEAD] for h in range(heads)]
        values = [vc_ref[0, pl.ds(start, size), h * HEAD : (h + 1) * HEAD] for h in range(heads)]
        return keys, values

    def fresh(start, size):
        keys = [kn_ref[pl.ds(start, size), h * HEAD : (h + 1) * HEAD] for h in range(heads)]
        values = [vn_ref[pl.ds(start, size), h * HEAD : (h + 1) * HEAD] for h in range(heads)]
        return keys, values

    def sink_step(j, state):
        places = lax.broadcasted_iota(jnp.int32, (bq, HEAD), 1)
        rows = lax.broadcasted_iota(jnp.int32, (bq, HEAD), 0)
        allowed = (places < SINKS) & (places < lowest * bk) & (first + rows - places >= WINDOW)
        return update(state, *cached(0, HEAD), allowed)

    def masked_step(j, state):
        start = pl.multiple_of(j * bk, bk)
        places = start + lax.broadcasted_iota(jnp.int32, (bq, bk), 1)
        rows = lax.broadcasted_iota(jnp.int32, (bq, bk), 0)
        allowed = (places < length) & ((first + rows - places < WINDOW) | (places < SINKS))
        return update(state, *cached(start, bk), allowed)

    def plain_step(j, state):
        return update(state, *cached(pl.multiple_of(j * bk, bk), bk), None)

    def fresh_step(j, state):
        return update(state, *fresh(pl.multiple_of(j * bq, bq), bq), None)

    state = tuple(
        (
            jnp.full((bq, 1), NEG, jnp.float32),
            jnp.zeros((bq, 1), jnp.float32),
            jnp.zeros((bq, HEAD), jnp.float32),
        )
        for h in range(heads)
    )
    state = lax.fori_loop(0, jnp.minimum(lowest, 1), sink_step, state)
    state = lax.fori_loop(lowest, inside, masked_step, state)
    state = lax.fori_loop(inside, whole, plain_step, state)
    state = lax.fori_loop(whole, blocks, masked_step, state)
    state = lax.fori_loop(0, pl.program_id(0), fresh_step, state)
    rows = lax.broadcasted_iota(jnp.int32, (bq, bq), 0)
    places = lax.broadcasted_iota(jnp.int32, (bq, bq), 1)
    state = update(state, *fresh(pl.multiple_of(q_start, bq), bq), places <= rows)
    for h in range(heads):
        m, l, acc = state[h]
        o_ref[:, h * HEAD : (h + 1) * HEAD] = (acc / l).astype(o_ref.dtype)


def attention_call(length, q, cache_keys, cache_values, new_keys, new_values, bq=256, bk=512):
    rows, width = q.shape
    heads = width // HEAD
    cache_rows = cache_keys.shape[1]
    bk = min(bk, cache_rows)
    fixed = lambda shape: pl.BlockSpec(shape, lambda i, n: (0,) * len(shape))
    return pl.pallas_call(
        functools.partial(attention_kernel, heads, bq, bk),
        grid_spec=pltpu.PrefetchScalarGridSpec(
            num_scalar_prefetch=1,
            grid=(rows // bq,),
            in_specs=[
                pl.BlockSpec((bq, width), lambda i, n: (i, 0)),
                fixed(cache_keys.shape),
                fixed(cache_values.shape),
                fixed(new_keys.shape),
                fixed(new_values.shape),
            ],
            out_specs=pl.BlockSpec((bq, width), lambda i, n: (i, 0)),
        ),
        out_shape=jax.ShapeDtypeStruct((rows, width), jnp.bfloat16),
        compiler_params=pltpu.CompilerParams(vmem_limit_bytes=40 * MIB),
        cost_estimate=pl.CostEstimate(
            flops=4 * rows * width * (cache_rows + rows),
            bytes_accessed=4 * (cache_rows + 2 * rows) * width,
            transcendentals=rows * heads * (cache_rows + rows),
        ),
        name="attention",
    )(length, q, cache_keys, cache_values, new_keys, new_values)


def project_kernel(x_ref, w_ref, hidden_ref, gain_ref, resid_ref, normed_ref):
    g = pl.program_id(0)
    share = jnp.dot(x_ref[0], w_ref[0], preferred_element_type=jnp.float32)
    share = share.astype(jnp.bfloat16).astype(jnp.float32)

    @pl.when(g == 0)
    def _():
        resid_ref[...] = share

    @pl.when(g > 0)
    def _():
        resid_ref[...] += share

    @pl.when(g == pl.num_programs(0) - 1)
    def _():
        resid = resid_ref[...] + hidden_ref[...].astype(jnp.float32)
        resid_ref[...] = resid
        normed_ref[...] = rms_scale(resid, gain_ref[...]).astype(jnp.bfloat16)


def project_call(x, w, hidden, gain):
    groups, rows, width = x.shape
    model = w.shape[2]
    fixed = pl.BlockSpec((rows, model), lambda g: (0, 0))
    return pl.pallas_call(
        project_kernel,
        grid=(groups,),
        in_specs=[
            pl.BlockSpec((1, rows, width), lambda g: (g, 0, 0)),
            pl.BlockSpec((1, width, model), lambda g: (g, 0, 0)),
            fixed,
            pl.BlockSpec((1, model), lambda g: (0, 0)),
        ],
        out_specs=[fixed, fixed],
        out_shape=[
            jax.ShapeDtypeStruct((rows, model), jnp.float32),
            jax.ShapeDtypeStruct((rows, model), jnp.bfloat16),
        ],
        compiler_params=pltpu.CompilerParams(vmem_limit_bytes=24 * MIB),
        cost_estimate=pl.CostEstimate(
            flops=2 * rows * model * groups * width,
            bytes_accessed=2 * (w.size + x.size) + 8 * rows * model,
            transcendentals=0,
        ),
        name="project",
    )(x, w, hidden, gain.reshape(1, model))


def expert_kernel(half, x_ref, win_ref, wdown_ref, o_ref, acc_ref):
    h = pl.program_id(1)
    senders, unused, slots, width = x_ref.shape
    x = x_ref[...].reshape(senders * slots, width)
    both = jnp.dot(x, win_ref[0], preferred_element_type=jnp.float32)
    a = both[:, :half]
    b = both[:, half:]
    act = (a / (1.0 + jnp.exp(-a)) * b).astype(jnp.bfloat16)
    part = jnp.dot(act, wdown_ref[0], preferred_element_type=jnp.float32)

    @pl.when(h == 0)
    def _():
        acc_ref[...] = part

    @pl.when(h > 0)
    def _():
        acc_ref[...] += part

    @pl.when(h == pl.num_programs(1) - 1)
    def _():
        o_ref[...] = acc_ref[...].astype(jnp.bfloat16).reshape(o_ref.shape)


def expert_call(x, w_in, w_down, halves):
    senders, experts, slots, width = x.shape
    units, model = w_down.shape[1:]
    rows = senders * slots
    block = pl.BlockSpec((senders, 1, slots, width), lambda e, h: (0, e, 0, 0))
    return pl.pallas_call(
        functools.partial(expert_kernel, units),
        grid=(experts, halves),
        in_specs=[
            block,
            pl.BlockSpec((1, width, 2 * units), lambda e, h: (e * halves + h, 0, 0)),
            pl.BlockSpec((1, units, model), lambda e, h: (e * halves + h, 0, 0)),
        ],
        out_specs=block,
        out_shape=jax.ShapeDtypeStruct(x.shape, jnp.bfloat16),
        scratch_shapes=[pltpu.VMEM((rows, model), jnp.float32)],
        compiler_params=pltpu.CompilerParams(vmem_limit_bytes=56 * MIB),
        cost_estimate=pl.CostEstimate(
            flops=6 * rows * experts * halves * width * units,
            bytes_accessed=2 * (w_in.size + w_down.size + 2 * x.size),
            transcendentals=rows * experts * halves * units,
        ),
        name="experts",
    )(x, w_in, w_down)


def body(
    hidden,
    cached_lengths,
    request_order,
    cache_keys,
    cache_values,
    attn_gain,
    w_qkv,
    w_out,
    moe_gain,
    expert_ids,
    gate_weights,
    w_in,
    w_down,
):
    tok_rows, model_width = hidden.shape
    heads_here = w_qkv.shape[1]
    row_count = lax.axis_size("row")
    col_count = lax.axis_size("col")
    device_count = row_count * col_count
    new_rows = tok_rows * col_count

    normed = rms_scale(hidden, attn_gain).astype(jnp.bfloat16)
    gathered = lax.all_gather(normed, "col", axis=0, tiled=True)
    w_out_all = lax.all_gather(w_out, "col", axis=0)

    row_index = lax.axis_index("row")
    places = jnp.arange(request_order.shape[0], dtype=jnp.int32)
    request = jnp.sum(jnp.where(places == row_index, request_order, 0))
    length = jnp.sum(jnp.where(places == request, cached_lengths, 0))
    query_pos = length + jnp.arange(new_rows, dtype=jnp.int32)
    frequency = THETA ** (-2.0 * jnp.arange(HEAD // 2, dtype=jnp.float32) / HEAD)
    angles = query_pos.astype(jnp.float32)[:, None] * frequency
    cosine, sine = jnp.cos(angles), jnp.sin(angles)
    cosine = jnp.concatenate([cosine, cosine], axis=1)
    sine = jnp.concatenate([-sine, sine], axis=1)

    queries, new_keys, new_values = qkv_call(
        gathered, w_qkv.reshape(model_width, -1), cosine, sine, heads_here
    )
    context = attention_call(
        length.reshape(1), queries, cache_keys, cache_values, new_keys, new_values
    )
    shares = lax.all_to_all(
        context.reshape(col_count, tok_rows, heads_here * HEAD), "col", 0, 0, tiled=True
    )
    residual, moe_in = project_call(shares, w_out_all, hidden, moe_gain)

    chosen = expert_ids[:, :, None] == jnp.arange(EXPERTS, dtype=jnp.int32)
    named = jnp.any(chosen, axis=1)
    gates = jnp.sum(jnp.where(chosen, gate_weights.astype(jnp.float32)[:, :, None], 0.0), axis=1)
    earlier = jnp.arange(tok_rows)[:, None] > jnp.arange(tok_rows)[None, :]
    rank = jnp.dot(
        earlier.astype(jnp.bfloat16),
        named.astype(jnp.bfloat16),
        preferred_element_type=jnp.float32,
    ).astype(jnp.int32)
    rank = jnp.where(named, rank, -1)
    place = (rank[:, :, None] == jnp.arange(CAP, dtype=jnp.int32)).reshape(tok_rows, EXPERTS * CAP)
    place_gates = jnp.where(place, jnp.repeat(gates, CAP, axis=1), 0.0).astype(jnp.bfloat16)

    per_device = w_in.shape[0]
    halves = 2 if per_device % 2 == 0 else 1
    copies = 2 // halves
    routed = lax.dot_general(
        place.astype(jnp.bfloat16),
        moe_in,
        (((0,), (0,)), ((), ())),
        preferred_element_type=jnp.float32,
    ).astype(jnp.bfloat16)
    routed = routed.reshape(EXPERTS, 1, CAP, model_width)
    routed = jnp.broadcast_to(routed, (EXPERTS, copies, CAP, model_width))
    routed = routed.reshape(device_count, per_device // halves, CAP, model_width)
    received = lax.all_to_all(routed, ("row", "col"), split_axis=0, concat_axis=0, tiled=True)
    parts = expert_call(received, w_in, w_down, halves)
    returned = lax.all_to_all(parts, ("row", "col"), split_axis=0, concat_axis=0, tiled=True)
    if copies > 1:
        returned = returned.reshape(EXPERTS, copies, CAP, model_width).astype(jnp.float32)
        returned = jnp.sum(returned, axis=1).astype(jnp.bfloat16)
    returned = returned.reshape(EXPERTS * CAP, model_width)
    expert_sum = jnp.dot(place_gates, returned, preferred_element_type=jnp.float32)
    new_hidden = (residual + expert_sum).astype(jnp.bfloat16)
    return (new_hidden, new_keys, new_values)


def solution(mesh):
    in_specs = (
        P(("row", "col"), None),
        P(),
        P(),
        P("row", None, "col"),
        P("row", None, "col"),
        P(),
        P(None, "col", None),
        P("col", None),
        P(),
        P(("row", "col"), None),
        P(("row", "col"), None),
        P(("row", "col"), None, None),
        P(("row", "col"), None, None),
    )
    out_specs = (P(("row", "col"), None), P("row", "col"), P("row", "col"))
    return jax.shard_map(body, mesh=mesh, in_specs=in_specs, out_specs=out_specs, check_vma=False)
```

time: 766 us -> 356 us (0.46)
  local copies, waits for them, and re-layouts: 114 us -> 12.5 us
  waiting for transfers between devices: 244 us -> 146 us
  other arithmetic: 102 us -> 10.1 us
  blocking collectives: 188 us -> 98.2 us
  matrix products: 91.8 us -> 5.11 us
  Pallas kernels: 0 us -> 61.2 us
    all_to_all x1, blocking collectives: 188 us -> 98.2 us  [body(): lax.all_to_all(routed, ('row', 'col'), split_axis=0, concat_axis=0, tiled...]
    dot_general x9 -> x3, matrix products: 91.8 us -> 5.11 us  [the longest x1 3.73 us: body(): jnp.dot(place_gates, returned, preferred_element_type=jnp.float32)]
    all_to_all x1 -> x2, waiting for transfers between devices: 182 us -> 109 us  [the longest x1 93.7 us: body(): lax.all_to_all(parts, ('row', 'col'), split_axis=0, concat_axis=0, tiled=...]
    pallas_call x0 -> x4, Pallas kernels: none -> 61.2 us  [the longest x1 27.6 us: expert_call(): pl.pallas_call(functools.partial(expert_kernel, units), grid=(experts, ha...]
    sub x3 -> x0, other arithmetic: 52.2 us -> none  [the longest x2 49.9 us: attend(): weights = jnp.exp(scores - highest)]
    reduce_scatter x1 -> x0, waiting for transfers between devices: 44.7 us -> none  [body(): lax.psum_scatter(jnp.dot(context, w_out, preferred_element_type=jnp.float...]
    gather x2 -> x0, local copies, waits for them, and re-layouts: 24.3 us -> none  [the longest x1 18.3 us: body(): flat_returned[gather_index.reshape(-1)]]
    all_gather x1 -> x2, waiting for transfers between devices: 17.6 us -> 37 us  [the longest x1 30.5 us: body(): gathered = lax.all_gather(normed, 'col', axis=0, tiled=True)]
  transfers between devices with their start and end apart: 3 -> 4, of which waited for: 3 -> 4; matrix products, arithmetic and copies ran while one was open for 4% -> 3% of each run, Pallas kernels for 0% -> 8%
where the time goes in v1:
time: 356 us; the launch traced here: 355 us
  waiting for transfers between devices  146 us (41%)
  blocking collectives  98.2 us (28%)
  Pallas kernels  61.2 us (17%)
  between operations  14.2 us (4%)
  local copies, waits for them, and re-layouts  12.5 us (4%)
  other arithmetic  10.1 us (3%)
  starting transfers between devices  7.44 us (2%)
  matrix products  5.11 us (1%)
    all_to_all x1, blocking collectives, body(): lax.all_to_all(routed, ('row', 'col'), split_axis=0, concat_axis=0, tiled...  98.2 us
    all_to_all x1, waiting for transfers between devices, body(): lax.all_to_all(parts, ('row', 'col'), split_axis=0, concat_axis=0, tiled=...  93.7 us
    all_gather x1, waiting for transfers between devices, body(): gathered = lax.all_gather(normed, 'col', axis=0, tiled=True)  30.5 us
    pallas_call x1, Pallas kernels, expert_call(): pl.pallas_call(functools.partial(expert_kernel, units), grid=(experts, ha...  27.6 us
    pallas_call x1, Pallas kernels, attention_call(): pl.pallas_call(functools.partial(attention_kernel, heads, bq, bk), grid_s...  25.1 us
    all_to_all x1, waiting for transfers between devices, body(): lax.all_to_all(context.reshape(col_count, tok_rows, heads_here * HEAD), '...  15.1 us
    unnamed x29, local copies, waits for them, and re-layouts  12.4 us
  transfers between devices with their start and end apart: 4, of which 4 were waited for; matrix products, arithmetic and copies ran while one was open for 3% of the time, Pallas kernels for 8%

profile of v1, /device:TPU:0, one launch (start us, length us, event | category | flops | bytes accessed | tf_op | source)
XLA Modules:
  0.0 355.1 jit_solution(11602993164844650874)
XLA Ops:
  7.2 0.7 convert_element_type.44
  7.9 1.2 fusion.2
  9.1 2.0 fusion.4
  11.2 0.7 all-gather.6.cloned.1.call-update
  12.0 2.5 copy.21
  14.5 0.6 fusion.7
  15.1 1.3 fusion.8
  16.4 0.6 add_convert_fusion
  17.1 1.9 fusion.6
  19.0 1.3 pad_maximum_fusion
  20.3 30.5 %all-gather.4.cloned.1.call-done.x_ref = bf16[1024,2048]{1,0:T(8,128)(2,1)} async-done(((bf16[128,2048]{1,0:T(8,128)(2,1)}), bf16[1024,2048]{1,0:T(8,128)(2,1)}) %all-gather.4.cloned.1.call-update) | async-done | bytes 4194320 | tf_op jit(solution)/shard_map/all_gather | solution.py:304
  50.8 1.0 copy-done.2
  51.8 1.0 copy-done.3
  52.9 2.2 copy-done.4
  55.0 4.9 %qkv.1 = (bf16[1024,256]{1,0:T(8,128)(2,1)S(1)}, bf16[1024,256]{1,0:T(8,128)(2,1)}, bf16[1024,256]{1,0:T(8,128)(2,1)}) custom-call(bf16[1024,2048]{1,0:T(8,128)(2,1)S(1)} %copy-done.4, bf16[2048,768]{1,0:T(8,128)(2,1)S(1)} %bitcast.16, f32[1024,128]{1,0:T(8,128)S(1)} %copy-done.2, f32[1024,128]{1,0:T(8,128)S(1)} %copy-done.3), custom_call_target="tpu_custom_call" | custom-call | flops 3221225472 | bytes 8912896 | tf_op jit(solution)/shard_map/qkv/pallas_call | solution.py:49
  60.0 1.1 copy-done.7
  61.1 1.1 copy-done.8
  62.1 25.1 %attention.1 = bf16[1024,256]{1,0:T(8,128)(2,1)} custom-call(s32[1]{0:T(128)} %bitcast.len_ref, bf16[1024,256]{1,0:T(8,128)(2,1)S(1)} %get-tuple-element.8.q_ref, bf16[1,4096,256]{2,1,0:T(8,128)(2,1)S(1)} %copy-done.5, bf16[1,4096,256]{2,1,0:T(8,128)(2,1)S(1)} %copy-done.6, bf16[1024,256]{1,0:T(8,128)(2,1)S(1)} %copy-done.7, bf16[1024,256]{1,0:T(8,128)(2,1)S(1)} %copy-done.8), custom_call_target="tpu_custom_call" | custom-call | flops 5368709120 | bytes 6291456 | tf_op jit(solution)/shard_map/attention/pallas_call | solution.py:159
  87.2 3.5 all-to-all-start
  90.9 0.1 fusion.1
  91.0 0.2 bitcast_compare_fusion
  91.2 15.1 %all-to-all-done.x_ref = bf16[8,128,256]{2,1,0:T(8,128)(2,1)S(1)} async-done(((bf16[8,128,256]{2,1,0:T(8,128)(2,1)}), bf16[8,128,256]{2,1,0:T(8,128)(2,1)S(1)}, u32[]{:S(2)}, u32[]{:S(2)}) %all-to-all-start) | async-done | bytes 524320 | tf_op jit(solution)/shard_map/all_to_all | solution.py:324
  106.3 6.5 %all-gather.6.cloned.1.call-done = bf16[2048,2048]{1,0:T(8,128)(2,1)} async-done(((bf16[256,2048]{1,0:T(8,128)(2,1)}), bf16[2048,2048]{1,0:T(8,128)(2,1)}) %all-gather.6.cloned.1.call-update) | async-done | bytes 8388624 | tf_op jit(solution)/shard_map/all_gather | solution.py:305
  112.8 3.4 copy-done
  116.2 3.6 %project.1 = (f32[128,2048]{1,0:T(8,128)S(1)}, bf16[128,2048]{1,0:T(8,128)(2,1)S(1)}) custom-call(bf16[8,128,256]{2,1,0:T(8,128)(2,1)S(1)} %all-to-all-done.x_ref, bf16[8,256,2048]{2,1,0:T(8,128)(2,1)S(1)} %bitcast.15, bf16[128,2048]{1,0:T(8,128)(2,1)S(1)} %copy-done.1, bf16[1,2048]{1,0:T(2,128)(2,1)S(1)} %reshape.83.gain_ref), custom_call_target="tpu_custom_call" | custom-call | flops 1073741824 | bytes 11010048 | tf_op jit(solution)/shard_map/project/pallas_call | solution.py:208
  119.8 1.2 convolution_convert_fusion
  121.1 98.2 %all_to_all.15.x_ref = bf16[32,2,16,2048]{3,2,1,0:T(8,128)(2,1)} all-to-all(bf16[32,2,16,2048]{3,2,1,0:T(8,128)(2,1)S(1)} %bitcast.17), channel_id=1, replica_groups=mesh['row'=4,'col'=8] {'row','col'}, dimensions={0} | all-to-all | bytes 8388608 | tf_op jit(solution)/shard_map/all_to_all | solution.py:354
  219.2 27.6 %experts.1 = bf16[32,2,16,2048]{3,2,1,0:T(8,128)(2,1)} custom-call(bf16[32,2,16,2048]{3,2,1,0:T(8,128)(2,1)} %all_to_all.15.x_ref, bf16[4,2048,1408]{2,1,0:T(8,128)(2,1)} %win_ref.1, bf16[4,704,2048]{2,1,0:T(8,128)(2,1)} %wdown_ref.1), custom_call_target="tpu_custom_call" | custom-call | flops 17716740096 | bytes 42991616 | tf_op jit(solution)/shard_map/experts/pallas_call | solution.py:260
  246.8 3.8 %all-to-all-start.2 = ((bf16[32,2,16,2048]{3,2,1,0:T(8,128)(2,1)}), bf16[32,2,16,2048]{3,2,1,0:T(8,128)(2,1)}, u32[]{:S(2)}, u32[]{:S(2)}) async-start(bf16[32,2,16,2048]{3,2,1,0:T(8,128)(2,1)} %experts.1), calls=%async_computation.2 | async-start | bytes 8388608 | tf_op jit(solution)/shard_map/all_to_all | solution.py:356
  250.8 0.1 select_convert_fusion
  250.9 93.7 %all-to-all-done.2 = bf16[32,2,16,2048]{3,2,1,0:T(8,128)(2,1)} async-done(((bf16[32,2,16,2048]{3,2,1,0:T(8,128)(2,1)}), bf16[32,2,16,2048]{3,2,1,0:T(8,128)(2,1)}, u32[]{:S(2)}, u32[]{:S(2)}) %all-to-all-start.2) | async-done | bytes 4194336 | tf_op jit(solution)/shard_map/all_to_all | solution.py:356
  344.6 3.7 %fusion = bf16[128,2048]{1,0:T(8,128)(2,1)} fusion(f32[128,2048]{1,0:T(8,128)S(1)} %get-tuple-element.11, bf16[128,1024]{0,1:T(8,128)(2,1)S(1)} %bitcast.19, bf16[1024,2048]{1,0:T(8,128)(2,1)} %bitcast.6), kind=kOutput, calls=%fused_computation.2 | convolution fusion | flops 537395200 | bytes 6029312 | tf_op jit(solution)/shard_map/dot_general | solution.py:361
  (33 shorter events, 0.3 us)
Async XLA Ops:
  7.2 43.6 %all-gather.4.cloned.1.call-start = ((), (), s32[]{:S(2)}) async-start(), calls=%async_computation.3 | async-start | bytes 4718592 | tf_op jit(solution)/shard_map/all_gather | solution.py:304
  11.2 3.3 copy-start.12
  11.2 4.0 %copy-start.13 = (s32[4]{0:T(128)S(1)}, s32[4]{0:T(128)}, u32[]{:S(2)}) copy-start(s32[4]{0:T(128)} %param.14) | copy-start | bytes 52
  11.2 101.6 %all-gather.6.cloned.1.call-start = ((), (), s32[]{:S(2)}) async-start(), calls=%async_computation.4 | async-start | bytes 9437184 | tf_op jit(solution)/shard_map/all_gather | solution.py:305
  50.8 1.0 copy-start.2
  51.8 1.0 copy-start.3
  52.9 2.2 copy-start.4
  55.0 4.9 %copy-start.5 = (bf16[1,4096,256]{2,1,0:T(8,128)(2,1)S(1)}, bf16[1,4096,256]{2,1,0:T(8,128)(2,1)}, u32[]{:S(2)}) copy-start(bf16[1,4096,256]{2,1,0:T(8,128)(2,1)} %kc_ref.1) | copy-start | bytes 6291460
  55.0 4.9 %copy-start.6 = (bf16[1,4096,256]{2,1,0:T(8,128)(2,1)S(1)}, bf16[1,4096,256]{2,1,0:T(8,128)(2,1)}, u32[]{:S(2)}) copy-start(bf16[1,4096,256]{2,1,0:T(8,128)(2,1)} %vc_ref.1) | copy-start | bytes 6291460
  59.9 1.1 copy-start.7
  61.1 1.1 copy-start.8
  62.1 28.6 %copy-start.10 = (bf16[2048]{0:T(1024)(128)(2,1)S(1)}, bf16[2048]{0:T(1024)(128)(2,1)}, u32[]{:S(2)}) copy-start(bf16[2048]{0:T(1024)(128)(2,1)} %param.21) | copy-start | bytes 12292
  62.1 28.7 %copy-start.9 = (s32[128,6]{0,1:T(8,128)S(1)}, s32[128,6]{0,1:T(8,128)}, u32[]{:S(2)}) copy-start(s32[128,6]{0,1:T(8,128)} %param.22) | copy-start | bytes 9220
  62.1 50.7 %copy-start.1 = (bf16[128,2048]{1,0:T(8,128)(2,1)S(1)}, bf16[128,2048]{1,0:T(8,128)(2,1)}, u32[]{:S(2)}) copy-start(bf16[128,2048]{1,0:T(8,128)(2,1)} %hidden_ref.1) | copy-start | bytes 1572868
  87.2 19.1 %all-to-all-start = ((bf16[8,128,256]{2,1,0:T(8,128)(2,1)}), bf16[8,128,256]{2,1,0:T(8,128)(2,1)S(1)}, u32[]{:S(2)}, u32[]{:S(2)}) async-start(bf16[8,128,256]{2,1,0:T(8,128)(2,1)} %bitcast.1), calls=%async_computation | async-start | bytes 1048576 | tf_op jit(solution)/shard_map/all_to_all | solution.py:324
  112.8 3.4 copy-start
  246.8 3.9 %copy-start.11 = (bf16[128,6]{0,1:T(8,128)(2,1)S(1)}, bf16[128,6]{0,1:T(8,128)(2,1)}, u32[]{:S(2)}) copy-start(bf16[128,6]{0,1:T(8,128)(2,1)} %param.23) | copy-start | bytes 4612
  246.8 97.7 %all-to-all-start.2 = ((bf16[32,2,16,2048]{3,2,1,0:T(8,128)(2,1)}), bf16[32,2,16,2048]{3,2,1,0:T(8,128)(2,1)}, u32[]{:S(2)}, u32[]{:S(2)}) async-start(bf16[32,2,16,2048]{3,2,1,0:T(8,128)(2,1)} %experts.1), calls=%async_computation.2 | async-start | bytes 8388608 | tf_op jit(solution)/shard_map/all_to_all | solution.py:356
Sparse Core Ops, SparseCore 0:
  11.3 39.4 all-gather.3
  52.7 60.1 all-gather.5

commit v2 on v1

--- a/solution.py
+++ b/solution.py
@@ -26,7 +26,8 @@
     return values * factor * scaling.astype(jnp.float32)
 
 
-def qkv_kernel(heads, x_ref, w_ref, cos_ref, sin_ref, q_ref, k_ref, v_ref):
+def qkv_kernel(heads, order_ref, x_ref, w_ref, cos_ref, sin_ref, *refs):
+    q_ref, k_ref, v_ref = refs[-3:]
     projected = jnp.dot(x_ref[...], w_ref[...], preferred_element_type=jnp.float32)
     cosine = cos_ref[...]
     sine = sin_ref[...]
@@ -42,29 +43,37 @@
         v_ref[:, out] = projected[:, base + 2 * HEAD : base + 3 * HEAD].astype(jnp.bfloat16)
 
 
-def qkv_call(x, w, cosine, sine, heads, block=256):
+def qkv_call(order, x, w, cosine, sine, heads, before=()):
     rows, width = x.shape
-    out = jax.ShapeDtypeStruct((rows, heads * HEAD), jnp.bfloat16)
-    out_spec = pl.BlockSpec((block, heads * HEAD), lambda i: (i, 0))
+    total = cosine.shape[0]
+    block = rows // order.shape[0]
+    out = jax.ShapeDtypeStruct((total, heads * HEAD), jnp.bfloat16)
+    placed = lambda i, n: (n[i], 0)
+    out_spec = pl.BlockSpec((block, heads * HEAD), placed)
     return pl.pallas_call(
         functools.partial(qkv_kernel, heads),
-        grid=(rows // block,),
-        in_specs=[
-            pl.BlockSpec((block, width), lambda i: (i, 0)),
-            pl.BlockSpec(w.shape, lambda i: (0, 0)),
-            pl.BlockSpec((block, HEAD), lambda i: (i, 0)),
-            pl.BlockSpec((block, HEAD), lambda i: (i, 0)),
-        ],
-        out_specs=[out_spec] * 3,
+        grid_spec=pltpu.PrefetchScalarGridSpec(
+            num_scalar_prefetch=1,
+            grid=(rows // block,),
+            in_specs=[
+                pl.BlockSpec((block, width), lambda i, n: (i, 0)),
+                pl.BlockSpec(w.shape, lambda i, n: (0, 0)),
+                pl.BlockSpec((block, HEAD), placed),
+                pl.BlockSpec((block, HEAD), placed),
+            ]
+            + [pl.BlockSpec(memory_space=pl.ANY)] * len(before),
+            out_specs=[out_spec] * 3,
+        ),
         out_shape=[out] * 3,
-        compiler_params=pltpu.CompilerParams(vmem_limit_bytes=32 * MIB),
+        input_output_aliases={5 + i: i for i in range(len(before))},
+        compiler_params=pltpu.CompilerParams(vmem_limit_bytes=24 * MIB),
         cost_estimate=pl.CostEstimate(
             flops=2 * rows * width * w.shape[1],
             bytes_accessed=2 * (rows * width + w.size + 3 * rows * heads * HEAD),
             transcendentals=0,
         ),
         name="qkv",
-    )(x, w, cosine, sine)
+    )(order, x, w, cosine, sine, *before)
 
 
 def attention_kernel(heads, bq, bk, len_ref, q_ref, kc_ref, vc_ref, kn_ref, vn_ref, o_ref):
@@ -181,40 +190,43 @@
     )(length, q, cache_keys, cache_values, new_keys, new_values)
 
 
-def project_kernel(x_ref, w_ref, hidden_ref, gain_ref, resid_ref, normed_ref):
+def project_kernel(parts, order_ref, *refs):
+    x_refs, w_refs = refs[:parts], refs[parts : 2 * parts]
+    hidden_ref, gain_ref, resid_ref, normed_ref = refs[2 * parts :]
     g = pl.program_id(0)
-    share = jnp.dot(x_ref[0], w_ref[0], preferred_element_type=jnp.float32)
-    share = share.astype(jnp.bfloat16).astype(jnp.float32)
 
     @pl.when(g == 0)
     def _():
-        resid_ref[...] = share
-
-    @pl.when(g > 0)
-    def _():
-        resid_ref[...] += share
+        resid_ref[...] = hidden_ref[...].astype(jnp.float32)
+
+    for x_ref, w_ref in zip(x_refs, w_refs):
+        share = jnp.dot(x_ref[0], w_ref[0], preferred_element_type=jnp.float32)
+        resid_ref[...] += share.astype(jnp.bfloat16).astype(jnp.float32)
 
     @pl.when(g == pl.num_programs(0) - 1)
     def _():
-        resid = resid_ref[...] + hidden_ref[...].astype(jnp.float32)
-        resid_ref[...] = resid
-        normed_ref[...] = rms_scale(resid, gain_ref[...]).astype(jnp.bfloat16)
-
-
-def project_call(x, w, hidden, gain):
+        normed_ref[...] = rms_scale(resid_ref[...], gain_ref[...]).astype(jnp.bfloat16)
+
+
+def project_call(order, x, weights, hidden, gain):
     groups, rows, width = x.shape
-    model = w.shape[2]
-    fixed = pl.BlockSpec((rows, model), lambda g: (0, 0))
+    parts = len(weights)
+    steps, unused, model = weights[0].shape
+    fixed = pl.BlockSpec((rows, model), lambda g, n: (0, 0))
+
+    def share_spec(part):
+        return pl.BlockSpec((1, rows, width), lambda g, n: (n[g * parts + part], 0, 0))
+
     return pl.pallas_call(
-        project_kernel,
-        grid=(groups,),
-        in_specs=[
-            pl.BlockSpec((1, rows, width), lambda g: (g, 0, 0)),
-            pl.BlockSpec((1, width, model), lambda g: (g, 0, 0)),
-            fixed,
-            pl.BlockSpec((1, model), lambda g: (0, 0)),
-        ],
-        out_specs=[fixed, fixed],
+        functools.partial(project_kernel, parts),
+        grid_spec=pltpu.PrefetchScalarGridSpec(
+            num_scalar_prefetch=1,
+            grid=(steps,),
+            in_specs=[share_spec(part) for part in range(parts)]
+            + [pl.BlockSpec((1, width, model), lambda g, n: (g, 0, 0))] * parts
+            + [fixed, pl.BlockSpec((1, model), lambda g, n: (0, 0))],
+            out_specs=[fixed, fixed],
+        ),
         out_shape=[
             jax.ShapeDtypeStruct((rows, model), jnp.float32),
             jax.ShapeDtypeStruct((rows, model), jnp.bfloat16),
@@ -222,18 +234,23 @@
         compiler_params=pltpu.CompilerParams(vmem_limit_bytes=24 * MIB),
         cost_estimate=pl.CostEstimate(
             flops=2 * rows * model * groups * width,
-            bytes_accessed=2 * (w.size + x.size) + 8 * rows * model,
+            bytes_accessed=2 * groups * (width * model + rows * width) + 8 * rows * model,
             transcendentals=0,
         ),
         name="project",
-    )(x, w, hidden, gain.reshape(1, model))
-
-
-def expert_kernel(half, x_ref, win_ref, wdown_ref, o_ref, acc_ref):
+    )(order, *[x] * parts, *weights, hidden, gain.reshape(1, model))
+
+
+def expert_kernel(half, counts, resident, *refs):
+    x_refs = refs[: len(counts)]
+    win_ref, wdown_ref = refs[len(counts) : len(counts) + 2]
+    o_refs, acc_ref = refs[len(counts) + 2 : -1], refs[-1]
     h = pl.program_id(1)
-    senders, unused, slots, width = x_ref.shape
-    x = x_ref[...].reshape(senders * slots, width)
-    both = jnp.dot(x, win_ref[0], preferred_element_type=jnp.float32)
+    width = x_refs[0].shape[-1]
+    x = [ref[...].reshape(-1, width) for ref in x_refs]
+    x = x[0] if len(x) == 1 else jnp.concatenate(x, axis=0)
+    at = pl.program_id(0) * pl.num_programs(1) + h if resident else 0
+    both = jnp.dot(x, win_ref[at], preferred_element_type=jnp.float32)
     a = both[:, :half]
     b = both[:, half:]
     act = (a / (1.0 + jnp.exp(-a)) * b).astype(jnp.bfloat16)
@@ -249,33 +266,211 @@
 
     @pl.when(h == pl.num_programs(1) - 1)
     def _():
-        o_ref[...] = acc_ref[...].astype(jnp.bfloat16).reshape(o_ref.shape)
-
-
-def expert_call(x, w_in, w_down, halves):
-    senders, experts, slots, width = x.shape
+        start = 0
+        for ref in o_refs:
+            size = ref.shape[0] * ref.shape[2]
+            ref[...] = acc_ref[start : start + size].astype(jnp.bfloat16).reshape(ref.shape)
+            start += size
+
+
+def expert_call(xs, takes, outs, w_in, w_down, halves, resident=False):
+    unused, unused, slots, width = xs[0].shape
+    experts = w_in.shape[0] // halves
     units, model = w_down.shape[1:]
-    rows = senders * slots
-    block = pl.BlockSpec((senders, 1, slots, width), lambda e, h: (0, e, 0, 0))
+    rows = sum(takes) * slots
+    block = lambda senders: pl.BlockSpec((senders, 1, slots, width), lambda e, h: (0, e, 0, 0))
+    weight_specs = [
+        pl.BlockSpec((1, width, 2 * units), lambda e, h: (e * halves + h, 0, 0)),
+        pl.BlockSpec((1, units, model), lambda e, h: (e * halves + h, 0, 0)),
+    ]
+    if resident:
+        weight_specs[0] = pl.BlockSpec(memory_space=pltpu.VMEM)
     return pl.pallas_call(
-        functools.partial(expert_kernel, units),
+        functools.partial(expert_kernel, units, takes, resident),
         grid=(experts, halves),
-        in_specs=[
-            block,
-            pl.BlockSpec((1, width, 2 * units), lambda e, h: (e * halves + h, 0, 0)),
-            pl.BlockSpec((1, units, model), lambda e, h: (e * halves + h, 0, 0)),
+        in_specs=[block(senders) for senders in takes] + weight_specs,
+        out_specs=[block(senders) for senders in outs],
+        out_shape=[
+            jax.ShapeDtypeStruct((senders, experts, slots, width), jnp.bfloat16) for senders in outs
         ],
-        out_specs=block,
-        out_shape=jax.ShapeDtypeStruct(x.shape, jnp.bfloat16),
         scratch_shapes=[pltpu.VMEM((rows, model), jnp.float32)],
-        compiler_params=pltpu.CompilerParams(vmem_limit_bytes=56 * MIB),
+        compiler_params=pltpu.CompilerParams(vmem_limit_bytes=(24 if resident else 56) * MIB),
         cost_estimate=pl.CostEstimate(
             flops=6 * rows * experts * halves * width * units,
-            bytes_accessed=2 * (w_in.size + w_down.size + 2 * x.size),
+            bytes_accessed=2 * (w_in.size + w_down.size + 2 * rows * experts * width),
             transcendentals=rows * experts * halves * units,
         ),
         name="experts",
-    )(x, w_in, w_down)
+    )(*xs, w_in, w_down)
+
+
+def xor_pairs(count, bits):
+    return [(i, i ^ bits) for i in range(count)]
+
+
+def gather_plane(block, later):
+    rows = block.shape[0]
+    along_x = lax.ppermute(block, "col", xor_pairs(8, 2))
+    along_y = lax.ppermute(block, "col", xor_pairs(8, 4))
+    along_x, along_y, later = lax.optimization_barrier((along_x, along_y, later))
+    across_0 = lax.ppermute(along_x[: rows // 2], "col", xor_pairs(8, 4))
+    across_1 = lax.ppermute(along_y[rows // 2 :], "col", xor_pairs(8, 2))
+    mine = jnp.concatenate([block, along_x, along_y, across_0, across_1], axis=0)
+    return mine, lax.ppermute(mine, "col", xor_pairs(8, 1)), later
+
+
+def slot_places(ids, gates, experts):
+    rows = ids.shape[-2]
+    chosen = ids[..., None] == experts
+    named = jnp.any(chosen, axis=-2)
+    weight = jnp.sum(jnp.where(chosen, gates[..., None], 0.0), axis=-2)
+    earlier = jnp.arange(rows)[:, None] > jnp.arange(rows)[None, :]
+    rank = jnp.einsum(
+        "ij,...je->...ie",
+        earlier.astype(jnp.bfloat16),
+        named.astype(jnp.bfloat16),
+        preferred_element_type=jnp.float32,
+    ).astype(jnp.int32)
+    rank = jnp.where(named, rank, -1)
+    place = rank[..., None] == jnp.arange(CAP, dtype=jnp.int32)
+    gated = jnp.where(place, weight[..., None], 0.0).astype(jnp.bfloat16)
+    flat = ids.shape[:-1] + (experts.shape[0] * CAP,)
+    return place.reshape(flat).astype(jnp.bfloat16), gated.reshape(flat)
+
+
+def route(place, rows):
+    return lax.dot_general(
+        place, rows, (((0,), (0,)), ((), ())), preferred_element_type=jnp.float32
+    ).astype(jnp.bfloat16)
+
+
+def experts_direct(moe_in, residual, expert_ids, gate_weights, w_in, w_down):
+    tok_rows, model_width = moe_in.shape
+    device_count = lax.axis_size("row") * lax.axis_size("col")
+    place, place_gates = slot_places(
+        expert_ids, gate_weights.astype(jnp.float32), jnp.arange(EXPERTS, dtype=jnp.int32)
+    )
+    per_device = w_in.shape[0]
+    halves = 2 if per_device % 2 == 0 else 1
+    copies = 2 // halves
+    routed = route(place, moe_in).reshape(EXPERTS, 1, CAP, model_width)
+    routed = jnp.broadcast_to(routed, (EXPERTS, copies, CAP, model_width))
+    routed = routed.reshape(device_count, per_device // halves, CAP, model_width)
+    received = lax.all_to_all(routed, ("row", "col"), split_axis=0, concat_axis=0, tiled=True)
+    (parts,) = expert_call([received], [device_count], [device_count], w_in, w_down, halves)
+    returned = lax.all_to_all(parts, ("row", "col"), split_axis=0, concat_axis=0, tiled=True)
+    if copies > 1:
+        returned = returned.reshape(EXPERTS, copies, CAP, model_width).astype(jnp.float32)
+        returned = jnp.sum(returned, axis=1).astype(jnp.bfloat16)
+    returned = returned.reshape(EXPERTS * CAP, model_width)
+    expert_sum = jnp.dot(place_gates, returned, preferred_element_type=jnp.float32)
+    return (residual + expert_sum).astype(jnp.bfloat16)
+
+
+def plane_places(expert_ids, gate_weights):
+    row, col = lax.axis_index("row"), lax.axis_index("col")
+    packed = jnp.concatenate(
+        [expert_ids.astype(jnp.float32), gate_weights.astype(jnp.float32)], axis=1
+    )
+    one, two, three = [lax.ppermute(packed, "row", xor_pairs(4, bits)) for bits in (1, 2, 3)]
+    outer = (row == 0) | (row == 3)
+    packed = jnp.stack(
+        [packed, one, jnp.where(outer, two, three), jnp.where(outer, three, two)]
+    )
+    top = expert_ids.shape[1]
+    device = row * 8 + (col ^ jnp.arange(8, dtype=jnp.int32))
+    experts = (device[:, None] * 2 + jnp.arange(2, dtype=jnp.int32)).reshape(-1)
+    return slot_places(packed[..., :top].astype(jnp.int32), packed[..., top:], experts)
+
+
+def experts_planes(moe_in, residual, places, gated, w_in, w_down):
+    model_width = moe_in.shape[1]
+    swap, middle, outward = xor_pairs(4, 1), [(1, 2), (2, 1)], [(1, 0), (2, 3)]
+    inward = [(0, 1), (3, 2)]
+    near = lax.ppermute(moe_in, "row", swap)
+    cross = lax.ppermute(moe_in, "row", middle)
+    cross_out = lax.ppermute(cross, "row", outward)
+    far = lax.ppermute(near, "row", middle)
+    far_out = lax.ppermute(far, "row", outward)
+
+    def send(place, block):
+        routed = route(place, block)
+        chips = [routed[:64]]
+        chips += [
+            lax.ppermute(routed[64 * r : 64 * (r + 1)], "col", xor_pairs(8, 2 * r))
+            for r in range(1, 4)
+        ]
+        return chips
+
+    def share(chips):
+        return jnp.concatenate([chip[32:] for chip in chips], axis=0)
+
+    def swap_cores(rows):
+        return lax.ppermute(rows, "col", xor_pairs(8, 1))
+
+    def views(chips, other):
+        return [chip.reshape(2, 2, CAP, model_width) for chip in chips] + [
+            other.reshape(4, 2, CAP, model_width)
+        ]
+
+    chips_0 = send(places[0], moe_in)
+    shared_0, near, cross = lax.optimization_barrier((share(chips_0), near, cross))
+    other_0 = swap_cores(shared_0)
+    chips_1 = send(places[1], near)
+    shared_1, cross_out, far = lax.optimization_barrier((share(chips_1), cross_out, far))
+    other_1 = swap_cores(shared_1)
+    chips_2 = send(places[2], cross + cross_out)
+    shared_2, far_out = lax.optimization_barrier((share(chips_2), far_out))
+    other_2 = swap_cores(shared_2)
+    chips_3 = send(places[3], far + far_out)
+    other_3 = swap_cores(share(chips_3))
+
+    def expert_parts(*blocks):
+        xs = [view for chips, other in blocks for view in views(chips, other)]
+        takes, outs = [1, 1, 1, 1, 4] * len(blocks), [4, 4] * len(blocks)
+        return expert_call(xs, takes, outs, w_in, w_down, 2)
+
+    parts = expert_parts(
+        (chips_0, other_0), (chips_1, other_1), (chips_2, other_2), (chips_3, other_3)
+    )
+
+    def give_back(own, other, before=None):
+        both = [
+            jnp.concatenate([own[r].reshape(32, model_width), other[r].reshape(32, model_width)])
+            for r in range(4)
+        ]
+        if before is not None:
+            *both, unused = lax.optimization_barrier((*both, before[1]))
+        return both[:1] + [
+            lax.ppermute(both[r], "col", xor_pairs(8, 2 * r)) for r in range(1, 4)
+        ]
+
+    def combine(gates, chips):
+        total = jnp.dot(gates[:, :64], chips[0], preferred_element_type=jnp.float32)
+        for r in range(1, 4):
+            total += jnp.dot(
+                gates[:, 64 * r : 64 * (r + 1)], chips[r], preferred_element_type=jnp.float32
+            )
+        return total
+
+    def narrow(total):
+        return total.astype(jnp.bfloat16)
+
+    back_3 = give_back(parts[6], swap_cores(parts[7]))
+    back_2 = give_back(parts[4], swap_cores(parts[5]), back_3)
+    sum_3 = narrow(combine(gated[3], back_3))
+    ends = lax.ppermute(sum_3, "row", [(0, 3), (3, 0)])
+    inner = lax.ppermute(sum_3, "row", [(1, 3), (2, 0)])
+    back_1 = give_back(parts[2], swap_cores(parts[3]), back_2)
+    sum_2 = combine(gated[2], back_2)
+    hop = lax.ppermute(narrow(sum_2), "row", inward)
+    back_0 = give_back(parts[0], swap_cores(parts[1]), back_1)
+    beside = lax.ppermute(narrow(combine(gated[1], back_1)), "row", swap)
+    middles = lax.ppermute(narrow(sum_2 + hop.astype(jnp.float32)), "row", middle)
+    total = residual + combine(gated[0], back_0)
+    for arrived in (ends, inner, beside, middles):
+        total += arrived.astype(jnp.float32)
+    return total.astype(jnp.bfloat16)
 
 
 def body(
@@ -300,9 +495,17 @@
     device_count = row_count * col_count
     new_rows = tok_rows * col_count
 
+    planes = row_count == 4 and col_count == 8 and w_in.shape[0] == 4
+
     normed = rms_scale(hidden, attn_gain).astype(jnp.bfloat16)
-    gathered = lax.all_gather(normed, "col", axis=0, tiled=True)
-    w_out_all = lax.all_gather(w_out, "col", axis=0)
+    if planes:
+        slots, gated = plane_places(expert_ids, gate_weights)
+        mine, other, w_out_late = gather_plane(normed, w_out)
+        even_odd = [[0, 2, 4, 6], [1, 3, 5, 7]]
+        w_out_mine = lax.all_gather(w_out_late, "col", axis=0, axis_index_groups=even_odd)
+    else:
+        gathered = lax.all_gather(normed, "col", axis=0, tiled=True)
+        w_out_all = lax.all_gather(w_out, "col", axis=0)
 
     row_index = lax.axis_index("row")
     places = jnp.arange(request_order.shape[0], dtype=jnp.int32)
@@ -315,51 +518,38 @@
     cosine = jnp.concatenate([cosine, cosine], axis=1)
     sine = jnp.concatenate([-sine, sine], axis=1)
 
-    queries, new_keys, new_values = qkv_call(
-        gathered, w_qkv.reshape(model_width, -1), cosine, sine, heads_here
-    )
+    w_matrix = w_qkv.reshape(model_width, -1)
+    if planes:
+        col = lax.axis_index("col")
+        chips = 2 * jnp.arange(4, dtype=jnp.int32)
+        fresh = qkv_call(col ^ chips, mine, w_matrix, cosine, sine, heads_here)
+        queries, new_keys, new_values = qkv_call(
+            col ^ chips ^ 1, other, w_matrix, cosine, sine, heads_here, fresh
+        )
+    else:
+        blocks = jnp.arange(col_count, dtype=jnp.int32)
+        queries, new_keys, new_values = qkv_call(
+            blocks, gathered, w_matrix, cosine, sine, heads_here
+        )
     context = attention_call(
         length.reshape(1), queries, cache_keys, cache_values, new_keys, new_values
     )
+    if planes:
+        w_out_mine, context = lax.optimization_barrier((w_out_mine, context))
     shares = lax.all_to_all(
         context.reshape(col_count, tok_rows, heads_here * HEAD), "col", 0, 0, tiled=True
     )
-    residual, moe_in = project_call(shares, w_out_all, hidden, moe_gain)
-
-    chosen = expert_ids[:, :, None] == jnp.arange(EXPERTS, dtype=jnp.int32)
-    named = jnp.any(chosen, axis=1)
-    gates = jnp.sum(jnp.where(chosen, gate_weights.astype(jnp.float32)[:, :, None], 0.0), axis=1)
-    earlier = jnp.arange(tok_rows)[:, None] > jnp.arange(tok_rows)[None, :]
-    rank = jnp.dot(
-        earlier.astype(jnp.bfloat16),
-        named.astype(jnp.bfloat16),
-        preferred_element_type=jnp.float32,
-    ).astype(jnp.int32)
-    rank = jnp.where(named, rank, -1)
-    place = (rank[:, :, None] == jnp.arange(CAP, dtype=jnp.int32)).reshape(tok_rows, EXPERTS * CAP)
-    place_gates = jnp.where(place, jnp.repeat(gates, CAP, axis=1), 0.0).astype(jnp.bfloat16)
-
-    per_device = w_in.shape[0]
-    halves = 2 if per_device % 2 == 0 else 1
-    copies = 2 // halves
-    routed = lax.dot_general(
-        place.astype(jnp.bfloat16),
-        moe_in,
-        (((0,), (0,)), ((), ())),
-        preferred_element_type=jnp.float32,
-    ).astype(jnp.bfloat16)
-    routed = routed.reshape(EXPERTS, 1, CAP, model_width)
-    routed = jnp.broadcast_to(routed, (EXPERTS, copies, CAP, model_width))
-    routed = routed.reshape(device_count, per_device // halves, CAP, model_width)
-    received = lax.all_to_all(routed, ("row", "col"), split_axis=0, concat_axis=0, tiled=True)
-    parts = expert_call(received, w_in, w_down, halves)
-    returned = lax.all_to_all(parts, ("row", "col"), split_axis=0, concat_axis=0, tiled=True)
-    if copies > 1:
-        returned = returned.reshape(EXPERTS, copies, CAP, model_width).astype(jnp.float32)
-        returned = jnp.sum(returned, axis=1).astype(jnp.bfloat16)
-    returned = returned.reshape(EXPERTS * CAP, model_width)
-    expert_sum = jnp.dot(place_gates, returned, preferred_element_type=jnp.float32)
-    new_hidden = (residual + expert_sum).astype(jnp.bfloat16)
+    if planes:
+        w_out_other = lax.ppermute(w_out_mine, "col", xor_pairs(8, 1))
+        core = col & 1
+        order = (chips[:, None] + jnp.stack([core, 1 - core])).reshape(-1)
+        residual, moe_in = project_call(
+            order, shares, [w_out_mine, w_out_other], hidden, moe_gain
+        )
+        new_hidden = experts_planes(moe_in, residual, slots, gated, w_in, w_down)
+    else:
+        residual, moe_in = project_call(blocks, shares, [w_out_all], hidden, moe_gain)
+        new_hidden = experts_direct(moe_in, residual, expert_ids, gate_weights, w_in, w_down)
     return (new_hidden, new_keys, new_values)
 
 

time: 356 us -> 293 us (0.82)
  blocking collectives: 98.2 us -> 0 us
  starting transfers between devices: 7.44 us -> 63.6 us
  waiting for transfers between devices: 146 us -> 99.6 us
  Pallas kernels: 61.2 us -> 80.8 us
    all_to_all x1 -> x0, blocking collectives: 98.2 us -> none  [body(): lax.all_to_all(routed, ('row', 'col'), split_axis=0, concat_axis=0, tiled...]
    all_to_all x1 -> x0, waiting for transfers between devices: 93.7 us -> none  [body(): lax.all_to_all(parts, ('row', 'col'), split_axis=0, concat_axis=0, tiled=...]
    ppermute x0 -> x51, waiting for transfers between devices: none -> 90.2 us  [the longest x12 37.7 us: send(): lax.ppermute(routed[64 * r:64 * (r + 1)], 'col', xor_pairs(8, 2 * r))]
    ppermute x0 -> x51, starting transfers between devices: none -> 60.1 us  [the longest x12 15.2 us: give_back(): lax.ppermute(both[r], 'col', xor_pairs(8, 2 * r))]
    all_gather x2 -> x1, waiting for transfers between devices: 37 us -> 0.01 us  [body(): lax.all_gather(w_out_late, 'col', axis=0, axis_index_groups=even_odd)]
    pallas_call x1, Pallas kernels: 25.1 us -> 38.4 us  [attention_call(): pl.pallas_call(functools.partial(attention_kernel, heads, bq, bk), grid_s...]
    pallas_call x3 -> x4, Pallas kernels: 36.1 us -> 42.4 us  [the longest x1 28.1 us: expert_call(): pl.pallas_call(functools.partial(expert_kernel, units, takes, resident),...]
    slice x0 -> x32, local copies, waits for them, and re-layouts: none -> 6.03 us  [the longest x4 3.2 us: send(): routed[64 * r:64 * (r + 1)]]
  transfers between devices with their start and end apart: 4 -> 53, of which waited for: 4 -> 25; matrix products, arithmetic and copies ran while one was open for 3% -> 7% of each run, Pallas kernels for 8% -> 16%
where the time goes in v2:
time: 293 us; the launch traced here: 291 us
  waiting for transfers between devices  99.6 us (34%)
  Pallas kernels  80.8 us (28%)
  starting transfers between devices  63.6 us (22%)
  between operations  15 us (5%)
  local copies, waits for them, and re-layouts  14.4 us (5%)
  other arithmetic  10.4 us (4%)
  matrix products  6.92 us (2%)
    pallas_call x1, Pallas kernels, attention_call(): pl.pallas_call(functools.partial(attention_kernel, heads, bq, bk), grid_s...  38.4 us
    ppermute x12, waiting for transfers between devices, send(): lax.ppermute(routed[64 * r:64 * (r + 1)], 'col', xor_pairs(8, 2 * r))  37.7 us
    pallas_call x1, Pallas kernels, expert_call(): pl.pallas_call(functools.partial(expert_kernel, units, takes, resident),...  28.1 us
    ppermute x12, waiting for transfers between devices, give_back(): lax.ppermute(both[r], 'col', xor_pairs(8, 2 * r))  18.8 us
    ppermute x12, starting transfers between devices, give_back(): lax.ppermute(both[r], 'col', xor_pairs(8, 2 * r))  15.2 us
    ppermute x12, starting transfers between devices, send(): lax.ppermute(routed[64 * r:64 * (r + 1)], 'col', xor_pairs(8, 2 * r))  14.2 us
    ppermute x1, waiting for transfers between devices, gather_plane(): along_x = lax.ppermute(block, 'col', xor_pairs(8, 2))  10.4 us
    pallas_call x2, Pallas kernels, qkv_call(): pl.pallas_call(functools.partial(qkv_kernel, heads), grid_spec=pltpu.Pref...  9.53 us
  transfers between devices with their start and end apart: 53, of which 25 were waited for; matrix products, arithmetic and copies ran while one was open for 7% of the time, Pallas kernels for 16%

profile of v2, /device:TPU:0, one launch (start us, length us, event | category | flops | bytes accessed | tf_op | source)
XLA Modules:
  0.0 290.7 jit_solution(6043516197693712811)
XLA Ops:
  10.4 3.0 %collective-permute-start = (bf16[128,2048]{1,0:T(8,128)(2,1)S(1)}, bf16[128,2048]{1,0:T(8,128)(2,1)S(1)}, u32[]{:S(2)}, u32[]{:S(2)}) collective-permute-start(bf16[128,2048]{1,0:T(8,128)(2,1)S(1)} %get-tuple-element.86), channel_id=1, source_target_pairs={{0,2},{1,3},{2,0},{3,1},{4,6},{5,7},{6,4},{7,5},{8,10},{9,11},{10,... | collective-permute-start | bytes 1572872 | tf_op jit(solution)/shard_map/ppermute | solution.py:313
  14.9 10.4 %collective-permute-done = bf16[128,2048]{1,0:T(8,128)(2,1)S(1)} collective-permute-done((bf16[128,2048]{1,0:T(8,128)(2,1)S(1)}, bf16[128,2048]{1,0:T(8,128)(2,1)S(1)}, u32[]{:S(2)}, u32[]{:S(2)}) %collective-permute-start) | collective-permute-done | bytes 524320 | tf_op jit(solution)/shard_map/ppermute | solution.py:313
  29.1 4.6 %collective-permute-done.2 = bf16[64,2048]{1,0:T(8,128)(2,1)S(1)} collective-permute-done((bf16[64,2048]{1,0:T(8,128)(2,1)S(1)}, bf16[64,2048]{1,0:T(8,128)(2,1)S(1)}, u32[]{:S(2)}, u32[]{:S(2)}) %collective-permute-start.2) | collective-permute-done | bytes 262176 | tf_op jit(solution)/shard_map/ppermute | solution.py:316
  35.2 2.9 copy.24
  42.9 3.9 %qkv.2 = (bf16[1024,256]{1,0:T(8,128)(2,1)S(1)}, bf16[1024,256]{1,0:T(8,128)(2,1)}, bf16[1024,256]{1,0:T(8,128)(2,1)}) custom-call(s32[4]{0:T(128)S(1)} %broadcast_xor_fusion.1.order_ref, bf16[512,2048]{1,0:T(8,128)(2,1)S(1)} %constant_dynamic-update-slice_fusion.x_ref, bf16[2048,768]{1,0:T(8,128)(2,1)S(1)} %bitcast.103, ...), custom_call_target="tpu_custom_call" | custom-call | flops 1610612736 | bytes 6029312 | tf_op jit(solution)/shard_map/qkv/pallas_call | solution.py:53
  46.8 5.6 %qkv.3 = (bf16[1024,256]{1,0:T(8,128)(2,1)S(1)}, bf16[1024,256]{1,0:T(8,128)(2,1)}, bf16[1024,256]{1,0:T(8,128)(2,1)}) custom-call(s32[4]{0:T(128)S(1)} %broadcast_xor_fusion.order_ref, bf16[512,2048]{1,0:T(8,128)(2,1)} %collective-permute-done.4.x_ref, bf16[2048,768]{1,0:T(8,128)(2,1)S(1)} %bitcast.104, ...), custom_call_target="tpu_custom_call", output_to_operand_aliasing={{0}: (5, {}), {1}: (6, {}), {2}: (7, {})} | custom-call | flops 1610612736 | bytes 6029312 | tf_op jit(solution)/shard_map/qkv/pallas_call | solution.py:53
  54.5 38.4 %attention.1 = bf16[1024,256]{1,0:T(8,128)(2,1)} custom-call(s32[1]{0:T(128)} %bitcast.3.len_ref, bf16[1024,256]{1,0:T(8,128)(2,1)S(1)} %get-tuple-element.50.q_ref, bf16[1,4096,256]{2,1,0:T(8,128)(2,1)S(1)} %copy-done.4, bf16[1,4096,256]{2,1,0:T(8,128)(2,1)S(1)} %copy-done.5, bf16[1024,256]{1,0:T(8,128)(2,1)S(1)} %copy-done.2, bf16[1024,256]{1,0:T(8,128)(2,1)S(1)} %copy-done.3), custom_call_target="tpu_custom_call" | custom-call | flops 5368709120 | bytes 6291456 | tf_op jit(solution)/shard_map/attention/pallas_call | solution.py:168
  93.4 3.4 %collective-permute-start.7 = (f32[128,12]{0,1:T(8,128)S(1)}, f32[128,12]{0,1:T(8,128)S(1)}, u32[]{:S(2)}, u32[]{:S(2)}) collective-permute-start(f32[128,12]{0,1:T(8,128)S(1)} %get-tuple-element.148), channel_id=1, source_target_pairs={{0,16},{8,24},{16,0},{24,8},{1,17},{9,25},{17,1},{25,9},{2,18},{10... | collective-permute-start | bytes 18440 | tf_op jit(solution)/shard_map/ppermute | solution.py:375
  98.5 3.8 %collective-permute-done.8 = f32[128,12]{0,1:T(8,128)S(1)} collective-permute-done((f32[128,12]{0,1:T(8,128)S(1)}, f32[128,12]{0,1:T(8,128)S(1)}, u32[]{:S(2)}, u32[]{:S(2)}) %collective-permute-start.8) | collective-permute-done | bytes 6176 | tf_op jit(solution)/shard_map/ppermute | solution.py:375
  102.4 3.5 %all-to-all-start = ((bf16[8,128,256]{2,1,0:T(8,128)(2,1)}), bf16[8,128,256]{2,1,0:T(8,128)(2,1)S(1)}, u32[]{:S(2)}, u32[]{:S(2)}) async-start(bf16[8,128,256]{2,1,0:T(8,128)(2,1)} %bitcast.4), calls=%async_computation | async-start | bytes 1048576 | tf_op jit(solution)/shard_map/all_to_all | solution.py:539
  106.2 9.4 %all-to-all-done.refs_0_.refs_1_ = bf16[8,128,256]{2,1,0:T(8,128)(2,1)S(1)} async-done(((bf16[8,128,256]{2,1,0:T(8,128)(2,1)}), bf16[8,128,256]{2,1,0:T(8,128)(2,1)S(1)}, u32[]{:S(2)}, u32[]{:S(2)}) %all-to-all-start) | async-done | bytes 524320 | tf_op jit(solution)/shard_map/all_to_all | solution.py:539
  115.6 2.2 copy-done.1
  117.8 4.8 %project.1 = (f32[128,2048]{1,0:T(8,128)S(1)}, bf16[128,2048]{1,0:T(8,128)(2,1)S(1)}) custom-call(s32[8]{0:T(128)S(1)} %add.131.order_ref, bf16[8,128,256]{2,1,0:T(8,128)(2,1)S(1)} %all-to-all-done.refs_0_.refs_1_, bf16[8,128,256]{2,1,0:T(8,128)(2,1)S(1)} %all-to-all-done.refs_0_.refs_1_, bf16[4,256,2048]{2,1,0:T(8,128)(2,1)S(1)} %bitcast.106, ...), custom_call_target="tpu_custom_call" | custom-call | flops 1073741824 | bytes 11010048 | tf_op jit(solution)/shard_map/project/pallas_call | solution.py:220
  125.9 2.4 collective-permute-start.11
  128.3 5.7 %collective-permute-done.9 = bf16[64,2048]{1,0:T(8,128)(2,1)S(1)} collective-permute-done((bf16[64,2048]{1,0:T(8,128)(2,1)S(1)}, bf16[64,2048]{1,0:T(8,128)(2,1)S(1)}, u32[]{:S(2)}, u32[]{:S(2)}) %collective-permute-start.9) | collective-permute-done | bytes 262176 | tf_op jit(solution)/shard_map/ppermute | solution.py:400
  134.0 4.9 %collective-permute-done.10 = bf16[64,2048]{1,0:T(8,128)(2,1)S(1)} collective-permute-done((bf16[64,2048]{1,0:T(8,128)(2,1)S(1)}, bf16[64,2048]{1,0:T(8,128)(2,1)S(1)}, u32[]{:S(2)}, u32[]{:S(2)}) %collective-permute-start.10) | collective-permute-done | bytes 262176 | tf_op jit(solution)/shard_map/ppermute | solution.py:400
  145.9 5.7 %collective-permute-done.15 = bf16[64,2048]{1,0:T(8,128)(2,1)S(1)} collective-permute-done((bf16[64,2048]{1,0:T(8,128)(2,1)S(1)}, bf16[64,2048]{1,0:T(8,128)(2,1)S(1)}, u32[]{:S(2)}, u32[]{:S(2)}) %collective-permute-start.15) | collective-permute-done | bytes 262176 | tf_op jit(solution)/shard_map/ppermute | solution.py:400
  151.6 3.5 %collective-permute-done.16 = bf16[64,2048]{1,0:T(8,128)(2,1)S(1)} collective-permute-done((bf16[64,2048]{1,0:T(8,128)(2,1)S(1)}, bf16[64,2048]{1,0:T(8,128)(2,1)S(1)}, u32[]{:S(2)}, u32[]{:S(2)}) %collective-permute-start.16) | collective-permute-done | bytes 262176 | tf_op jit(solution)/shard_map/ppermute | solution.py:400
  161.4 5.5 %collective-permute-done.21 = bf16[64,2048]{1,0:T(8,128)(2,1)S(1)} collective-permute-done((bf16[64,2048]{1,0:T(8,128)(2,1)S(1)}, bf16[64,2048]{1,0:T(8,128)(2,1)S(1)}, u32[]{:S(2)}, u32[]{:S(2)}) %collective-permute-start.21) | collective-permute-done | bytes 262176 | tf_op jit(solution)/shard_map/ppermute | solution.py:400
  167.0 4.2 %collective-permute-done.22 = bf16[64,2048]{1,0:T(8,128)(2,1)S(1)} collective-permute-done((bf16[64,2048]{1,0:T(8,128)(2,1)S(1)}, bf16[64,2048]{1,0:T(8,128)(2,1)S(1)}, u32[]{:S(2)}, u32[]{:S(2)}) %collective-permute-start.22) | collective-permute-done | bytes 262176 | tf_op jit(solution)/shard_map/ppermute | solution.py:400
  176.6 2.9 collective-permute-done.26
  179.5 3.3 %collective-permute-done.27 = bf16[64,2048]{1,0:T(8,128)(2,1)S(1)} collective-permute-done((bf16[64,2048]{1,0:T(8,128)(2,1)S(1)}, bf16[64,2048]{1,0:T(8,128)(2,1)S(1)}, u32[]{:S(2)}, u32[]{:S(2)}) %collective-permute-start.27) | collective-permute-done | bytes 262176 | tf_op jit(solution)/shard_map/ppermute | solution.py:400
  187.5 28.1 %experts.1 = (bf16[4,2,16,2048]{3,2,1,0:T(8,128)(2,1)}, bf16[4,2,16,2048]{3,2,1,0:T(8,128)(2,1)}, bf16[4,2,16,2048]{3,2,1,0:T(8,128)(2,1)}, bf16[4,2,16,2048]{3,...) custom-call(bf16[2,2,16,2048]{3,2,1,0:T(8,128)(2,1)} %bitcast.144, ...), custom_call_target="tpu_custom_call" | custom-call | flops 17716740096 | bytes 42991616 | tf_op jit(solution)/shard_map/experts/pallas_call | solution.py:288
  225.0 5.0 %collective-permute-done.34 = bf16[64,2048]{1,0:T(8,128)(2,1)S(1)} collective-permute-done((bf16[64,2048]{1,0:T(8,128)(2,1)S(1)}, bf16[64,2048]{1,0:T(8,128)(2,1)S(1)}, u32[]{:S(2)}, u32[]{:S(2)}) %collective-permute-start.34) | collective-permute-done | bytes 262176 | tf_op jit(solution)/shard_map/ppermute | solution.py:445
  232.9 2.8 collective-permute-done.41
  236.4 4.0 %collective-permute-start.42 = (bf16[128,2048]{1,0:T(8,128)(2,1)S(1)}, bf16[128,2048]{1,0:T(8,128)(2,1)S(1)}, u32[]{:S(2)}, u32[]{:S(2)}) collective-permute-start(bf16[128,2048]{1,0:T(8,128)(2,1)S(1)} %fusion.7), channel_id=1, source_target_pairs={{0,24},{24,0},{1,25},{25,1},{2,26},{26,2},{3,27},{27,3},{4,28},{28... | collective-permute-start | bytes 1572872 | tf_op jit(solution)/shard_map/ppermute | solution.py:462
  246.1 5.9 %collective-permute-done.48 = bf16[64,2048]{1,0:T(8,128)(2,1)S(1)} collective-permute-done((bf16[64,2048]{1,0:T(8,128)(2,1)S(1)}, bf16[64,2048]{1,0:T(8,128)(2,1)S(1)}, u32[]{:S(2)}, u32[]{:S(2)}) %collective-permute-start.48) | collective-permute-done | bytes 262176 | tf_op jit(solution)/shard_map/ppermute | solution.py:445
  254.1 3.5 %collective-permute-done.36 = bf16[64,2048]{1,0:T(8,128)(2,1)S(1)} collective-permute-done((bf16[64,2048]{1,0:T(8,128)(2,1)S(1)}, bf16[64,2048]{1,0:T(8,128)(2,1)S(1)}, u32[]{:S(2)}, u32[]{:S(2)}) %collective-permute-start.36) | collective-permute-done | bytes 262176 | tf_op jit(solution)/shard_map/ppermute | solution.py:445
  257.6 4.6 %collective-permute-start.49 = (bf16[128,2048]{1,0:T(8,128)(2,1)S(1)}, bf16[128,2048]{1,0:T(8,128)(2,1)S(1)}, u32[]{:S(2)}, u32[]{:S(2)}) collective-permute-start(bf16[128,2048]{1,0:T(8,128)(2,1)S(1)} %get-tuple-element.152), channel_id=1, source_target_pairs={{0,8},{24,16},{1,9},{25,17},{2,10},{26,18},{3,11},{27,19},{4,12},{... | collective-permute-start | bytes 1572872 | tf_op jit(solution)/shard_map/ppermute | solution.py:466
  266.0 5.1 %collective-permute-done.49 = bf16[128,2048]{1,0:T(8,128)(2,1)S(1)} collective-permute-done((bf16[128,2048]{1,0:T(8,128)(2,1)S(1)}, bf16[128,2048]{1,0:T(8,128)(2,1)S(1)}, u32[]{:S(2)}, u32[]{:S(2)}) %collective-permute-start.49) | collective-permute-done | bytes 524320 | tf_op jit(solution)/shard_map/ppermute | solution.py:466
  272.9 2.5 collective-permute-start.46
  279.0 3.5 %collective-permute-done.46 = bf16[128,2048]{1,0:T(8,128)(2,1)S(1)} collective-permute-done((bf16[128,2048]{1,0:T(8,128)(2,1)S(1)}, bf16[128,2048]{1,0:T(8,128)(2,1)S(1)}, u32[]{:S(2)}, u32[]{:S(2)}) %collective-permute-start.46) | collective-permute-done | bytes 524320 | tf_op jit(solution)/shard_map/ppermute | solution.py:468
  (251 shorter events, 76.5 us)
Async XLA Ops:
  7.2 85.8 %all-gather.3.cloned.1.call-start = ((), (), s32[]{:S(2)}) async-start(), calls=%async_computation.1 | async-start | bytes 5242880 | tf_op jit(solution)/shard_map/all_gather | solution.py:505
  10.4 14.9 %collective-permute-start = (bf16[128,2048]{1,0:T(8,128)(2,1)S(1)}, bf16[128,2048]{1,0:T(8,128)(2,1)S(1)}, u32[]{:S(2)}, u32[]{:S(2)}) collective-permute-start(bf16[128,2048]{1,0:T(8,128)(2,1)S(1)} %get-tuple-element.86), channel_id=1, source_target_pairs={{0,2},{1,3},{2,0},{3,1},{4,6},{5,7},{6,4},{7,5},{8,10},{9,11},{10,... | collective-permute-start | bytes 1572872 | tf_op jit(solution)/shard_map/ppermute | solution.py:313
  13.4 13.4 %collective-permute-start.1 = (bf16[128,2048]{1,0:T(8,128)(2,1)S(1)}, bf16[128,2048]{1,0:T(8,128)(2,1)S(1)}, u32[]{:S(2)}, u32[]{:S(2)}) collective-permute-start(bf16[128,2048]{1,0:T(8,128)(2,1)S(1)} %get-tuple-element.86), channel_id=1, source_target_pairs={{0,4},{1,5},{2,6},{3,7},{4,0},{5,1},{6,2},{7,3},{8,12},{9,13},{10,... | collective-permute-start | bytes 1572872 | tf_op jit(solution)/shard_map/ppermute | solution.py:314
  35.1 11.6 %collective-permute-start.4 = (bf16[512,2048]{1,0:T(8,128)(2,1)S(1)}, bf16[512,2048]{1,0:T(8,128)(2,1)}, u32[]{:S(2)}, u32[]{:S(2)}) collective-permute-start(bf16[512,2048]{1,0:T(8,128)(2,1)S(1)} %constant_dynamic-update-slice_fusion.x_ref), channel_id=1, source_target_pairs={{0,1},{1,0},{2,3},{3,2},{4,5},{5,4},{6,7},{7,6},{8,9},{9,8},{10,11... | collective-permute-start | bytes 6291464 | tf_op jit(solution)/shard_map/ppermute | solution.py:319
  92.9 22.7 %collective-permute-start.5 = (bf16[4,256,2048]{2,1,0:T(8,128)(2,1)}, bf16[4,256,2048]{2,1,0:T(8,128)(2,1)}, u32[]{:S(2)}, u32[]{:S(2)}) collective-permute-start(bf16[4,256,2048]{2,1,0:T(8,128)(2,1)} %bitcast.105), channel_id=1, source_target_pairs={{0,1},{1,0},{2,3},{3,2},{4,5},{5,4},{6,7},{7,6},{8,9},{9,8},{10,11... | collective-permute-start | bytes 12582920 | tf_op jit(solution)/shard_map/ppermute | solution.py:543
  102.4 13.2 %all-to-all-start = ((bf16[8,128,256]{2,1,0:T(8,128)(2,1)}), bf16[8,128,256]{2,1,0:T(8,128)(2,1)S(1)}, u32[]{:S(2)}, u32[]{:S(2)}) async-start(bf16[8,128,256]{2,1,0:T(8,128)(2,1)} %bitcast.4), calls=%async_computation | async-start | bytes 1048576 | tf_op jit(solution)/shard_map/all_to_all | solution.py:539
  122.6 16.5 %collective-permute-start.12 = (bf16[128,2048]{1,0:T(8,128)(2,1)S(1)}, bf16[128,2048]{1,0:T(8,128)(2,1)S(1)}, u32[]{:S(2)}, u32[]{:S(2)}) collective-permute-start(bf16[128,2048]{1,0:T(8,128)(2,1)S(1)} %get-tuple-element.56), channel_id=1, source_target_pairs={{0,8},{8,0},{16,24},{24,16},{1,9},{9,1},{17,25},{25,17},{2,10},{10... | collective-permute-start | bytes 1572872 | tf_op jit(solution)/shard_map/ppermute | solution.py:390
  122.7 16.4 %collective-permute-start.13 = (bf16[128,2048]{1,0:T(8,128)(2,1)S(1)}, bf16[128,2048]{1,0:T(8,128)(2,1)S(1)}, u32[]{:S(2)}, u32[]{:S(2)}) collective-permute-start(bf16[128,2048]{1,0:T(8,128)(2,1)S(1)} %get-tuple-element.56), channel_id=1, source_target_pairs={{8,16},{16,8},{9,17},{17,9},{10,18},{18,10},{11,19},{19,11},{12,20... | collective-permute-start | bytes 1572872 | tf_op jit(solution)/shard_map/ppermute | solution.py:391
  125.3 13.6 %collective-permute-start.10 = (bf16[64,2048]{1,0:T(8,128)(2,1)S(1)}, bf16[64,2048]{1,0:T(8,128)(2,1)S(1)}, u32[]{:S(2)}, u32[]{:S(2)}) collective-permute-start(bf16[64,2048]{1,0:T(8,128)(2,1)S(1)} %get-tuple-element.100), channel_id=1, source_target_pairs={{0,4},{1,5},{2,6},{3,7},{4,0},{5,1},{6,2},{7,3},{8,12},{9,13},{10,... | collective-permute-start | bytes 786440 | tf_op jit(solution)/shard_map/ppermute | solution.py:400
  125.9 13.1 %collective-permute-start.11 = (bf16[64,2048]{1,0:T(8,128)(2,1)S(1)}, bf16[64,2048]{1,0:T(8,128)(2,1)S(1)}, u32[]{:S(2)}, u32[]{:S(2)}) collective-permute-start(bf16[64,2048]{1,0:T(8,128)(2,1)S(1)} %get-tuple-element.99), channel_id=1, source_target_pairs={{0,6},{1,7},{2,4},{3,5},{4,2},{5,3},{6,0},{7,1},{8,14},{9,15},{10,... | collective-permute-start | bytes 786440 | tf_op jit(solution)/shard_map/ppermute | solution.py:400
  139.5 15.8 %collective-permute-start.18 = (bf16[128,2048]{1,0:T(8,128)(2,1)S(1)}, bf16[128,2048]{1,0:T(8,128)(2,1)S(1)}, u32[]{:S(2)}, u32[]{:S(2)}) collective-permute-start(bf16[128,2048]{1,0:T(8,128)(2,1)S(1)} %collective-permute-done.13), channel_id=1, source_target_pairs={{8,0},{16,24},{9,1},{17,25},{10,2},{18,26},{11,3},{19,27},{12,4},{... | collective-permute-start | bytes 1572872 | tf_op jit(solution)/shard_map/ppermute | solution.py:392
  140.8 14.5 %collective-permute-start.19 = (bf16[128,2048]{1,0:T(8,128)(2,1)S(1)}, bf16[128,2048]{1,0:T(8,128)(2,1)S(1)}, u32[]{:S(2)}, u32[]{:S(2)}) collective-permute-start(bf16[128,2048]{1,0:T(8,128)(2,1)S(1)} %collective-permute-done.12), channel_id=1, source_target_pairs={{8,16},{16,8},{9,17},{17,9},{10,18},{18,10},{11,19},{19,11},{12,20... | collective-permute-start | bytes 1572872 | tf_op jit(solution)/shard_map/ppermute | solution.py:393
  142.7 12.5 %collective-permute-start.16 = (bf16[64,2048]{1,0:T(8,128)(2,1)S(1)}, bf16[64,2048]{1,0:T(8,128)(2,1)S(1)}, u32[]{:S(2)}, u32[]{:S(2)}) collective-permute-start(bf16[64,2048]{1,0:T(8,128)(2,1)S(1)} %get-tuple-element.96), channel_id=1, source_target_pairs={{0,4},{1,5},{2,6},{3,7},{4,0},{5,1},{6,2},{7,3},{8,12},{9,13},{10,... | collective-permute-start | bytes 786440 | tf_op jit(solution)/shard_map/ppermute | solution.py:400
  144.1 11.1 %collective-permute-start.17 = (bf16[64,2048]{1,0:T(8,128)(2,1)S(1)}, bf16[64,2048]{1,0:T(8,128)(2,1)S(1)}, u32[]{:S(2)}, u32[]{:S(2)}) collective-permute-start(bf16[64,2048]{1,0:T(8,128)(2,1)S(1)} %get-tuple-element.95), channel_id=1, source_target_pairs={{0,6},{1,7},{2,4},{3,5},{4,2},{5,3},{6,0},{7,1},{8,14},{9,15},{10,... | collective-permute-start | bytes 786440 | tf_op jit(solution)/shard_map/ppermute | solution.py:400
  155.7 15.5 %collective-permute-start.24 = (bf16[128,2048]{1,0:T(8,128)(2,1)S(1)}, bf16[128,2048]{1,0:T(8,128)(2,1)S(1)}, u32[]{:S(2)}, u32[]{:S(2)}) collective-permute-start(bf16[128,2048]{1,0:T(8,128)(2,1)S(1)} %collective-permute-done.19), channel_id=1, source_target_pairs={{8,0},{16,24},{9,1},{17,25},{10,2},{18,26},{11,3},{19,27},{12,4},{... | collective-permute-start | bytes 1572872 | tf_op jit(solution)/shard_map/ppermute | solution.py:394
  159.6 11.6 %collective-permute-start.22 = (bf16[64,2048]{1,0:T(8,128)(2,1)S(1)}, bf16[64,2048]{1,0:T(8,128)(2,1)S(1)}, u32[]{:S(2)}, u32[]{:S(2)}) collective-permute-start(bf16[64,2048]{1,0:T(8,128)(2,1)S(1)} %get-tuple-element.92), channel_id=1, source_target_pairs={{0,4},{1,5},{2,6},{3,7},{4,0},{5,1},{6,2},{7,3},{8,12},{9,13},{10,... | collective-permute-start | bytes 786440 | tf_op jit(solution)/shard_map/ppermute | solution.py:400
  159.9 11.2 %collective-permute-start.23 = (bf16[64,2048]{1,0:T(8,128)(2,1)S(1)}, bf16[64,2048]{1,0:T(8,128)(2,1)S(1)}, u32[]{:S(2)}, u32[]{:S(2)}) collective-permute-start(bf16[64,2048]{1,0:T(8,128)(2,1)S(1)} %get-tuple-element.91), channel_id=1, source_target_pairs={{0,6},{1,7},{2,4},{3,5},{4,2},{5,3},{6,0},{7,1},{8,14},{9,15},{10,... | collective-permute-start | bytes 786440 | tf_op jit(solution)/shard_map/ppermute | solution.py:400
  174.7 9.9 %collective-permute-start.28 = (bf16[64,2048]{1,0:T(8,128)(2,1)S(1)}, bf16[64,2048]{1,0:T(8,128)(2,1)S(1)}, u32[]{:S(2)}, u32[]{:S(2)}) collective-permute-start(bf16[64,2048]{1,0:T(8,128)(2,1)S(1)} %get-tuple-element.87), channel_id=1, source_target_pairs={{0,6},{1,7},{2,4},{3,5},{4,2},{5,3},{6,0},{7,1},{8,14},{9,15},{10,... | collective-permute-start | bytes 786440 | tf_op jit(solution)/shard_map/ppermute | solution.py:400
  221.4 14.6 %collective-permute-start.40 = (bf16[64,2048]{1,0:T(8,128)(2,1)S(1)}, bf16[64,2048]{1,0:T(8,128)(2,1)S(1)}, u32[]{:S(2)}, u32[]{:S(2)}) collective-permute-start(bf16[64,2048]{1,0:T(8,128)(2,1)S(1)} %pad_maximum_fusion.19), channel_id=1, source_target_pairs={{0,4},{1,5},{2,6},{3,7},{4,0},{5,1},{6,2},{7,3},{8,12},{9,13},{10,... | collective-permute-start | bytes 786440 | tf_op jit(solution)/shard_map/ppermute | solution.py:445
  223.2 12.5 %collective-permute-start.41 = (bf16[64,2048]{1,0:T(8,128)(2,1)S(1)}, bf16[64,2048]{1,0:T(8,128)(2,1)S(1)}, u32[]{:S(2)}, u32[]{:S(2)}) collective-permute-start(bf16[64,2048]{1,0:T(8,128)(2,1)S(1)} %pad_maximum_fusion.20), channel_id=1, source_target_pairs={{0,6},{1,7},{2,4},{3,5},{4,2},{5,3},{6,0},{7,1},{8,14},{9,15},{10,... | collective-permute-start | bytes 786440 | tf_op jit(solution)/shard_map/ppermute | solution.py:445
  229.9 13.4 %collective-permute-start.35 = (bf16[64,2048]{1,0:T(8,128)(2,1)S(1)}, bf16[64,2048]{1,0:T(8,128)(2,1)S(1)}, u32[]{:S(2)}, u32[]{:S(2)}) collective-permute-start(bf16[64,2048]{1,0:T(8,128)(2,1)S(1)} %pad_maximum_fusion.15), channel_id=1, source_target_pairs={{0,2},{1,3},{2,0},{3,1},{4,6},{5,7},{6,4},{7,5},{8,10},{9,11},{10,... | collective-permute-start | bytes 786440 | tf_op jit(solution)/shard_map/ppermute | solution.py:445
  230.5 14.6 %collective-permute-start.47 = (bf16[64,2048]{1,0:T(8,128)(2,1)S(1)}, bf16[64,2048]{1,0:T(8,128)(2,1)S(1)}, u32[]{:S(2)}, u32[]{:S(2)}) collective-permute-start(bf16[64,2048]{1,0:T(8,128)(2,1)S(1)} %pad_maximum_fusion.16), channel_id=1, source_target_pairs={{0,4},{1,5},{2,6},{3,7},{4,0},{5,1},{6,2},{7,3},{8,12},{9,13},{10,... | collective-permute-start | bytes 786440 | tf_op jit(solution)/shard_map/ppermute | solution.py:445
  236.4 42.6 %collective-permute-start.42 = (bf16[128,2048]{1,0:T(8,128)(2,1)S(1)}, bf16[128,2048]{1,0:T(8,128)(2,1)S(1)}, u32[]{:S(2)}, u32[]{:S(2)}) collective-permute-start(bf16[128,2048]{1,0:T(8,128)(2,1)S(1)} %fusion.7), channel_id=1, source_target_pairs={{0,24},{24,0},{1,25},{25,1},{2,26},{26,2},{3,27},{27,3},{4,28},{28... | collective-permute-start | bytes 1572872 | tf_op jit(solution)/shard_map/ppermute | solution.py:462
  240.4 38.7 %collective-permute-start.43 = (bf16[128,2048]{1,0:T(8,128)(2,1)S(1)}, bf16[128,2048]{1,0:T(8,128)(2,1)S(1)}, u32[]{:S(2)}, u32[]{:S(2)}) collective-permute-start(bf16[128,2048]{1,0:T(8,128)(2,1)S(1)} %fusion.7), channel_id=1, source_target_pairs={{8,24},{16,0},{9,25},{17,1},{10,26},{18,2},{11,27},{19,3},{12,28},... | collective-permute-start | bytes 1572872 | tf_op jit(solution)/shard_map/ppermute | solution.py:463
  241.9 10.2 %collective-permute-start.48 = (bf16[64,2048]{1,0:T(8,128)(2,1)S(1)}, bf16[64,2048]{1,0:T(8,128)(2,1)S(1)}, u32[]{:S(2)}, u32[]{:S(2)}) collective-permute-start(bf16[64,2048]{1,0:T(8,128)(2,1)S(1)} %pad_maximum_fusion.17), channel_id=1, source_target_pairs={{0,6},{1,7},{2,4},{3,5},{4,2},{5,3},{6,0},{7,1},{8,14},{9,15},{10,... | collective-permute-start | bytes 786440 | tf_op jit(solution)/shard_map/ppermute | solution.py:445
  243.3 14.3 %collective-permute-start.36 = (bf16[64,2048]{1,0:T(8,128)(2,1)S(1)}, bf16[64,2048]{1,0:T(8,128)(2,1)S(1)}, u32[]{:S(2)}, u32[]{:S(2)}) collective-permute-start(bf16[64,2048]{1,0:T(8,128)(2,1)S(1)} %pad_maximum_fusion.11), channel_id=1, source_target_pairs={{0,2},{1,3},{2,0},{3,1},{4,6},{5,7},{6,4},{7,5},{8,10},{9,11},{10,... | collective-permute-start | bytes 786440 | tf_op jit(solution)/shard_map/ppermute | solution.py:445
  245.1 17.4 %collective-permute-start.44 = (bf16[64,2048]{1,0:T(8,128)(2,1)S(1)}, bf16[64,2048]{1,0:T(8,128)(2,1)S(1)}, u32[]{:S(2)}, u32[]{:S(2)}) collective-permute-start(bf16[64,2048]{1,0:T(8,128)(2,1)S(1)} %pad_maximum_fusion.12), channel_id=1, source_target_pairs={{0,4},{1,5},{2,6},{3,7},{4,0},{5,1},{6,2},{7,3},{8,12},{9,13},{10,... | collective-permute-start | bytes 786440 | tf_op jit(solution)/shard_map/ppermute | solution.py:445
  252.1 11.5 %collective-permute-start.45 = (bf16[64,2048]{1,0:T(8,128)(2,1)S(1)}, bf16[64,2048]{1,0:T(8,128)(2,1)S(1)}, u32[]{:S(2)}, u32[]{:S(2)}) collective-permute-start(bf16[64,2048]{1,0:T(8,128)(2,1)S(1)} %pad_maximum_fusion.13), channel_id=1, source_target_pairs={{0,6},{1,7},{2,4},{3,5},{4,2},{5,3},{6,0},{7,1},{8,14},{9,15},{10,... | collective-permute-start | bytes 786440 | tf_op jit(solution)/shard_map/ppermute | solution.py:445
  257.6 13.5 %collective-permute-start.49 = (bf16[128,2048]{1,0:T(8,128)(2,1)S(1)}, bf16[128,2048]{1,0:T(8,128)(2,1)S(1)}, u32[]{:S(2)}, u32[]{:S(2)}) collective-permute-start(bf16[128,2048]{1,0:T(8,128)(2,1)S(1)} %get-tuple-element.152), channel_id=1, source_target_pairs={{0,8},{24,16},{1,9},{25,17},{2,10},{26,18},{3,11},{27,19},{4,12},{... | collective-permute-start | bytes 1572872 | tf_op jit(solution)/shard_map/ppermute | solution.py:466
  262.6 10.3 %collective-permute-start.38 = (bf16[64,2048]{1,0:T(8,128)(2,1)S(1)}, bf16[64,2048]{1,0:T(8,128)(2,1)S(1)}, u32[]{:S(2)}, u32[]{:S(2)}) collective-permute-start(bf16[64,2048]{1,0:T(8,128)(2,1)S(1)} %pad_maximum_fusion.8), channel_id=1, source_target_pairs={{0,4},{1,5},{2,6},{3,7},{4,0},{5,1},{6,2},{7,3},{8,12},{9,13},{10,... | collective-permute-start | bytes 786440 | tf_op jit(solution)/shard_map/ppermute | solution.py:445
  263.6 12.1 %collective-permute-start.37 = (bf16[64,2048]{1,0:T(8,128)(2,1)S(1)}, bf16[64,2048]{1,0:T(8,128)(2,1)S(1)}, u32[]{:S(2)}, u32[]{:S(2)}) collective-permute-start(bf16[64,2048]{1,0:T(8,128)(2,1)S(1)} %pad_maximum_fusion.7), channel_id=1, source_target_pairs={{0,2},{1,3},{2,0},{3,1},{4,6},{5,7},{6,4},{7,5},{8,10},{9,11},{10,... | collective-permute-start | bytes 786440 | tf_op jit(solution)/shard_map/ppermute | solution.py:445
  272.9 9.7 %collective-permute-start.46 = (bf16[128,2048]{1,0:T(8,128)(2,1)S(1)}, bf16[128,2048]{1,0:T(8,128)(2,1)S(1)}, u32[]{:S(2)}, u32[]{:S(2)}) collective-permute-start(bf16[128,2048]{1,0:T(8,128)(2,1)S(1)} %fusion.8), channel_id=1, source_target_pairs={{0,8},{8,0},{16,24},{24,16},{1,9},{9,1},{17,25},{25,17},{2,10},{10... | collective-permute-start | bytes 1572872 | tf_op jit(solution)/shard_map/ppermute | solution.py:468
  (52 other events, 377.8 us)
Sparse Core Ops, SparseCore 0:
  26.9 53.0 all-gather.2

commit v3 on v2

--- a/solution.py
+++ b/solution.py
@@ -76,9 +76,10 @@
     )(order, x, w, cosine, sine, *before)
 
 
-def attention_kernel(heads, bq, bk, len_ref, q_ref, kc_ref, vc_ref, kn_ref, vn_ref, o_ref):
+def attention_kernel(heads, bq, bk, info_ref, q_ref, kc_ref, vc_ref, kn_ref, vn_ref, o_ref, *scores):
+    length, flip = info_ref[0], info_ref[1]
+    cache_rows, new_rows = kc_ref.shape[1], kn_ref.shape[0]
     q_start = pl.program_id(0) * bq
-    length = len_ref[0]
     first = length + q_start
     last = first + bq - 1
     blocks = (length + bk - 1) // bk
@@ -86,85 +87,113 @@
     inside = jnp.minimum((jnp.maximum(last - WINDOW + 1, 0) + bk - 1) // bk, blocks)
     whole = jnp.maximum(inside, length // bk)
 
-    def update(state, keys, values, allowed):
+    def rows_and_places(size):
+        return (
+            lax.broadcasted_iota(jnp.int32, (bq, size), 0),
+            lax.broadcasted_iota(jnp.int32, (bq, size), 1),
+        )
+
+    def walk(visit, state):
+        def cached(start, size):
+            def load(ref, h):
+                return ref[0, pl.ds(start, size), h * HEAD : (h + 1) * HEAD]
+
+            return functools.partial(load, kc_ref), functools.partial(load, vc_ref)
+
+        def fresh(start, size):
+            def load(ref, h):
+                return ref[pl.ds(start, size), h * HEAD : (h + 1) * HEAD]
+
+            return functools.partial(load, kn_ref), functools.partial(load, vn_ref)
+
+        def sink_step(j, state):
+            def allowed():
+                rows, places = rows_and_places(HEAD)
+                out_of_window = first + rows - places >= WINDOW
+                return (places < SINKS) & (places < lowest * bk) & out_of_window
+
+            return visit(state, *cached(0, HEAD), allowed, cache_rows + new_rows, HEAD)
+
+        def masked_step(j, state):
+            start = pl.multiple_of(j * bk, bk)
+
+            def allowed():
+                rows, places = rows_and_places(bk)
+                places = start + places
+                in_window = first + rows - places < WINDOW
+                return (places < length) & (in_window | (places < SINKS))
+
+            return visit(state, *cached(start, bk), allowed, start, bk)
+
+        def plain_step(j, state):
+            start = pl.multiple_of(j * bk, bk)
+            return visit(state, *cached(start, bk), None, start, bk)
+
+        def fresh_step(j, state):
+            start = pl.multiple_of(j * bq, bq)
+            slot = pl.multiple_of(cache_rows + start, bq)
+            return visit(state, *fresh(start, bq), None, slot, bq)
+
+        def causal():
+            rows, places = rows_and_places(bq)
+            return places <= rows
+
+        state = lax.fori_loop(0, jnp.minimum(lowest, 1), sink_step, state)
+        state = lax.fori_loop(lowest, inside, masked_step, state)
+        state = lax.fori_loop(inside, whole, plain_step, state)
+        state = lax.fori_loop(whole, blocks, masked_step, state)
+        state = lax.fori_loop(0, pl.program_id(0), fresh_step, state)
+        start = pl.multiple_of(q_start, bq)
+        slot = pl.multiple_of(cache_rows + q_start, bq)
+        return visit(state, *fresh(start, bq), causal, slot, bq)
+
+    def score(state, keys, values, allowed, slot, size):
+        allowed = None if allowed is None else allowed()
         new_state = []
         for h in range(heads):
-            m, l, acc = state[h]
-            cols = slice(h * HEAD, (h + 1) * HEAD)
             s = lax.dot_general(
-                q_ref[:, cols],
-                keys[h],
+                q_ref[:, h * HEAD : (h + 1) * HEAD],
+                keys(h),
                 (((1,), (1,)), ((), ())),
                 preferred_element_type=jnp.float32,
             )
             if allowed is not None:
                 s = jnp.where(allowed, s, NEG)
-            m_new = jnp.maximum(m, jnp.max(s, axis=1, keepdims=True))
-            alpha = jnp.exp2(m - m_new)
-            p = jnp.exp2(s - m_new)
-            l = l * alpha + jnp.sum(p, axis=1, keepdims=True)
-            acc = acc * alpha + jnp.dot(
-                p.astype(jnp.bfloat16), values[h], preferred_element_type=jnp.float32
-            )
-            new_state.append((m_new, l, acc))
+            scores[h][:, pl.ds(slot, size)] = s
+            highest = state[h]
+            for c in range(0, size, HEAD):
+                highest = jnp.maximum(highest, s[:, c : c + HEAD])
+            new_state.append(highest)
         return tuple(new_state)
 
-    def cached(start, size):
-        keys = [kc_ref[0, pl.ds(start, size), h * HEAD : (h + 1) * HEAD] for h in range(heads)]
-        values = [vc_ref[0, pl.ds(start, size), h * HEAD : (h + 1) * HEAD] for h in range(heads)]
-        return keys, values
-
-    def fresh(start, size):
-        keys = [kn_ref[pl.ds(start, size), h * HEAD : (h + 1) * HEAD] for h in range(heads)]
-        values = [vn_ref[pl.ds(start, size), h * HEAD : (h + 1) * HEAD] for h in range(heads)]
-        return keys, values
-
-    def sink_step(j, state):
-        places = lax.broadcasted_iota(jnp.int32, (bq, HEAD), 1)
-        rows = lax.broadcasted_iota(jnp.int32, (bq, HEAD), 0)
-        allowed = (places < SINKS) & (places < lowest * bk) & (first + rows - places >= WINDOW)
-        return update(state, *cached(0, HEAD), allowed)
-
-    def masked_step(j, state):
-        start = pl.multiple_of(j * bk, bk)
-        places = start + lax.broadcasted_iota(jnp.int32, (bq, bk), 1)
-        rows = lax.broadcasted_iota(jnp.int32, (bq, bk), 0)
-        allowed = (places < length) & ((first + rows - places < WINDOW) | (places < SINKS))
-        return update(state, *cached(start, bk), allowed)
-
-    def plain_step(j, state):
-        return update(state, *cached(pl.multiple_of(j * bk, bk), bk), None)
-
-    def fresh_step(j, state):
-        return update(state, *fresh(pl.multiple_of(j * bq, bq), bq), None)
-
-    state = tuple(
-        (
-            jnp.full((bq, 1), NEG, jnp.float32),
-            jnp.zeros((bq, 1), jnp.float32),
-            jnp.zeros((bq, HEAD), jnp.float32),
-        )
-        for h in range(heads)
-    )
-    state = lax.fori_loop(0, jnp.minimum(lowest, 1), sink_step, state)
-    state = lax.fori_loop(lowest, inside, masked_step, state)
-    state = lax.fori_loop(inside, whole, plain_step, state)
-    state = lax.fori_loop(whole, blocks, masked_step, state)
-    state = lax.fori_loop(0, pl.program_id(0), fresh_step, state)
-    rows = lax.broadcasted_iota(jnp.int32, (bq, bq), 0)
-    places = lax.broadcasted_iota(jnp.int32, (bq, bq), 1)
-    state = update(state, *fresh(pl.multiple_of(q_start, bq), bq), places <= rows)
+    highest = walk(score, (jnp.full((bq, HEAD), NEG, jnp.float32),) * heads)
+    highest = [jnp.max(part, axis=1, keepdims=True) for part in highest]
+
+    def weigh(state, keys, values, allowed, slot, size):
+        new_state = []
+        for h in range(heads):
+            p = jnp.exp2(scores[h][:, pl.ds(slot, size)] - highest[h]).astype(jnp.bfloat16)
+            v = values(h)
+            v = jnp.concatenate([v, jnp.ones_like(v)], axis=1)
+            new_state.append(state[h] + jnp.dot(p, v, preferred_element_type=jnp.float32))
+        return tuple(new_state)
+
+    sums = walk(weigh, (jnp.zeros((bq, 2 * HEAD), jnp.float32),) * heads)
+    tokens = o_ref.shape[1]
     for h in range(heads):
-        m, l, acc = state[h]
-        o_ref[:, h * HEAD : (h + 1) * HEAD] = (acc / l).astype(o_ref.dtype)
-
-
-def attention_call(length, q, cache_keys, cache_values, new_keys, new_values, bq=256, bk=512):
+        out = (sums[h][:, :HEAD] / sums[h][:, HEAD:]).astype(o_ref.dtype)
+        for j in range(bq // tokens):
+            place = (pl.program_id(0) * (bq // tokens) + j) ^ flip
+            o_ref[place, :, h * HEAD : (h + 1) * HEAD] = out[j * tokens : (j + 1) * tokens]
+
+
+def attention_call(length, flip, tokens, q, cache_keys, cache_values, new_keys, new_values):
     rows, width = q.shape
     heads = width // HEAD
     cache_rows = cache_keys.shape[1]
-    bk = min(bk, cache_rows)
+    bq, bk = min(512, rows), min(1024, cache_rows)
     fixed = lambda shape: pl.BlockSpec(shape, lambda i, n: (0,) * len(shape))
+    out_shape = (rows // tokens, tokens, width)
     return pl.pallas_call(
         functools.partial(attention_kernel, heads, bq, bk),
         grid_spec=pltpu.PrefetchScalarGridSpec(
@@ -177,17 +206,18 @@
                 fixed(new_keys.shape),
                 fixed(new_values.shape),
             ],
-            out_specs=pl.BlockSpec((bq, width), lambda i, n: (i, 0)),
-        ),
-        out_shape=jax.ShapeDtypeStruct((rows, width), jnp.bfloat16),
-        compiler_params=pltpu.CompilerParams(vmem_limit_bytes=40 * MIB),
+            out_specs=fixed(out_shape),
+            scratch_shapes=[pltpu.VMEM((bq, cache_rows + rows + HEAD), jnp.float32)] * heads,
+        ),
+        out_shape=jax.ShapeDtypeStruct(out_shape, jnp.bfloat16),
+        compiler_params=pltpu.CompilerParams(vmem_limit_bytes=50 * MIB),
         cost_estimate=pl.CostEstimate(
             flops=4 * rows * width * (cache_rows + rows),
             bytes_accessed=4 * (cache_rows + 2 * rows) * width,
             transcendentals=rows * heads * (cache_rows + rows),
         ),
         name="attention",
-    )(length, q, cache_keys, cache_values, new_keys, new_values)
+    )(jnp.stack([length, flip]), q, cache_keys, cache_values, new_keys, new_values)
 
 
 def project_kernel(parts, order_ref, *refs):
@@ -208,22 +238,18 @@
         normed_ref[...] = rms_scale(resid_ref[...], gain_ref[...]).astype(jnp.bfloat16)
 
 
-def project_call(order, x, weights, hidden, gain):
-    groups, rows, width = x.shape
+def project_call(order, xs, weights, hidden, gain):
     parts = len(weights)
-    steps, unused, model = weights[0].shape
+    steps, rows, width = xs[0].shape
+    model = weights[0].shape[2]
     fixed = pl.BlockSpec((rows, model), lambda g, n: (0, 0))
-
-    def share_spec(part):
-        return pl.BlockSpec((1, rows, width), lambda g, n: (n[g * parts + part], 0, 0))
-
     return pl.pallas_call(
         functools.partial(project_kernel, parts),
         grid_spec=pltpu.PrefetchScalarGridSpec(
             num_scalar_prefetch=1,
             grid=(steps,),
-            in_specs=[share_spec(part) for part in range(parts)]
-            + [pl.BlockSpec((1, width, model), lambda g, n: (g, 0, 0))] * parts
+            in_specs=[pl.BlockSpec((1, rows, width), lambda g, n: (g, 0, 0))] * parts
+            + [pl.BlockSpec((1, width, model), lambda g, n: (n[g], 0, 0))] * parts
             + [fixed, pl.BlockSpec((1, model), lambda g, n: (0, 0))],
             out_specs=[fixed, fixed],
         ),
@@ -233,12 +259,76 @@
         ],
         compiler_params=pltpu.CompilerParams(vmem_limit_bytes=24 * MIB),
         cost_estimate=pl.CostEstimate(
-            flops=2 * rows * model * groups * width,
-            bytes_accessed=2 * groups * (width * model + rows * width) + 8 * rows * model,
+            flops=2 * rows * model * steps * parts * width,
+            bytes_accessed=2 * steps * parts * (width * model + rows * width) + 8 * rows * model,
             transcendentals=0,
         ),
         name="project",
-    )(order, *[x] * parts, *weights, hidden, gain.reshape(1, model))
+    )(order, *xs, *weights, hidden, gain.reshape(1, model))
+
+
+def share_kernel(order_ref, x_ref, w_ref, here_ref, beside_ref):
+    tokens = here_ref.shape[0]
+    x = x_ref[0].reshape(2 * tokens, x_ref.shape[3])
+    share = jnp.dot(x, w_ref[0], preferred_element_type=jnp.float32)
+    share = share.astype(jnp.bfloat16).astype(jnp.float32)
+
+    @pl.when(pl.program_id(0) == 0)
+    def _():
+        here_ref[...] = share[:tokens]
+        beside_ref[...] = share[tokens:]
+
+    @pl.when(pl.program_id(0) > 0)
+    def _():
+        here_ref[...] += share[:tokens]
+        beside_ref[...] += share[tokens:]
+
+
+def share_call(order, x, weight):
+    steps, unused, tokens, width = x.shape
+    model = weight.shape[2]
+    fixed = pl.BlockSpec((tokens, model), lambda g, n: (0, 0))
+    return pl.pallas_call(
+        share_kernel,
+        grid_spec=pltpu.PrefetchScalarGridSpec(
+            num_scalar_prefetch=1,
+            grid=(steps,),
+            in_specs=[
+                pl.BlockSpec((1, 2, tokens, width), lambda g, n: (g, 0, 0, 0)),
+                pl.BlockSpec((1, width, model), lambda g, n: (n[g], 0, 0)),
+            ],
+            out_specs=[fixed] * 2,
+        ),
+        out_shape=[jax.ShapeDtypeStruct((tokens, model), jnp.float32)] * 2,
+        compiler_params=pltpu.CompilerParams(vmem_limit_bytes=24 * MIB),
+        cost_estimate=pl.CostEstimate(
+            flops=4 * tokens * model * steps * width,
+            bytes_accessed=2 * steps * width * model + 8 * tokens * model,
+            transcendentals=0,
+        ),
+        name="share",
+    )(order, x, weight)
+
+
+def norm_kernel(hidden_ref, here_ref, beside_ref, gain_ref, resid_ref, normed_ref):
+    resid = hidden_ref[...].astype(jnp.float32) + here_ref[...] + beside_ref[...]
+    resid_ref[...] = resid
+    normed_ref[...] = rms_scale(resid, gain_ref[...]).astype(jnp.bfloat16)
+
+
+def norm_call(hidden, here, beside, gain):
+    return pl.pallas_call(
+        norm_kernel,
+        out_shape=[
+            jax.ShapeDtypeStruct(hidden.shape, jnp.float32),
+            jax.ShapeDtypeStruct(hidden.shape, jnp.bfloat16),
+        ],
+        compiler_params=pltpu.CompilerParams(vmem_limit_bytes=16 * MIB),
+        cost_estimate=pl.CostEstimate(
+            flops=8 * hidden.size, bytes_accessed=16 * hidden.size, transcendentals=0
+        ),
+        name="norm",
+    )(hidden, here, beside, gain.reshape(1, -1))
 
 
 def expert_kernel(half, counts, resident, *refs):
@@ -393,8 +483,7 @@
     far = lax.ppermute(near, "row", middle)
     far_out = lax.ppermute(far, "row", outward)
 
-    def send(place, block):
-        routed = route(place, block)
+    def send(routed):
         chips = [routed[:64]]
         chips += [
             lax.ppermute(routed[64 * r : 64 * (r + 1)], "col", xor_pairs(8, 2 * r))
@@ -413,16 +502,19 @@
             other.reshape(4, 2, CAP, model_width)
         ]
 
-    chips_0 = send(places[0], moe_in)
-    shared_0, near, cross = lax.optimization_barrier((share(chips_0), near, cross))
+    chips_0 = send(route(places[0], moe_in))
+    routed_1 = route(places[1], near)
+    shared_0, routed_1, cross = lax.optimization_barrier((share(chips_0), routed_1, cross))
     other_0 = swap_cores(shared_0)
-    chips_1 = send(places[1], near)
-    shared_1, cross_out, far = lax.optimization_barrier((share(chips_1), cross_out, far))
+    chips_1 = send(routed_1)
+    routed_2 = route(places[2], cross + cross_out)
+    shared_1, routed_2, far = lax.optimization_barrier((share(chips_1), routed_2, far))
     other_1 = swap_cores(shared_1)
-    chips_2 = send(places[2], cross + cross_out)
-    shared_2, far_out = lax.optimization_barrier((share(chips_2), far_out))
+    chips_2 = send(routed_2)
+    routed_3 = route(places[3], far + far_out)
+    shared_2, routed_3 = lax.optimization_barrier((share(chips_2), routed_3))
     other_2 = swap_cores(shared_2)
-    chips_3 = send(places[3], far + far_out)
+    chips_3 = send(routed_3)
     other_3 = swap_cores(share(chips_3))
 
     def expert_parts(*blocks):
@@ -456,17 +548,17 @@
     def narrow(total):
         return total.astype(jnp.bfloat16)
 
-    back_3 = give_back(parts[6], swap_cores(parts[7]))
-    back_2 = give_back(parts[4], swap_cores(parts[5]), back_3)
+    back_2 = give_back(parts[4], swap_cores(parts[5]))
+    back_3 = give_back(parts[6], swap_cores(parts[7]), back_2)
+    sum_2 = combine(gated[2], back_2)
+    hop = lax.ppermute(narrow(sum_2), "row", inward)
+    back_1 = give_back(parts[2], swap_cores(parts[3]), back_3)
     sum_3 = narrow(combine(gated[3], back_3))
     ends = lax.ppermute(sum_3, "row", [(0, 3), (3, 0)])
     inner = lax.ppermute(sum_3, "row", [(1, 3), (2, 0)])
-    back_1 = give_back(parts[2], swap_cores(parts[3]), back_2)
-    sum_2 = combine(gated[2], back_2)
-    hop = lax.ppermute(narrow(sum_2), "row", inward)
     back_0 = give_back(parts[0], swap_cores(parts[1]), back_1)
+    middles = lax.ppermute(narrow(sum_2 + hop.astype(jnp.float32)), "row", middle)
     beside = lax.ppermute(narrow(combine(gated[1], back_1)), "row", swap)
-    middles = lax.ppermute(narrow(sum_2 + hop.astype(jnp.float32)), "row", middle)
     total = residual + combine(gated[0], back_0)
     for arrived in (ends, inner, beside, middles):
         total += arrived.astype(jnp.float32)
@@ -497,16 +589,6 @@
 
     planes = row_count == 4 and col_count == 8 and w_in.shape[0] == 4
 
-    normed = rms_scale(hidden, attn_gain).astype(jnp.bfloat16)
-    if planes:
-        slots, gated = plane_places(expert_ids, gate_weights)
-        mine, other, w_out_late = gather_plane(normed, w_out)
-        even_odd = [[0, 2, 4, 6], [1, 3, 5, 7]]
-        w_out_mine = lax.all_gather(w_out_late, "col", axis=0, axis_index_groups=even_odd)
-    else:
-        gathered = lax.all_gather(normed, "col", axis=0, tiled=True)
-        w_out_all = lax.all_gather(w_out, "col", axis=0)
-
     row_index = lax.axis_index("row")
     places = jnp.arange(request_order.shape[0], dtype=jnp.int32)
     request = jnp.sum(jnp.where(places == row_index, request_order, 0))
@@ -519,36 +601,48 @@
     sine = jnp.concatenate([-sine, sine], axis=1)
 
     w_matrix = w_qkv.reshape(model_width, -1)
+    normed = rms_scale(hidden, attn_gain).astype(jnp.bfloat16)
     if planes:
         col = lax.axis_index("col")
-        chips = 2 * jnp.arange(4, dtype=jnp.int32)
-        fresh = qkv_call(col ^ chips, mine, w_matrix, cosine, sine, heads_here)
+        chips = jnp.arange(4, dtype=jnp.int32)
+        slots, gated = plane_places(expert_ids, gate_weights)
+        mine, other, w_out_late = gather_plane(normed, w_out)
+        even_odd = [[0, 2, 4, 6], [1, 3, 5, 7]]
+        w_out_mine = lax.all_gather(w_out_late, "col", axis=0, axis_index_groups=even_odd)
+        fresh = qkv_call(col ^ 2 * chips, mine, w_matrix, cosine, sine, heads_here)
         queries, new_keys, new_values = qkv_call(
-            col ^ chips ^ 1, other, w_matrix, cosine, sine, heads_here, fresh
+            col ^ 2 * chips ^ 1, other, w_matrix, cosine, sine, heads_here, fresh
         )
+        context = attention_call(
+            length, col, tok_rows, queries, cache_keys, cache_values, new_keys, new_values
+        )
+        arrived = [context[:2]] + [
+            lax.ppermute(context[2 * r : 2 * r + 2], "col", xor_pairs(8, 2 * r))
+            for r in range(1, 4)
+        ]
+        here, beside = share_call((col >> 1) ^ chips, jnp.stack(arrived), w_out_mine)
+        beside = lax.ppermute(beside, "col", xor_pairs(8, 1))
+        residual, moe_in = norm_call(hidden, here, beside, moe_gain)
+        new_hidden = experts_planes(moe_in, residual, slots, gated, w_in, w_down)
     else:
+        gathered = lax.all_gather(normed, "col", axis=0, tiled=True)
+        w_out_all = lax.all_gather(w_out, "col", axis=0)
         blocks = jnp.arange(col_count, dtype=jnp.int32)
         queries, new_keys, new_values = qkv_call(
             blocks, gathered, w_matrix, cosine, sine, heads_here
         )
-    context = attention_call(
-        length.reshape(1), queries, cache_keys, cache_values, new_keys, new_values
-    )
-    if planes:
-        w_out_mine, context = lax.optimization_barrier((w_out_mine, context))
-    shares = lax.all_to_all(
-        context.reshape(col_count, tok_rows, heads_here * HEAD), "col", 0, 0, tiled=True
-    )
-    if planes:
-        w_out_other = lax.ppermute(w_out_mine, "col", xor_pairs(8, 1))
-        core = col & 1
-        order = (chips[:, None] + jnp.stack([core, 1 - core])).reshape(-1)
-        residual, moe_in = project_call(
-            order, shares, [w_out_mine, w_out_other], hidden, moe_gain
+        context = attention_call(
+            length,
+            jnp.int32(0),
+            tok_rows,
+            queries,
+            cache_keys,
+            cache_values,
+            new_keys,
+            new_values,
         )
-        new_hidden = experts_planes(moe_in, residual, slots, gated, w_in, w_down)
-    else:
-        residual, moe_in = project_call(blocks, shares, [w_out_all], hidden, moe_gain)
+        shares = lax.all_to_all(context, "col", 0, 0, tiled=True)
+        residual, moe_in = project_call(blocks, [shares], [w_out_all], hidden, moe_gain)
         new_hidden = experts_direct(moe_in, residual, expert_ids, gate_weights, w_in, w_down)
     return (new_hidden, new_keys, new_values)
 

time: 293 us -> 278 us (0.949)
  Pallas kernels: 80.8 us -> 61.8 us
    pallas_call x1, Pallas kernels: 38.4 us -> 18.9 us  [attention_call(): pl.pallas_call(functools.partial(attention_kernel, heads, bq, bk), grid_s...]
    all_to_all x1 -> x0, waiting for transfers between devices: 9.41 us -> none  [body(): lax.all_to_all(context.reshape(col_count, tok_rows, heads_here * HEAD), '...]
    ppermute x1, waiting for transfers between devices: 3.55 us -> 10.6 us  [experts_planes(): beside = lax.ppermute(narrow(combine(gated[1], back_1)), 'row', swap)]
    ppermute x1 -> x4, waiting for transfers between devices: 0.01 us -> 7.06 us  [the longest x3 4.81 us: body(): lax.ppermute(context[2 * r:2 * r + 2], 'col', xor_pairs(8, 2 * r))]
    ppermute x1, waiting for transfers between devices: 5.05 us -> 0.01 us  [experts_planes(): hop = lax.ppermute(narrow(sum_2), 'row', inward)]
    ppermute x1, waiting for transfers between devices: 0.01 us -> 4.88 us  [experts_planes(): cross_out = lax.ppermute(cross, 'row', outward)]
    ppermute x3, waiting for transfers between devices: 4.39 us -> 0.01 us  [plane_places(): lax.ppermute(packed, 'row', xor_pairs(4, bits))]
    all_to_all x1 -> x0, starting transfers between devices: 3.51 us -> none  [body(): lax.all_to_all(context.reshape(col_count, tok_rows, heads_here * HEAD), '...]
  transfers between devices with their start and end apart: 53 -> 55, of which waited for: 25 -> 26; matrix products, arithmetic and copies ran while one was open for 7% -> 9% of each run, Pallas kernels for 16% -> 12%
where the time goes in v3:
time: 278 us; the launch traced here: 277 us
  waiting for transfers between devices  101 us (36%)
  starting transfers between devices  63.7 us (23%)
  Pallas kernels  61.8 us (22%)
  local copies, waits for them, and re-layouts  16.9 us (6%)
  between operations  15.1 us (5%)
  other arithmetic  12 us (4%)
  matrix products  6.91 us (2%)
    ppermute x12, waiting for transfers between devices, send(): lax.ppermute(routed[64 * r:64 * (r + 1)], 'col', xor_pairs(8, 2 * r))  35.8 us
    pallas_call x1, Pallas kernels, expert_call(): pl.pallas_call(functools.partial(expert_kernel, units, takes, resident),...  28.1 us
    pallas_call x1, Pallas kernels, attention_call(): pl.pallas_call(functools.partial(attention_kernel, heads, bq, bk), grid_s...  18.9 us
    ppermute x12, waiting for transfers between devices, give_back(): lax.ppermute(both[r], 'col', xor_pairs(8, 2 * r))  18.1 us
    ppermute x12, starting transfers between devices, give_back(): lax.ppermute(both[r], 'col', xor_pairs(8, 2 * r))  14.9 us
    ppermute x12, starting transfers between devices, send(): lax.ppermute(routed[64 * r:64 * (r + 1)], 'col', xor_pairs(8, 2 * r))  14.1 us
    pallas_call x2, Pallas kernels, qkv_call(): pl.pallas_call(functools.partial(qkv_kernel, heads), grid_spec=pltpu.Pref...  11.2 us
    ppermute x1, waiting for transfers between devices, experts_planes(): beside = lax.ppermute(narrow(combine(gated[1], back_1)), 'row', swap)  10.6 us
  transfers between devices with their start and end apart: 55, of which 26 were waited for; matrix products, arithmetic and copies ran while one was open for 9% of the time, Pallas kernels for 12%

profile of v3, /device:TPU:0, one launch (start us, length us, event | category | flops | bytes accessed | tf_op | source)
XLA Modules:
  0.0 277.3 jit_solution(8483534087383336314)
XLA Ops:
  11.2 2.9 %collective-permute-start = (bf16[128,2048]{1,0:T(8,128)(2,1)S(1)}, bf16[128,2048]{1,0:T(8,128)(2,1)S(1)}, u32[]{:S(2)}, u32[]{:S(2)}) collective-permute-start(bf16[128,2048]{1,0:T(8,128)(2,1)S(1)} %get-tuple-element.86), channel_id=1, source_target_pairs={{0,2},{1,3},{2,0},{3,1},{4,6},{5,7},{6,4},{7,5},{8,10},{9,11},{10,... | collective-permute-start | bytes 1572872 | tf_op jit(solution)/shard_map/ppermute | solution.py:403
  15.6 10.4 %collective-permute-done = bf16[128,2048]{1,0:T(8,128)(2,1)S(1)} collective-permute-done((bf16[128,2048]{1,0:T(8,128)(2,1)S(1)}, bf16[128,2048]{1,0:T(8,128)(2,1)S(1)}, u32[]{:S(2)}, u32[]{:S(2)}) %collective-permute-start) | collective-permute-done | bytes 524320 | tf_op jit(solution)/shard_map/ppermute | solution.py:403
  31.5 3.0 %collective-permute-done.2 = bf16[64,2048]{1,0:T(8,128)(2,1)S(1)} collective-permute-done((bf16[64,2048]{1,0:T(8,128)(2,1)S(1)}, bf16[64,2048]{1,0:T(8,128)(2,1)S(1)}, u32[]{:S(2)}, u32[]{:S(2)}) %collective-permute-start.2) | collective-permute-done | bytes 262176 | tf_op jit(solution)/shard_map/ppermute | solution.py:406
  37.4 2.7 collective-permute-start.10
  41.7 2.6 copy.24
  50.0 5.6 %qkv.2 = (bf16[1024,256]{1,0:T(8,128)(2,1)S(1)}, bf16[1024,256]{1,0:T(8,128)(2,1)}, bf16[1024,256]{1,0:T(8,128)(2,1)}) custom-call(s32[4]{0:T(128)S(1)} %multiply_xor_fusion.order_ref, bf16[512,2048]{1,0:T(8,128)(2,1)} %constant_dynamic-update-slice_fusion.x_ref, bf16[2048,768]{1,0:T(8,128)(2,1)S(1)} %bitcast.106, ...), custom_call_target="tpu_custom_call" | custom-call | flops 1610612736 | bytes 6029312 | tf_op jit(solution)/shard_map/qkv/pallas_call | solution.py:53
  55.6 5.6 %qkv.3 = (bf16[1024,256]{1,0:T(8,128)(2,1)S(1)}, bf16[1024,256]{1,0:T(8,128)(2,1)}, bf16[1024,256]{1,0:T(8,128)(2,1)}) custom-call(s32[4]{0:T(128)S(1)} %broadcast_xor_fusion.order_ref, bf16[512,2048]{1,0:T(8,128)(2,1)} %collective-permute-done.4.x_ref, bf16[2048,768]{1,0:T(8,128)(2,1)S(1)} %bitcast.107, ...), custom_call_target="tpu_custom_call", output_to_operand_aliasing={{0}: (5, {}), {1}: (6, {}), {2}: (7, {})} | custom-call | flops 1610612736 | bytes 6029312 | tf_op jit(solution)/shard_map/qkv/pallas_call | solution.py:53
  63.3 18.9 %attention.1 = bf16[8,128,256]{2,1,0:T(8,128)(2,1)S(1)} custom-call(s32[2]{0:T(128)S(1)} %pad_add_fusion.info_ref, bf16[1024,256]{1,0:T(8,128)(2,1)S(1)} %get-tuple-element.49.q_ref, bf16[1,4096,256]{2,1,0:T(8,128)(2,1)} %kc_ref.1, bf16[1,4096,256]{2,1,0:T(8,128)(2,1)} %vc_ref.1, bf16[1024,256]{1,0:T(8,128)(2,1)S(1)} %copy-done.2, ...), custom_call_target="tpu_custom_call" | custom-call | flops 5368709120 | bytes 6291456 | tf_op jit(solution)/shard_map/attention/pallas_call | solution.py:197
  83.4 2.4 collective-permute-start.7
  85.8 2.9 %collective-permute-done.5 = bf16[2,128,256]{2,1,0:T(8,128)(2,1)S(1)} collective-permute-done((bf16[2,128,256]{2,1,0:T(8,128)(2,1)S(1)}, bf16[2,128,256]{2,1,0:T(8,128)(2,1)S(1)}, u32[]{:S(2)}, u32[]{:S(2)}) %collective-permute-start.5) | collective-permute-done | bytes 131104 | tf_op jit(solution)/shard_map/ppermute | solution.py:620
  90.7 2.2 copy-done.1
  92.9 3.2 %share.1 = (f32[128,2048]{1,0:T(8,128)S(1)}, f32[128,2048]{1,0:T(8,128)S(1)}) custom-call(s32[4]{0:T(128)S(1)} %iota_xor_fusion.order_ref, bf16[4,2,128,256]{3,2,1,0:T(8,128)(2,1)S(1)} %pad_maximum_fusion.2.x_ref, bf16[4,256,2048]{2,1,0:T(8,128)(2,1)S(1)} %bitcast.108), custom_call_target="tpu_custom_call" | custom-call | flops 1073741824 | bytes 6291456 | tf_op jit(solution)/shard_map/share/pallas_call | solution.py:291
  96.6 2.2 collective-permute-done.8.beside_ref
  104.8 5.0 %collective-permute-done.12 = bf16[64,2048]{1,0:T(8,128)(2,1)S(1)} collective-permute-done((bf16[64,2048]{1,0:T(8,128)(2,1)S(1)}, bf16[64,2048]{1,0:T(8,128)(2,1)S(1)}, u32[]{:S(2)}, u32[]{:S(2)}) %collective-permute-start.12) | collective-permute-done | bytes 262176 | tf_op jit(solution)/shard_map/ppermute | solution.py:489
  109.7 6.1 %collective-permute-done.13 = bf16[64,2048]{1,0:T(8,128)(2,1)S(1)} collective-permute-done((bf16[64,2048]{1,0:T(8,128)(2,1)S(1)}, bf16[64,2048]{1,0:T(8,128)(2,1)S(1)}, u32[]{:S(2)}, u32[]{:S(2)}) %collective-permute-start.13) | collective-permute-done | bytes 262176 | tf_op jit(solution)/shard_map/ppermute | solution.py:489
  122.8 5.0 %collective-permute-done.18 = bf16[64,2048]{1,0:T(8,128)(2,1)S(1)} collective-permute-done((bf16[64,2048]{1,0:T(8,128)(2,1)S(1)}, bf16[64,2048]{1,0:T(8,128)(2,1)S(1)}, u32[]{:S(2)}, u32[]{:S(2)}) %collective-permute-start.18) | collective-permute-done | bytes 262176 | tf_op jit(solution)/shard_map/ppermute | solution.py:489
  127.8 3.7 %collective-permute-done.19 = bf16[64,2048]{1,0:T(8,128)(2,1)S(1)} collective-permute-done((bf16[64,2048]{1,0:T(8,128)(2,1)S(1)}, bf16[64,2048]{1,0:T(8,128)(2,1)S(1)}, u32[]{:S(2)}, u32[]{:S(2)}) %collective-permute-start.19) | collective-permute-done | bytes 262176 | tf_op jit(solution)/shard_map/ppermute | solution.py:489
  131.6 4.9 %collective-permute-done.21 = bf16[128,2048]{1,0:T(8,128)(2,1)S(1)} collective-permute-done((bf16[128,2048]{1,0:T(8,128)(2,1)S(1)}, bf16[128,2048]{1,0:T(8,128)(2,1)S(1)}, u32[]{:S(2)}, u32[]{:S(2)}) %collective-permute-start.21) | collective-permute-done | bytes 524320 | tf_op jit(solution)/shard_map/ppermute | solution.py:482
  142.6 5.2 %collective-permute-done.24 = bf16[64,2048]{1,0:T(8,128)(2,1)S(1)} collective-permute-done((bf16[64,2048]{1,0:T(8,128)(2,1)S(1)}, bf16[64,2048]{1,0:T(8,128)(2,1)S(1)}, u32[]{:S(2)}, u32[]{:S(2)}) %collective-permute-start.24) | collective-permute-done | bytes 262176 | tf_op jit(solution)/shard_map/ppermute | solution.py:489
  147.9 3.9 %collective-permute-done.25 = bf16[64,2048]{1,0:T(8,128)(2,1)S(1)} collective-permute-done((bf16[64,2048]{1,0:T(8,128)(2,1)S(1)}, bf16[64,2048]{1,0:T(8,128)(2,1)S(1)}, u32[]{:S(2)}, u32[]{:S(2)}) %collective-permute-start.25) | collective-permute-done | bytes 262176 | tf_op jit(solution)/shard_map/ppermute | solution.py:489
  159.0 3.0 %collective-permute-done.29 = bf16[64,2048]{1,0:T(8,128)(2,1)S(1)} collective-permute-done((bf16[64,2048]{1,0:T(8,128)(2,1)S(1)}, bf16[64,2048]{1,0:T(8,128)(2,1)S(1)}, u32[]{:S(2)}, u32[]{:S(2)}) %collective-permute-start.29) | collective-permute-done | bytes 262176 | tf_op jit(solution)/shard_map/ppermute | solution.py:489
  162.0 3.9 %collective-permute-done.30 = bf16[64,2048]{1,0:T(8,128)(2,1)S(1)} collective-permute-done((bf16[64,2048]{1,0:T(8,128)(2,1)S(1)}, bf16[64,2048]{1,0:T(8,128)(2,1)S(1)}, u32[]{:S(2)}, u32[]{:S(2)}) %collective-permute-start.30) | collective-permute-done | bytes 262176 | tf_op jit(solution)/shard_map/ppermute | solution.py:489
  168.8 28.1 %experts.1 = (bf16[4,2,16,2048]{3,2,1,0:T(8,128)(2,1)}, bf16[4,2,16,2048]{3,2,1,0:T(8,128)(2,1)}, bf16[4,2,16,2048]{3,2,1,0:T(8,128)(2,1)}, bf16[4,2,16,2048]{3,...) custom-call(bf16[2,2,16,2048]{3,2,1,0:T(8,128)(2,1)} %bitcast.146, ...), custom_call_target="tpu_custom_call" | custom-call | flops 17716740096 | bytes 42991616 | tf_op jit(solution)/shard_map/experts/pallas_call | solution.py:378
  206.3 5.0 %collective-permute-done.37 = bf16[64,2048]{1,0:T(8,128)(2,1)S(1)} collective-permute-done((bf16[64,2048]{1,0:T(8,128)(2,1)S(1)}, bf16[64,2048]{1,0:T(8,128)(2,1)S(1)}, u32[]{:S(2)}, u32[]{:S(2)}) %collective-permute-start.37) | collective-permute-done | bytes 262176 | tf_op jit(solution)/shard_map/ppermute | solution.py:537
  217.8 5.5 %collective-permute-start.52 = (bf16[128,2048]{1,0:T(8,128)(2,1)S(1)}, bf16[128,2048]{1,0:T(8,128)(2,1)S(1)}, u32[]{:S(2)}, u32[]{:S(2)}) collective-permute-start(bf16[128,2048]{1,0:T(8,128)(2,1)S(1)} %get-tuple-element.156), channel_id=1, source_target_pairs={{0,8},{24,16},{1,9},{25,17},{2,10},{26,18},{3,11},{27,19},{4,12},{... | collective-permute-start | bytes 1572872 | tf_op jit(solution)/shard_map/ppermute | solution.py:554
  225.9 2.5 collective-permute-done.44
  229.3 3.7 %collective-permute-start.45 = (bf16[128,2048]{1,0:T(8,128)(2,1)S(1)}, bf16[128,2048]{1,0:T(8,128)(2,1)S(1)}, u32[]{:S(2)}, u32[]{:S(2)}) collective-permute-start(bf16[128,2048]{1,0:T(8,128)(2,1)S(1)} %fusion.7), channel_id=1, source_target_pairs={{0,24},{24,0},{1,25},{25,1},{2,26},{26,2},{3,27},{27,3},{4,28},{28... | collective-permute-start | bytes 1572872 | tf_op jit(solution)/shard_map/ppermute | solution.py:557
  237.7 4.2 %collective-permute-done.48 = bf16[64,2048]{1,0:T(8,128)(2,1)S(1)} collective-permute-done((bf16[64,2048]{1,0:T(8,128)(2,1)S(1)}, bf16[64,2048]{1,0:T(8,128)(2,1)S(1)}, u32[]{:S(2)}, u32[]{:S(2)}) %collective-permute-start.48) | collective-permute-done | bytes 262176 | tf_op jit(solution)/shard_map/ppermute | solution.py:537
  245.5 4.7 %collective-permute-done.41 = bf16[64,2048]{1,0:T(8,128)(2,1)S(1)} collective-permute-done((bf16[64,2048]{1,0:T(8,128)(2,1)S(1)}, bf16[64,2048]{1,0:T(8,128)(2,1)S(1)}, u32[]{:S(2)}, u32[]{:S(2)}) %collective-permute-start.41) | collective-permute-done | bytes 262176 | tf_op jit(solution)/shard_map/ppermute | solution.py:537
  250.2 2.9 %collective-permute-start.49 = (bf16[128,2048]{1,0:T(8,128)(2,1)S(1)}, bf16[128,2048]{1,0:T(8,128)(2,1)S(1)}, u32[]{:S(2)}, u32[]{:S(2)}) collective-permute-start(bf16[128,2048]{1,0:T(8,128)(2,1)S(1)} %fusion.8), channel_id=1, source_target_pairs={{0,8},{8,0},{16,24},{24,16},{1,9},{9,1},{17,25},{25,17},{2,10},{10... | collective-permute-start | bytes 1572872 | tf_op jit(solution)/shard_map/ppermute | solution.py:561
  255.2 3.3 %collective-permute-done.46 = bf16[128,2048]{1,0:T(8,128)(2,1)S(1)} collective-permute-done((bf16[128,2048]{1,0:T(8,128)(2,1)S(1)}, bf16[128,2048]{1,0:T(8,128)(2,1)S(1)}, u32[]{:S(2)}, u32[]{:S(2)}) %collective-permute-start.46) | collective-permute-done | bytes 524320 | tf_op jit(solution)/shard_map/ppermute | solution.py:558
  258.5 10.6 %collective-permute-done.49 = bf16[128,2048]{1,0:T(8,128)(2,1)S(1)} collective-permute-done((bf16[128,2048]{1,0:T(8,128)(2,1)S(1)}, bf16[128,2048]{1,0:T(8,128)(2,1)S(1)}, u32[]{:S(2)}, u32[]{:S(2)}) %collective-permute-start.49) | collective-permute-done | bytes 524320 | tf_op jit(solution)/shard_map/ppermute | solution.py:561
  (252 shorter events, 86.3 us)
Async XLA Ops:
  7.2 83.5 %all-gather.3.cloned.1.call-start = ((), (), s32[]{:S(2)}) async-start(), calls=%async_computation | async-start | bytes 5242880 | tf_op jit(solution)/shard_map/all_gather | solution.py:611
  11.2 14.9 %collective-permute-start = (bf16[128,2048]{1,0:T(8,128)(2,1)S(1)}, bf16[128,2048]{1,0:T(8,128)(2,1)S(1)}, u32[]{:S(2)}, u32[]{:S(2)}) collective-permute-start(bf16[128,2048]{1,0:T(8,128)(2,1)S(1)} %get-tuple-element.86), channel_id=1, source_target_pairs={{0,2},{1,3},{2,0},{3,1},{4,6},{5,7},{6,4},{7,5},{8,10},{9,11},{10,... | collective-permute-start | bytes 1572872 | tf_op jit(solution)/shard_map/ppermute | solution.py:403
  14.1 13.4 %collective-permute-start.1 = (bf16[128,2048]{1,0:T(8,128)(2,1)S(1)}, bf16[128,2048]{1,0:T(8,128)(2,1)S(1)}, u32[]{:S(2)}, u32[]{:S(2)}) collective-permute-start(bf16[128,2048]{1,0:T(8,128)(2,1)S(1)} %get-tuple-element.86), channel_id=1, source_target_pairs={{0,4},{1,5},{2,6},{3,7},{4,0},{5,1},{6,2},{7,3},{8,12},{9,13},{10,... | collective-permute-start | bytes 1572872 | tf_op jit(solution)/shard_map/ppermute | solution.py:404
  37.4 18.3 %collective-permute-start.4 = (bf16[512,2048]{1,0:T(8,128)(2,1)}, bf16[512,2048]{1,0:T(8,128)(2,1)}, u32[]{:S(2)}, u32[]{:S(2)}) collective-permute-start(bf16[512,2048]{1,0:T(8,128)(2,1)} %constant_dynamic-update-slice_fusion.x_ref), channel_id=1, source_target_pairs={{0,1},{1,0},{2,3},{3,2},{4,5},{5,4},{6,7},{7,6},{8,9},{9,8},{10,11... | collective-permute-start | bytes 6291464 | tf_op jit(solution)/shard_map/ppermute | solution.py:409
  37.4 46.0 %collective-permute-start.10 = (f32[128,12]{0,1:T(8,128)S(1)}, f32[128,12]{0,1:T(8,128)S(1)}, u32[]{:S(2)}, u32[]{:S(2)}) collective-permute-start(f32[128,12]{0,1:T(8,128)S(1)} %get-tuple-element.152), channel_id=1, source_target_pairs={{0,16},{8,24},{16,0},{24,8},{1,17},{9,25},{17,1},{25,9},{2,18},{10... | collective-permute-start | bytes 18440 | tf_op jit(solution)/shard_map/ppermute | solution.py:465
  40.1 45.7 %collective-permute-start.11 = (f32[128,12]{0,1:T(8,128)S(1)}, f32[128,12]{0,1:T(8,128)S(1)}, u32[]{:S(2)}, u32[]{:S(2)}) collective-permute-start(f32[128,12]{0,1:T(8,128)S(1)} %get-tuple-element.152), channel_id=1, source_target_pairs={{0,24},{8,16},{16,8},{24,0},{1,25},{9,17},{17,9},{25,1},{2,26},{10... | collective-permute-start | bytes 18440 | tf_op jit(solution)/shard_map/ppermute | solution.py:465
  41.4 54.8 %collective-permute-start.9 = (f32[128,12]{0,1:T(8,128)S(1)}, f32[128,12]{0,1:T(8,128)S(1)}, u32[]{:S(2)}, u32[]{:S(2)}) collective-permute-start(f32[128,12]{0,1:T(8,128)S(1)} %get-tuple-element.152), channel_id=1, source_target_pairs={{0,8},{8,0},{16,24},{24,16},{1,9},{9,1},{17,25},{25,17},{2,10},{10... | collective-permute-start | bytes 18440 | tf_op jit(solution)/shard_map/ppermute | solution.py:465
  99.3 16.7 %collective-permute-start.15 = (bf16[128,2048]{1,0:T(8,128)(2,1)S(1)}, bf16[128,2048]{1,0:T(8,128)(2,1)S(1)}, u32[]{:S(2)}, u32[]{:S(2)}) collective-permute-start(bf16[128,2048]{1,0:T(8,128)(2,1)S(1)} %get-tuple-element.56), channel_id=1, source_target_pairs={{0,8},{8,0},{16,24},{24,16},{1,9},{9,1},{17,25},{25,17},{2,10},{10... | collective-permute-start | bytes 1572872 | tf_op jit(solution)/shard_map/ppermute | solution.py:480
  102.1 13.7 %collective-permute-start.13 = (bf16[64,2048]{1,0:T(8,128)(2,1)S(1)}, bf16[64,2048]{1,0:T(8,128)(2,1)S(1)}, u32[]{:S(2)}, u32[]{:S(2)}) collective-permute-start(bf16[64,2048]{1,0:T(8,128)(2,1)S(1)} %get-tuple-element.100), channel_id=1, source_target_pairs={{0,4},{1,5},{2,6},{3,7},{4,0},{5,1},{6,2},{7,3},{8,12},{9,13},{10,... | collective-permute-start | bytes 786440 | tf_op jit(solution)/shard_map/ppermute | solution.py:489
  102.5 13.3 %collective-permute-start.14 = (bf16[64,2048]{1,0:T(8,128)(2,1)S(1)}, bf16[64,2048]{1,0:T(8,128)(2,1)S(1)}, u32[]{:S(2)}, u32[]{:S(2)}) collective-permute-start(bf16[64,2048]{1,0:T(8,128)(2,1)S(1)} %get-tuple-element.99), channel_id=1, source_target_pairs={{0,6},{1,7},{2,4},{3,5},{4,2},{5,3},{6,0},{7,1},{8,14},{9,15},{10,... | collective-permute-start | bytes 786440 | tf_op jit(solution)/shard_map/ppermute | solution.py:489
  104.1 12.3 %collective-permute-start.16 = (bf16[128,2048]{1,0:T(8,128)(2,1)S(1)}, bf16[128,2048]{1,0:T(8,128)(2,1)S(1)}, u32[]{:S(2)}, u32[]{:S(2)}) collective-permute-start(bf16[128,2048]{1,0:T(8,128)(2,1)S(1)} %get-tuple-element.56), channel_id=1, source_target_pairs={{8,16},{16,8},{9,17},{17,9},{10,18},{18,10},{11,19},{19,11},{12,20... | collective-permute-start | bytes 1572872 | tf_op jit(solution)/shard_map/ppermute | solution.py:481
  116.4 20.1 %collective-permute-start.21 = (bf16[128,2048]{1,0:T(8,128)(2,1)S(1)}, bf16[128,2048]{1,0:T(8,128)(2,1)S(1)}, u32[]{:S(2)}, u32[]{:S(2)}) collective-permute-start(bf16[128,2048]{1,0:T(8,128)(2,1)S(1)} %collective-permute-done.16), channel_id=1, source_target_pairs={{8,0},{16,24},{9,1},{17,25},{10,2},{18,26},{11,3},{19,27},{12,4},{... | collective-permute-start | bytes 1572872 | tf_op jit(solution)/shard_map/ppermute | solution.py:482
  119.0 12.5 %collective-permute-start.19 = (bf16[64,2048]{1,0:T(8,128)(2,1)S(1)}, bf16[64,2048]{1,0:T(8,128)(2,1)S(1)}, u32[]{:S(2)}, u32[]{:S(2)}) collective-permute-start(bf16[64,2048]{1,0:T(8,128)(2,1)S(1)} %get-tuple-element.96), channel_id=1, source_target_pairs={{0,4},{1,5},{2,6},{3,7},{4,0},{5,1},{6,2},{7,3},{8,12},{9,13},{10,... | collective-permute-start | bytes 786440 | tf_op jit(solution)/shard_map/ppermute | solution.py:489
  120.3 11.3 %collective-permute-start.20 = (bf16[64,2048]{1,0:T(8,128)(2,1)S(1)}, bf16[64,2048]{1,0:T(8,128)(2,1)S(1)}, u32[]{:S(2)}, u32[]{:S(2)}) collective-permute-start(bf16[64,2048]{1,0:T(8,128)(2,1)S(1)} %get-tuple-element.95), channel_id=1, source_target_pairs={{0,6},{1,7},{2,4},{3,5},{4,2},{5,3},{6,0},{7,1},{8,14},{9,15},{10,... | collective-permute-start | bytes 786440 | tf_op jit(solution)/shard_map/ppermute | solution.py:489
  122.1 14.9 %collective-permute-start.22 = (bf16[128,2048]{1,0:T(8,128)(2,1)S(1)}, bf16[128,2048]{1,0:T(8,128)(2,1)S(1)}, u32[]{:S(2)}, u32[]{:S(2)}) collective-permute-start(bf16[128,2048]{1,0:T(8,128)(2,1)S(1)} %collective-permute-done.15), channel_id=1, source_target_pairs={{8,16},{16,8},{9,17},{17,9},{10,18},{18,10},{11,19},{19,11},{12,20... | collective-permute-start | bytes 1572872 | tf_op jit(solution)/shard_map/ppermute | solution.py:483
  136.9 16.7 %collective-permute-start.27 = (bf16[128,2048]{1,0:T(8,128)(2,1)S(1)}, bf16[128,2048]{1,0:T(8,128)(2,1)S(1)}, u32[]{:S(2)}, u32[]{:S(2)}) collective-permute-start(bf16[128,2048]{1,0:T(8,128)(2,1)S(1)} %collective-permute-done.22), channel_id=1, source_target_pairs={{8,0},{16,24},{9,1},{17,25},{10,2},{18,26},{11,3},{19,27},{12,4},{... | collective-permute-start | bytes 1572872 | tf_op jit(solution)/shard_map/ppermute | solution.py:484
  140.5 11.3 %collective-permute-start.25 = (bf16[64,2048]{1,0:T(8,128)(2,1)S(1)}, bf16[64,2048]{1,0:T(8,128)(2,1)S(1)}, u32[]{:S(2)}, u32[]{:S(2)}) collective-permute-start(bf16[64,2048]{1,0:T(8,128)(2,1)S(1)} %get-tuple-element.92), channel_id=1, source_target_pairs={{0,4},{1,5},{2,6},{3,7},{4,0},{5,1},{6,2},{7,3},{8,12},{9,13},{10,... | collective-permute-start | bytes 786440 | tf_op jit(solution)/shard_map/ppermute | solution.py:489
  202.8 14.6 %collective-permute-start.50 = (bf16[64,2048]{1,0:T(8,128)(2,1)S(1)}, bf16[64,2048]{1,0:T(8,128)(2,1)S(1)}, u32[]{:S(2)}, u32[]{:S(2)}) collective-permute-start(bf16[64,2048]{1,0:T(8,128)(2,1)S(1)} %pad_maximum_fusion.20), channel_id=1, source_target_pairs={{0,4},{1,5},{2,6},{3,7},{4,0},{5,1},{6,2},{7,3},{8,12},{9,13},{10,... | collective-permute-start | bytes 786440 | tf_op jit(solution)/shard_map/ppermute | solution.py:537
  204.0 13.1 %collective-permute-start.51 = (bf16[64,2048]{1,0:T(8,128)(2,1)S(1)}, bf16[64,2048]{1,0:T(8,128)(2,1)S(1)}, u32[]{:S(2)}, u32[]{:S(2)}) collective-permute-start(bf16[64,2048]{1,0:T(8,128)(2,1)S(1)} %pad_maximum_fusion.21), channel_id=1, source_target_pairs={{0,6},{1,7},{2,4},{3,5},{4,2},{5,3},{6,0},{7,1},{8,14},{9,15},{10,... | collective-permute-start | bytes 786440 | tf_op jit(solution)/shard_map/ppermute | solution.py:537
  211.3 12.0 %collective-permute-start.38 = (bf16[64,2048]{1,0:T(8,128)(2,1)S(1)}, bf16[64,2048]{1,0:T(8,128)(2,1)S(1)}, u32[]{:S(2)}, u32[]{:S(2)}) collective-permute-start(bf16[64,2048]{1,0:T(8,128)(2,1)S(1)} %pad_maximum_fusion.16), channel_id=1, source_target_pairs={{0,2},{1,3},{2,0},{3,1},{4,6},{5,7},{6,4},{7,5},{8,10},{9,11},{10,... | collective-permute-start | bytes 786440 | tf_op jit(solution)/shard_map/ppermute | solution.py:537
  212.0 16.4 %collective-permute-start.44 = (bf16[64,2048]{1,0:T(8,128)(2,1)S(1)}, bf16[64,2048]{1,0:T(8,128)(2,1)S(1)}, u32[]{:S(2)}, u32[]{:S(2)}) collective-permute-start(bf16[64,2048]{1,0:T(8,128)(2,1)S(1)} %pad_maximum_fusion.18), channel_id=1, source_target_pairs={{0,6},{1,7},{2,4},{3,5},{4,2},{5,3},{6,0},{7,1},{8,14},{9,15},{10,... | collective-permute-start | bytes 786440 | tf_op jit(solution)/shard_map/ppermute | solution.py:537
  213.5 15.2 %collective-permute-start.43 = (bf16[64,2048]{1,0:T(8,128)(2,1)S(1)}, bf16[64,2048]{1,0:T(8,128)(2,1)S(1)}, u32[]{:S(2)}, u32[]{:S(2)}) collective-permute-start(bf16[64,2048]{1,0:T(8,128)(2,1)S(1)} %pad_maximum_fusion.17), channel_id=1, source_target_pairs={{0,4},{1,5},{2,6},{3,7},{4,0},{5,1},{6,2},{7,3},{8,12},{9,13},{10,... | collective-permute-start | bytes 786440 | tf_op jit(solution)/shard_map/ppermute | solution.py:537
  217.8 25.5 %collective-permute-start.52 = (bf16[128,2048]{1,0:T(8,128)(2,1)S(1)}, bf16[128,2048]{1,0:T(8,128)(2,1)S(1)}, u32[]{:S(2)}, u32[]{:S(2)}) collective-permute-start(bf16[128,2048]{1,0:T(8,128)(2,1)S(1)} %get-tuple-element.156), channel_id=1, source_target_pairs={{0,8},{24,16},{1,9},{25,17},{2,10},{26,18},{3,11},{27,19},{4,12},{... | collective-permute-start | bytes 1572872 | tf_op jit(solution)/shard_map/ppermute | solution.py:554
  223.2 11.1 %collective-permute-start.39 = (bf16[64,2048]{1,0:T(8,128)(2,1)S(1)}, bf16[64,2048]{1,0:T(8,128)(2,1)S(1)}, u32[]{:S(2)}, u32[]{:S(2)}) collective-permute-start(bf16[64,2048]{1,0:T(8,128)(2,1)S(1)} %pad_maximum_fusion.12), channel_id=1, source_target_pairs={{0,2},{1,3},{2,0},{3,1},{4,6},{5,7},{6,4},{7,5},{8,10},{9,11},{10,... | collective-permute-start | bytes 786440 | tf_op jit(solution)/shard_map/ppermute | solution.py:537
  223.9 12.3 %collective-permute-start.47 = (bf16[64,2048]{1,0:T(8,128)(2,1)S(1)}, bf16[64,2048]{1,0:T(8,128)(2,1)S(1)}, u32[]{:S(2)}, u32[]{:S(2)}) collective-permute-start(bf16[64,2048]{1,0:T(8,128)(2,1)S(1)} %pad_maximum_fusion.13), channel_id=1, source_target_pairs={{0,4},{1,5},{2,6},{3,7},{4,0},{5,1},{6,2},{7,3},{8,12},{9,13},{10,... | collective-permute-start | bytes 786440 | tf_op jit(solution)/shard_map/ppermute | solution.py:537
  229.3 25.8 %collective-permute-start.45 = (bf16[128,2048]{1,0:T(8,128)(2,1)S(1)}, bf16[128,2048]{1,0:T(8,128)(2,1)S(1)}, u32[]{:S(2)}, u32[]{:S(2)}) collective-permute-start(bf16[128,2048]{1,0:T(8,128)(2,1)S(1)} %fusion.7), channel_id=1, source_target_pairs={{0,24},{24,0},{1,25},{25,1},{2,26},{26,2},{3,27},{27,3},{4,28},{28... | collective-permute-start | bytes 1572872 | tf_op jit(solution)/shard_map/ppermute | solution.py:557
  233.1 25.4 %collective-permute-start.46 = (bf16[128,2048]{1,0:T(8,128)(2,1)S(1)}, bf16[128,2048]{1,0:T(8,128)(2,1)S(1)}, u32[]{:S(2)}, u32[]{:S(2)}) collective-permute-start(bf16[128,2048]{1,0:T(8,128)(2,1)S(1)} %fusion.7), channel_id=1, source_target_pairs={{8,24},{16,0},{9,25},{17,1},{10,26},{18,2},{11,27},{19,3},{12,28},... | collective-permute-start | bytes 1572872 | tf_op jit(solution)/shard_map/ppermute | solution.py:558
  236.2 14.0 %collective-permute-start.41 = (bf16[64,2048]{1,0:T(8,128)(2,1)S(1)}, bf16[64,2048]{1,0:T(8,128)(2,1)S(1)}, u32[]{:S(2)}, u32[]{:S(2)}) collective-permute-start(bf16[64,2048]{1,0:T(8,128)(2,1)S(1)} %pad_maximum_fusion.9), channel_id=1, source_target_pairs={{0,4},{1,5},{2,6},{3,7},{4,0},{5,1},{6,2},{7,3},{8,12},{9,13},{10,... | collective-permute-start | bytes 786440 | tf_op jit(solution)/shard_map/ppermute | solution.py:537
  241.9 11.6 %collective-permute-start.40 = (bf16[64,2048]{1,0:T(8,128)(2,1)S(1)}, bf16[64,2048]{1,0:T(8,128)(2,1)S(1)}, u32[]{:S(2)}, u32[]{:S(2)}) collective-permute-start(bf16[64,2048]{1,0:T(8,128)(2,1)S(1)} %pad_maximum_fusion.8), channel_id=1, source_target_pairs={{0,2},{1,3},{2,0},{3,1},{4,6},{5,7},{6,4},{7,5},{8,10},{9,11},{10,... | collective-permute-start | bytes 786440 | tf_op jit(solution)/shard_map/ppermute | solution.py:537
  243.3 11.2 %collective-permute-start.42 = (bf16[64,2048]{1,0:T(8,128)(2,1)S(1)}, bf16[64,2048]{1,0:T(8,128)(2,1)S(1)}, u32[]{:S(2)}, u32[]{:S(2)}) collective-permute-start(bf16[64,2048]{1,0:T(8,128)(2,1)S(1)} %pad_maximum_fusion.10), channel_id=1, source_target_pairs={{0,6},{1,7},{2,4},{3,5},{4,2},{5,3},{6,0},{7,1},{8,14},{9,15},{10,... | collective-permute-start | bytes 786440 | tf_op jit(solution)/shard_map/ppermute | solution.py:537
  250.2 18.9 %collective-permute-start.49 = (bf16[128,2048]{1,0:T(8,128)(2,1)S(1)}, bf16[128,2048]{1,0:T(8,128)(2,1)S(1)}, u32[]{:S(2)}, u32[]{:S(2)}) collective-permute-start(bf16[128,2048]{1,0:T(8,128)(2,1)S(1)} %fusion.8), channel_id=1, source_target_pairs={{0,8},{8,0},{16,24},{24,16},{1,9},{9,1},{17,25},{25,17},{2,10},{10... | collective-permute-start | bytes 1572872 | tf_op jit(solution)/shard_map/ppermute | solution.py:561
  253.5 15.7 %collective-permute-start.53 = (bf16[128,2048]{1,0:T(8,128)(2,1)S(1)}, bf16[128,2048]{1,0:T(8,128)(2,1)S(1)}, u32[]{:S(2)}, u32[]{:S(2)}) collective-permute-start(bf16[128,2048]{1,0:T(8,128)(2,1)S(1)} %add_convert_fusion.1), channel_id=1, source_target_pairs={{8,16},{16,8},{9,17},{17,9},{10,18},{18,10},{11,19},{19,11},{12,20... | collective-permute-start | bytes 1572872 | tf_op jit(solution)/shard_map/ppermute | solution.py:560
  (52 other events, 284.1 us)
Sparse Core Ops, SparseCore 0:
  27.6 53.0 all-gather.2

commit v4 on v3

--- a/solution.py
+++ b/solution.py
@@ -191,7 +191,7 @@
     rows, width = q.shape
     heads = width // HEAD
     cache_rows = cache_keys.shape[1]
-    bq, bk = min(512, rows), min(1024, cache_rows)
+    bq, bk = min(512, rows), min(2048, cache_rows)
     fixed = lambda shape: pl.BlockSpec(shape, lambda i, n: (0,) * len(shape))
     out_shape = (rows // tokens, tokens, width)
     return pl.pallas_call(

time: 278 us -> 287 us (1.032)
  starting transfers between devices: 63.7 us -> 72.1 us
  Pallas kernels: 61.8 us -> 70.1 us
  waiting for transfers between devices: 101 us -> 94.8 us
    pallas_call x1, Pallas kernels: 18.9 us -> 27.5 us  [attention_call(): pl.pallas_call(functools.partial(attention_kernel, heads, bq, bk), grid_s...]
    ppermute x1, starting transfers between devices: 0.07 us -> 8.29 us  [experts_planes(): near = lax.ppermute(moe_in, 'row', swap)]
    ppermute x1, waiting for transfers between devices: 4.88 us -> 0.01 us  [experts_planes(): cross_out = lax.ppermute(cross, 'row', outward)]
  transfers between devices with their start and end apart: 55 -> 55, of which waited for: 26 -> 25; matrix products, arithmetic and copies ran while one was open for 9% -> 8% of each run, Pallas kernels for 12% -> 14%
where the time goes in v4:
time: 287 us; the launch traced here: 288 us
  waiting for transfers between devices  94.8 us (33%)
  starting transfers between devices  72.1 us (25%)
  Pallas kernels  70.1 us (24%)
  local copies, waits for them, and re-layouts  16.9 us (6%)
  between operations  15.3 us (5%)
  other arithmetic  12 us (4%)
  matrix products  6.91 us (2%)
    ppermute x12, waiting for transfers between devices, send(): lax.ppermute(routed[64 * r:64 * (r + 1)], 'col', xor_pairs(8, 2 * r))  35.5 us
    pallas_call x1, Pallas kernels, expert_call(): pl.pallas_call(functools.partial(expert_kernel, units, takes, resident),...  28.1 us
    pallas_call x1, Pallas kernels, attention_call(): pl.pallas_call(functools.partial(attention_kernel, heads, bq, bk), grid_s...  27.5 us
    ppermute x12, waiting for transfers between devices, give_back(): lax.ppermute(both[r], 'col', xor_pairs(8, 2 * r))  17.8 us
    ppermute x12, starting transfers between devices, give_back(): lax.ppermute(both[r], 'col', xor_pairs(8, 2 * r))  14.9 us
    ppermute x12, starting transfers between devices, send(): lax.ppermute(routed[64 * r:64 * (r + 1)], 'col', xor_pairs(8, 2 * r))  14.1 us
    ppermute x1, waiting for transfers between devices, experts_planes(): beside = lax.ppermute(narrow(combine(gated[1], back_1)), 'row', swap)  11.1 us
    pallas_call x2, Pallas kernels, qkv_call(): pl.pallas_call(functools.partial(qkv_kernel, heads), grid_spec=pltpu.Pref...  11 us
  transfers between devices with their start and end apart: 55, of which 25 were waited for; matrix products, arithmetic and copies ran while one was open for 8% of the time, Pallas kernels for 14%

profile of v4, /device:TPU:0, one launch (start us, length us, event | category | flops | bytes accessed | tf_op | source)
XLA Modules:
  0.0 288.0 jit_solution(451550429045798776)
XLA Ops:
  11.2 2.9 %collective-permute-start = (bf16[128,2048]{1,0:T(8,128)(2,1)S(1)}, bf16[128,2048]{1,0:T(8,128)(2,1)S(1)}, u32[]{:S(2)}, u32[]{:S(2)}) collective-permute-start(bf16[128,2048]{1,0:T(8,128)(2,1)S(1)} %get-tuple-element.86), channel_id=1, source_target_pairs={{0,2},{1,3},{2,0},{3,1},{4,6},{5,7},{6,4},{7,5},{8,10},{9,11},{10,... | collective-permute-start | bytes 1572872 | tf_op jit(solution)/shard_map/ppermute | solution.py:403
  15.6 10.4 %collective-permute-done = bf16[128,2048]{1,0:T(8,128)(2,1)S(1)} collective-permute-done((bf16[128,2048]{1,0:T(8,128)(2,1)S(1)}, bf16[128,2048]{1,0:T(8,128)(2,1)S(1)}, u32[]{:S(2)}, u32[]{:S(2)}) %collective-permute-start) | collective-permute-done | bytes 524320 | tf_op jit(solution)/shard_map/ppermute | solution.py:403
  31.5 3.0 %collective-permute-done.2 = bf16[64,2048]{1,0:T(8,128)(2,1)S(1)} collective-permute-done((bf16[64,2048]{1,0:T(8,128)(2,1)S(1)}, bf16[64,2048]{1,0:T(8,128)(2,1)S(1)}, u32[]{:S(2)}, u32[]{:S(2)}) %collective-permute-start.2) | collective-permute-done | bytes 262176 | tf_op jit(solution)/shard_map/ppermute | solution.py:406
  37.4 2.7 collective-permute-start.10
  41.7 2.6 copy.24
  50.0 5.4 %qkv.2 = (bf16[1024,256]{1,0:T(8,128)(2,1)S(1)}, bf16[1024,256]{1,0:T(8,128)(2,1)}, bf16[1024,256]{1,0:T(8,128)(2,1)}) custom-call(s32[4]{0:T(128)S(1)} %multiply_xor_fusion.order_ref, bf16[512,2048]{1,0:T(8,128)(2,1)} %constant_dynamic-update-slice_fusion.x_ref, bf16[2048,768]{1,0:T(8,128)(2,1)S(1)} %bitcast.106, ...), custom_call_target="tpu_custom_call" | custom-call | flops 1610612736 | bytes 6029312 | tf_op jit(solution)/shard_map/qkv/pallas_call | solution.py:53
  55.5 5.6 %qkv.3 = (bf16[1024,256]{1,0:T(8,128)(2,1)S(1)}, bf16[1024,256]{1,0:T(8,128)(2,1)}, bf16[1024,256]{1,0:T(8,128)(2,1)}) custom-call(s32[4]{0:T(128)S(1)} %broadcast_xor_fusion.order_ref, bf16[512,2048]{1,0:T(8,128)(2,1)} %collective-permute-done.4.x_ref, bf16[2048,768]{1,0:T(8,128)(2,1)S(1)} %bitcast.107, ...), custom_call_target="tpu_custom_call", output_to_operand_aliasing={{0}: (5, {}), {1}: (6, {}), {2}: (7, {})} | custom-call | flops 1610612736 | bytes 6029312 | tf_op jit(solution)/shard_map/qkv/pallas_call | solution.py:53
  63.1 27.5 %attention.1 = bf16[8,128,256]{2,1,0:T(8,128)(2,1)S(1)} custom-call(s32[2]{0:T(128)S(1)} %pad_add_fusion.info_ref, bf16[1024,256]{1,0:T(8,128)(2,1)S(1)} %get-tuple-element.49.q_ref, bf16[1,4096,256]{2,1,0:T(8,128)(2,1)} %kc_ref.1, bf16[1,4096,256]{2,1,0:T(8,128)(2,1)} %vc_ref.1, bf16[1024,256]{1,0:T(8,128)(2,1)S(1)} %copy-done.2, ...), custom_call_target="tpu_custom_call" | custom-call | flops 5368709120 | bytes 6291456 | tf_op jit(solution)/shard_map/attention/pallas_call | solution.py:197
  91.9 2.4 collective-permute-start.7
  94.3 2.9 collective-permute-done.5
  99.3 2.2 copy-done.1
  101.5 3.0 %share.1 = (f32[128,2048]{1,0:T(8,128)S(1)}, f32[128,2048]{1,0:T(8,128)S(1)}) custom-call(s32[4]{0:T(128)S(1)} %iota_xor_fusion.order_ref, bf16[4,2,128,256]{3,2,1,0:T(8,128)(2,1)S(1)} %pad_maximum_fusion.2.x_ref, bf16[4,256,2048]{2,1,0:T(8,128)(2,1)S(1)} %bitcast.108), custom_call_target="tpu_custom_call" | custom-call | flops 1073741824 | bytes 6291456 | tf_op jit(solution)/shard_map/share/pallas_call | solution.py:291
  105.0 2.2 collective-permute-done.8.beside_ref
  107.6 8.3 %collective-permute-start.15 = (bf16[128,2048]{1,0:T(8,128)(2,1)S(1)}, bf16[128,2048]{1,0:T(8,128)(2,1)S(1)}, u32[]{:S(2)}, u32[]{:S(2)}) collective-permute-start(bf16[128,2048]{1,0:T(8,128)(2,1)S(1)} %get-tuple-element.56), channel_id=1, source_target_pairs={{0,8},{8,0},{16,24},{24,16},{1,9},{9,1},{17,25},{25,17},{2,10},{10... | collective-permute-start | bytes 1572872 | tf_op jit(solution)/shard_map/ppermute | solution.py:480
  121.3 5.0 %collective-permute-done.12 = bf16[64,2048]{1,0:T(8,128)(2,1)S(1)} collective-permute-done((bf16[64,2048]{1,0:T(8,128)(2,1)S(1)}, bf16[64,2048]{1,0:T(8,128)(2,1)S(1)}, u32[]{:S(2)}, u32[]{:S(2)}) %collective-permute-start.12) | collective-permute-done | bytes 262176 | tf_op jit(solution)/shard_map/ppermute | solution.py:489
  126.3 5.7 %collective-permute-done.13 = bf16[64,2048]{1,0:T(8,128)(2,1)S(1)} collective-permute-done((bf16[64,2048]{1,0:T(8,128)(2,1)S(1)}, bf16[64,2048]{1,0:T(8,128)(2,1)S(1)}, u32[]{:S(2)}, u32[]{:S(2)}) %collective-permute-start.13) | collective-permute-done | bytes 262176 | tf_op jit(solution)/shard_map/ppermute | solution.py:489
  139.0 5.0 %collective-permute-done.18 = bf16[64,2048]{1,0:T(8,128)(2,1)S(1)} collective-permute-done((bf16[64,2048]{1,0:T(8,128)(2,1)S(1)}, bf16[64,2048]{1,0:T(8,128)(2,1)S(1)}, u32[]{:S(2)}, u32[]{:S(2)}) %collective-permute-start.18) | collective-permute-done | bytes 262176 | tf_op jit(solution)/shard_map/ppermute | solution.py:489
  144.0 3.5 %collective-permute-done.19 = bf16[64,2048]{1,0:T(8,128)(2,1)S(1)} collective-permute-done((bf16[64,2048]{1,0:T(8,128)(2,1)S(1)}, bf16[64,2048]{1,0:T(8,128)(2,1)S(1)}, u32[]{:S(2)}, u32[]{:S(2)}) %collective-permute-start.19) | collective-permute-done | bytes 262176 | tf_op jit(solution)/shard_map/ppermute | solution.py:489
  153.8 5.0 %collective-permute-done.24 = bf16[64,2048]{1,0:T(8,128)(2,1)S(1)} collective-permute-done((bf16[64,2048]{1,0:T(8,128)(2,1)S(1)}, bf16[64,2048]{1,0:T(8,128)(2,1)S(1)}, u32[]{:S(2)}, u32[]{:S(2)}) %collective-permute-start.24) | collective-permute-done | bytes 262176 | tf_op jit(solution)/shard_map/ppermute | solution.py:489
  158.7 4.3 %collective-permute-done.25 = bf16[64,2048]{1,0:T(8,128)(2,1)S(1)} collective-permute-done((bf16[64,2048]{1,0:T(8,128)(2,1)S(1)}, bf16[64,2048]{1,0:T(8,128)(2,1)S(1)}, u32[]{:S(2)}, u32[]{:S(2)}) %collective-permute-start.25) | collective-permute-done | bytes 262176 | tf_op jit(solution)/shard_map/ppermute | solution.py:489
  169.8 3.0 %collective-permute-done.29 = bf16[64,2048]{1,0:T(8,128)(2,1)S(1)} collective-permute-done((bf16[64,2048]{1,0:T(8,128)(2,1)S(1)}, bf16[64,2048]{1,0:T(8,128)(2,1)S(1)}, u32[]{:S(2)}, u32[]{:S(2)}) %collective-permute-start.29) | collective-permute-done | bytes 262176 | tf_op jit(solution)/shard_map/ppermute | solution.py:489
  172.9 3.9 %collective-permute-done.30 = bf16[64,2048]{1,0:T(8,128)(2,1)S(1)} collective-permute-done((bf16[64,2048]{1,0:T(8,128)(2,1)S(1)}, bf16[64,2048]{1,0:T(8,128)(2,1)S(1)}, u32[]{:S(2)}, u32[]{:S(2)}) %collective-permute-start.30) | collective-permute-done | bytes 262176 | tf_op jit(solution)/shard_map/ppermute | solution.py:489
  179.7 28.1 %experts.1 = (bf16[4,2,16,2048]{3,2,1,0:T(8,128)(2,1)}, bf16[4,2,16,2048]{3,2,1,0:T(8,128)(2,1)}, bf16[4,2,16,2048]{3,2,1,0:T(8,128)(2,1)}, bf16[4,2,16,2048]{3,...) custom-call(bf16[2,2,16,2048]{3,2,1,0:T(8,128)(2,1)} %bitcast.146, ...), custom_call_target="tpu_custom_call" | custom-call | flops 17716740096 | bytes 42991616 | tf_op jit(solution)/shard_map/experts/pallas_call | solution.py:378
  217.3 5.0 %collective-permute-done.37 = bf16[64,2048]{1,0:T(8,128)(2,1)S(1)} collective-permute-done((bf16[64,2048]{1,0:T(8,128)(2,1)S(1)}, bf16[64,2048]{1,0:T(8,128)(2,1)S(1)}, u32[]{:S(2)}, u32[]{:S(2)}) %collective-permute-start.37) | collective-permute-done | bytes 262176 | tf_op jit(solution)/shard_map/ppermute | solution.py:537
  228.6 5.8 %collective-permute-start.52 = (bf16[128,2048]{1,0:T(8,128)(2,1)S(1)}, bf16[128,2048]{1,0:T(8,128)(2,1)S(1)}, u32[]{:S(2)}, u32[]{:S(2)}) collective-permute-start(bf16[128,2048]{1,0:T(8,128)(2,1)S(1)} %get-tuple-element.156), channel_id=1, source_target_pairs={{0,8},{24,16},{1,9},{25,17},{2,10},{26,18},{3,11},{27,19},{4,12},{... | collective-permute-start | bytes 1572872 | tf_op jit(solution)/shard_map/ppermute | solution.py:554
  236.8 2.3 collective-permute-done.44
  240.1 3.4 %collective-permute-start.45 = (bf16[128,2048]{1,0:T(8,128)(2,1)S(1)}, bf16[128,2048]{1,0:T(8,128)(2,1)S(1)}, u32[]{:S(2)}, u32[]{:S(2)}) collective-permute-start(bf16[128,2048]{1,0:T(8,128)(2,1)S(1)} %fusion.7), channel_id=1, source_target_pairs={{0,24},{24,0},{1,25},{25,1},{2,26},{26,2},{3,27},{27,3},{4,28},{28... | collective-permute-start | bytes 1572872 | tf_op jit(solution)/shard_map/ppermute | solution.py:557
  248.3 4.2 %collective-permute-done.48 = bf16[64,2048]{1,0:T(8,128)(2,1)S(1)} collective-permute-done((bf16[64,2048]{1,0:T(8,128)(2,1)S(1)}, bf16[64,2048]{1,0:T(8,128)(2,1)S(1)}, u32[]{:S(2)}, u32[]{:S(2)}) %collective-permute-start.48) | collective-permute-done | bytes 262176 | tf_op jit(solution)/shard_map/ppermute | solution.py:537
  256.1 4.7 %collective-permute-done.41 = bf16[64,2048]{1,0:T(8,128)(2,1)S(1)} collective-permute-done((bf16[64,2048]{1,0:T(8,128)(2,1)S(1)}, bf16[64,2048]{1,0:T(8,128)(2,1)S(1)}, u32[]{:S(2)}, u32[]{:S(2)}) %collective-permute-start.41) | collective-permute-done | bytes 262176 | tf_op jit(solution)/shard_map/ppermute | solution.py:537
  260.8 3.1 %collective-permute-start.49 = (bf16[128,2048]{1,0:T(8,128)(2,1)S(1)}, bf16[128,2048]{1,0:T(8,128)(2,1)S(1)}, u32[]{:S(2)}, u32[]{:S(2)}) collective-permute-start(bf16[128,2048]{1,0:T(8,128)(2,1)S(1)} %fusion.8), channel_id=1, source_target_pairs={{0,8},{8,0},{16,24},{24,16},{1,9},{9,1},{17,25},{25,17},{2,10},{10... | collective-permute-start | bytes 1572872 | tf_op jit(solution)/shard_map/ppermute | solution.py:561
  266.0 2.6 collective-permute-done.46
  268.6 11.1 %collective-permute-done.49 = bf16[128,2048]{1,0:T(8,128)(2,1)S(1)} collective-permute-done((bf16[128,2048]{1,0:T(8,128)(2,1)S(1)}, bf16[128,2048]{1,0:T(8,128)(2,1)S(1)}, u32[]{:S(2)}, u32[]{:S(2)}) %collective-permute-start.49) | collective-permute-done | bytes 524320 | tf_op jit(solution)/shard_map/ppermute | solution.py:561
  (252 shorter events, 85.7 us)
Async XLA Ops:
  7.2 92.1 %all-gather.3.cloned.1.call-start = ((), (), s32[]{:S(2)}) async-start(), calls=%async_computation | async-start | bytes 5242880 | tf_op jit(solution)/shard_map/all_gather | solution.py:611
  11.2 14.9 %collective-permute-start = (bf16[128,2048]{1,0:T(8,128)(2,1)S(1)}, bf16[128,2048]{1,0:T(8,128)(2,1)S(1)}, u32[]{:S(2)}, u32[]{:S(2)}) collective-permute-start(bf16[128,2048]{1,0:T(8,128)(2,1)S(1)} %get-tuple-element.86), channel_id=1, source_target_pairs={{0,2},{1,3},{2,0},{3,1},{4,6},{5,7},{6,4},{7,5},{8,10},{9,11},{10,... | collective-permute-start | bytes 1572872 | tf_op jit(solution)/shard_map/ppermute | solution.py:403
  14.1 13.4 %collective-permute-start.1 = (bf16[128,2048]{1,0:T(8,128)(2,1)S(1)}, bf16[128,2048]{1,0:T(8,128)(2,1)S(1)}, u32[]{:S(2)}, u32[]{:S(2)}) collective-permute-start(bf16[128,2048]{1,0:T(8,128)(2,1)S(1)} %get-tuple-element.86), channel_id=1, source_target_pairs={{0,4},{1,5},{2,6},{3,7},{4,0},{5,1},{6,2},{7,3},{8,12},{9,13},{10,... | collective-permute-start | bytes 1572872 | tf_op jit(solution)/shard_map/ppermute | solution.py:404
  37.4 18.1 %collective-permute-start.4 = (bf16[512,2048]{1,0:T(8,128)(2,1)}, bf16[512,2048]{1,0:T(8,128)(2,1)}, u32[]{:S(2)}, u32[]{:S(2)}) collective-permute-start(bf16[512,2048]{1,0:T(8,128)(2,1)} %constant_dynamic-update-slice_fusion.x_ref), channel_id=1, source_target_pairs={{0,1},{1,0},{2,3},{3,2},{4,5},{5,4},{6,7},{7,6},{8,9},{9,8},{10,11... | collective-permute-start | bytes 6291464 | tf_op jit(solution)/shard_map/ppermute | solution.py:409
  37.4 54.4 %collective-permute-start.10 = (f32[128,12]{0,1:T(8,128)S(1)}, f32[128,12]{0,1:T(8,128)S(1)}, u32[]{:S(2)}, u32[]{:S(2)}) collective-permute-start(f32[128,12]{0,1:T(8,128)S(1)} %get-tuple-element.152), channel_id=1, source_target_pairs={{0,16},{8,24},{16,0},{24,8},{1,17},{9,25},{17,1},{25,9},{2,18},{10... | collective-permute-start | bytes 18440 | tf_op jit(solution)/shard_map/ppermute | solution.py:465
  40.1 54.2 %collective-permute-start.11 = (f32[128,12]{0,1:T(8,128)S(1)}, f32[128,12]{0,1:T(8,128)S(1)}, u32[]{:S(2)}, u32[]{:S(2)}) collective-permute-start(f32[128,12]{0,1:T(8,128)S(1)} %get-tuple-element.152), channel_id=1, source_target_pairs={{0,24},{8,16},{16,8},{24,0},{1,25},{9,17},{17,9},{25,1},{2,26},{10... | collective-permute-start | bytes 18440 | tf_op jit(solution)/shard_map/ppermute | solution.py:465
  41.4 63.2 %collective-permute-start.9 = (f32[128,12]{0,1:T(8,128)S(1)}, f32[128,12]{0,1:T(8,128)S(1)}, u32[]{:S(2)}, u32[]{:S(2)}) collective-permute-start(f32[128,12]{0,1:T(8,128)S(1)} %get-tuple-element.152), channel_id=1, source_target_pairs={{0,8},{8,0},{16,24},{24,16},{1,9},{9,1},{17,25},{25,17},{2,10},{10... | collective-permute-start | bytes 18440 | tf_op jit(solution)/shard_map/ppermute | solution.py:465
  107.6 24.5 %collective-permute-start.15 = (bf16[128,2048]{1,0:T(8,128)(2,1)S(1)}, bf16[128,2048]{1,0:T(8,128)(2,1)S(1)}, u32[]{:S(2)}, u32[]{:S(2)}) collective-permute-start(bf16[128,2048]{1,0:T(8,128)(2,1)S(1)} %get-tuple-element.56), channel_id=1, source_target_pairs={{0,8},{8,0},{16,24},{24,16},{1,9},{9,1},{17,25},{25,17},{2,10},{10... | collective-permute-start | bytes 1572872 | tf_op jit(solution)/shard_map/ppermute | solution.py:480
  118.6 13.4 %collective-permute-start.13 = (bf16[64,2048]{1,0:T(8,128)(2,1)S(1)}, bf16[64,2048]{1,0:T(8,128)(2,1)S(1)}, u32[]{:S(2)}, u32[]{:S(2)}) collective-permute-start(bf16[64,2048]{1,0:T(8,128)(2,1)S(1)} %get-tuple-element.100), channel_id=1, source_target_pairs={{0,4},{1,5},{2,6},{3,7},{4,0},{5,1},{6,2},{7,3},{8,12},{9,13},{10,... | collective-permute-start | bytes 786440 | tf_op jit(solution)/shard_map/ppermute | solution.py:489
  119.2 12.9 %collective-permute-start.14 = (bf16[64,2048]{1,0:T(8,128)(2,1)S(1)}, bf16[64,2048]{1,0:T(8,128)(2,1)S(1)}, u32[]{:S(2)}, u32[]{:S(2)}) collective-permute-start(bf16[64,2048]{1,0:T(8,128)(2,1)S(1)} %get-tuple-element.99), channel_id=1, source_target_pairs={{0,6},{1,7},{2,4},{3,5},{4,2},{5,3},{6,0},{7,1},{8,14},{9,15},{10,... | collective-permute-start | bytes 786440 | tf_op jit(solution)/shard_map/ppermute | solution.py:489
  120.6 12.0 %collective-permute-start.16 = (bf16[128,2048]{1,0:T(8,128)(2,1)S(1)}, bf16[128,2048]{1,0:T(8,128)(2,1)S(1)}, u32[]{:S(2)}, u32[]{:S(2)}) collective-permute-start(bf16[128,2048]{1,0:T(8,128)(2,1)S(1)} %get-tuple-element.56), channel_id=1, source_target_pairs={{8,16},{16,8},{9,17},{17,9},{10,18},{18,10},{11,19},{19,11},{12,20... | collective-permute-start | bytes 1572872 | tf_op jit(solution)/shard_map/ppermute | solution.py:481
  132.6 15.1 %collective-permute-start.21 = (bf16[128,2048]{1,0:T(8,128)(2,1)S(1)}, bf16[128,2048]{1,0:T(8,128)(2,1)S(1)}, u32[]{:S(2)}, u32[]{:S(2)}) collective-permute-start(bf16[128,2048]{1,0:T(8,128)(2,1)S(1)} %collective-permute-done.16), channel_id=1, source_target_pairs={{8,0},{16,24},{9,1},{17,25},{10,2},{18,26},{11,3},{19,27},{12,4},{... | collective-permute-start | bytes 1572872 | tf_op jit(solution)/shard_map/ppermute | solution.py:482
  135.3 12.3 %collective-permute-start.19 = (bf16[64,2048]{1,0:T(8,128)(2,1)S(1)}, bf16[64,2048]{1,0:T(8,128)(2,1)S(1)}, u32[]{:S(2)}, u32[]{:S(2)}) collective-permute-start(bf16[64,2048]{1,0:T(8,128)(2,1)S(1)} %get-tuple-element.96), channel_id=1, source_target_pairs={{0,4},{1,5},{2,6},{3,7},{4,0},{5,1},{6,2},{7,3},{8,12},{9,13},{10,... | collective-permute-start | bytes 786440 | tf_op jit(solution)/shard_map/ppermute | solution.py:489
  136.5 11.1 %collective-permute-start.20 = (bf16[64,2048]{1,0:T(8,128)(2,1)S(1)}, bf16[64,2048]{1,0:T(8,128)(2,1)S(1)}, u32[]{:S(2)}, u32[]{:S(2)}) collective-permute-start(bf16[64,2048]{1,0:T(8,128)(2,1)S(1)} %get-tuple-element.95), channel_id=1, source_target_pairs={{0,6},{1,7},{2,4},{3,5},{4,2},{5,3},{6,0},{7,1},{8,14},{9,15},{10,... | collective-permute-start | bytes 786440 | tf_op jit(solution)/shard_map/ppermute | solution.py:489
  148.1 16.4 %collective-permute-start.27 = (bf16[128,2048]{1,0:T(8,128)(2,1)S(1)}, bf16[128,2048]{1,0:T(8,128)(2,1)S(1)}, u32[]{:S(2)}, u32[]{:S(2)}) collective-permute-start(bf16[128,2048]{1,0:T(8,128)(2,1)S(1)} %collective-permute-done.22), channel_id=1, source_target_pairs={{8,0},{16,24},{9,1},{17,25},{10,2},{18,26},{11,3},{19,27},{12,4},{... | collective-permute-start | bytes 1572872 | tf_op jit(solution)/shard_map/ppermute | solution.py:484
  151.5 11.5 %collective-permute-start.25 = (bf16[64,2048]{1,0:T(8,128)(2,1)S(1)}, bf16[64,2048]{1,0:T(8,128)(2,1)S(1)}, u32[]{:S(2)}, u32[]{:S(2)}) collective-permute-start(bf16[64,2048]{1,0:T(8,128)(2,1)S(1)} %get-tuple-element.92), channel_id=1, source_target_pairs={{0,4},{1,5},{2,6},{3,7},{4,0},{5,1},{6,2},{7,3},{8,12},{9,13},{10,... | collective-permute-start | bytes 786440 | tf_op jit(solution)/shard_map/ppermute | solution.py:489
  152.3 10.7 %collective-permute-start.26 = (bf16[64,2048]{1,0:T(8,128)(2,1)S(1)}, bf16[64,2048]{1,0:T(8,128)(2,1)S(1)}, u32[]{:S(2)}, u32[]{:S(2)}) collective-permute-start(bf16[64,2048]{1,0:T(8,128)(2,1)S(1)} %get-tuple-element.91), channel_id=1, source_target_pairs={{0,6},{1,7},{2,4},{3,5},{4,2},{5,3},{6,0},{7,1},{8,14},{9,15},{10,... | collective-permute-start | bytes 786440 | tf_op jit(solution)/shard_map/ppermute | solution.py:489
  213.7 14.6 %collective-permute-start.50 = (bf16[64,2048]{1,0:T(8,128)(2,1)S(1)}, bf16[64,2048]{1,0:T(8,128)(2,1)S(1)}, u32[]{:S(2)}, u32[]{:S(2)}) collective-permute-start(bf16[64,2048]{1,0:T(8,128)(2,1)S(1)} %pad_maximum_fusion.20), channel_id=1, source_target_pairs={{0,4},{1,5},{2,6},{3,7},{4,0},{5,1},{6,2},{7,3},{8,12},{9,13},{10,... | collective-permute-start | bytes 786440 | tf_op jit(solution)/shard_map/ppermute | solution.py:537
  215.0 12.8 %collective-permute-start.51 = (bf16[64,2048]{1,0:T(8,128)(2,1)S(1)}, bf16[64,2048]{1,0:T(8,128)(2,1)S(1)}, u32[]{:S(2)}, u32[]{:S(2)}) collective-permute-start(bf16[64,2048]{1,0:T(8,128)(2,1)S(1)} %pad_maximum_fusion.21), channel_id=1, source_target_pairs={{0,6},{1,7},{2,4},{3,5},{4,2},{5,3},{6,0},{7,1},{8,14},{9,15},{10,... | collective-permute-start | bytes 786440 | tf_op jit(solution)/shard_map/ppermute | solution.py:537
  222.2 12.2 %collective-permute-start.38 = (bf16[64,2048]{1,0:T(8,128)(2,1)S(1)}, bf16[64,2048]{1,0:T(8,128)(2,1)S(1)}, u32[]{:S(2)}, u32[]{:S(2)}) collective-permute-start(bf16[64,2048]{1,0:T(8,128)(2,1)S(1)} %pad_maximum_fusion.16), channel_id=1, source_target_pairs={{0,2},{1,3},{2,0},{3,1},{4,6},{5,7},{6,4},{7,5},{8,10},{9,11},{10,... | collective-permute-start | bytes 786440 | tf_op jit(solution)/shard_map/ppermute | solution.py:537
  222.8 16.4 %collective-permute-start.44 = (bf16[64,2048]{1,0:T(8,128)(2,1)S(1)}, bf16[64,2048]{1,0:T(8,128)(2,1)S(1)}, u32[]{:S(2)}, u32[]{:S(2)}) collective-permute-start(bf16[64,2048]{1,0:T(8,128)(2,1)S(1)} %pad_maximum_fusion.18), channel_id=1, source_target_pairs={{0,6},{1,7},{2,4},{3,5},{4,2},{5,3},{6,0},{7,1},{8,14},{9,15},{10,... | collective-permute-start | bytes 786440 | tf_op jit(solution)/shard_map/ppermute | solution.py:537
  224.3 15.2 %collective-permute-start.43 = (bf16[64,2048]{1,0:T(8,128)(2,1)S(1)}, bf16[64,2048]{1,0:T(8,128)(2,1)S(1)}, u32[]{:S(2)}, u32[]{:S(2)}) collective-permute-start(bf16[64,2048]{1,0:T(8,128)(2,1)S(1)} %pad_maximum_fusion.17), channel_id=1, source_target_pairs={{0,4},{1,5},{2,6},{3,7},{4,0},{5,1},{6,2},{7,3},{8,12},{9,13},{10,... | collective-permute-start | bytes 786440 | tf_op jit(solution)/shard_map/ppermute | solution.py:537
  228.6 25.4 %collective-permute-start.52 = (bf16[128,2048]{1,0:T(8,128)(2,1)S(1)}, bf16[128,2048]{1,0:T(8,128)(2,1)S(1)}, u32[]{:S(2)}, u32[]{:S(2)}) collective-permute-start(bf16[128,2048]{1,0:T(8,128)(2,1)S(1)} %get-tuple-element.156), channel_id=1, source_target_pairs={{0,8},{24,16},{1,9},{25,17},{2,10},{26,18},{3,11},{27,19},{4,12},{... | collective-permute-start | bytes 1572872 | tf_op jit(solution)/shard_map/ppermute | solution.py:554
  234.4 10.5 %collective-permute-start.39 = (bf16[64,2048]{1,0:T(8,128)(2,1)S(1)}, bf16[64,2048]{1,0:T(8,128)(2,1)S(1)}, u32[]{:S(2)}, u32[]{:S(2)}) collective-permute-start(bf16[64,2048]{1,0:T(8,128)(2,1)S(1)} %pad_maximum_fusion.12), channel_id=1, source_target_pairs={{0,2},{1,3},{2,0},{3,1},{4,6},{5,7},{6,4},{7,5},{8,10},{9,11},{10,... | collective-permute-start | bytes 786440 | tf_op jit(solution)/shard_map/ppermute | solution.py:537
  234.9 11.8 %collective-permute-start.47 = (bf16[64,2048]{1,0:T(8,128)(2,1)S(1)}, bf16[64,2048]{1,0:T(8,128)(2,1)S(1)}, u32[]{:S(2)}, u32[]{:S(2)}) collective-permute-start(bf16[64,2048]{1,0:T(8,128)(2,1)S(1)} %pad_maximum_fusion.13), channel_id=1, source_target_pairs={{0,4},{1,5},{2,6},{3,7},{4,0},{5,1},{6,2},{7,3},{8,12},{9,13},{10,... | collective-permute-start | bytes 786440 | tf_op jit(solution)/shard_map/ppermute | solution.py:537
  240.1 25.8 %collective-permute-start.45 = (bf16[128,2048]{1,0:T(8,128)(2,1)S(1)}, bf16[128,2048]{1,0:T(8,128)(2,1)S(1)}, u32[]{:S(2)}, u32[]{:S(2)}) collective-permute-start(bf16[128,2048]{1,0:T(8,128)(2,1)S(1)} %fusion.7), channel_id=1, source_target_pairs={{0,24},{24,0},{1,25},{25,1},{2,26},{26,2},{3,27},{27,3},{4,28},{28... | collective-permute-start | bytes 1572872 | tf_op jit(solution)/shard_map/ppermute | solution.py:557
  243.6 25.0 %collective-permute-start.46 = (bf16[128,2048]{1,0:T(8,128)(2,1)S(1)}, bf16[128,2048]{1,0:T(8,128)(2,1)S(1)}, u32[]{:S(2)}, u32[]{:S(2)}) collective-permute-start(bf16[128,2048]{1,0:T(8,128)(2,1)S(1)} %fusion.7), channel_id=1, source_target_pairs={{8,24},{16,0},{9,25},{17,1},{10,26},{18,2},{11,27},{19,3},{12,28},... | collective-permute-start | bytes 1572872 | tf_op jit(solution)/shard_map/ppermute | solution.py:558
  246.7 14.1 %collective-permute-start.41 = (bf16[64,2048]{1,0:T(8,128)(2,1)S(1)}, bf16[64,2048]{1,0:T(8,128)(2,1)S(1)}, u32[]{:S(2)}, u32[]{:S(2)}) collective-permute-start(bf16[64,2048]{1,0:T(8,128)(2,1)S(1)} %pad_maximum_fusion.9), channel_id=1, source_target_pairs={{0,4},{1,5},{2,6},{3,7},{4,0},{5,1},{6,2},{7,3},{8,12},{9,13},{10,... | collective-permute-start | bytes 786440 | tf_op jit(solution)/shard_map/ppermute | solution.py:537
  252.5 11.8 %collective-permute-start.40 = (bf16[64,2048]{1,0:T(8,128)(2,1)S(1)}, bf16[64,2048]{1,0:T(8,128)(2,1)S(1)}, u32[]{:S(2)}, u32[]{:S(2)}) collective-permute-start(bf16[64,2048]{1,0:T(8,128)(2,1)S(1)} %pad_maximum_fusion.8), channel_id=1, source_target_pairs={{0,2},{1,3},{2,0},{3,1},{4,6},{5,7},{6,4},{7,5},{8,10},{9,11},{10,... | collective-permute-start | bytes 786440 | tf_op jit(solution)/shard_map/ppermute | solution.py:537
  253.9 11.4 %collective-permute-start.42 = (bf16[64,2048]{1,0:T(8,128)(2,1)S(1)}, bf16[64,2048]{1,0:T(8,128)(2,1)S(1)}, u32[]{:S(2)}, u32[]{:S(2)}) collective-permute-start(bf16[64,2048]{1,0:T(8,128)(2,1)S(1)} %pad_maximum_fusion.10), channel_id=1, source_target_pairs={{0,6},{1,7},{2,4},{3,5},{4,2},{5,3},{6,0},{7,1},{8,14},{9,15},{10,... | collective-permute-start | bytes 786440 | tf_op jit(solution)/shard_map/ppermute | solution.py:537
  260.8 18.8 %collective-permute-start.49 = (bf16[128,2048]{1,0:T(8,128)(2,1)S(1)}, bf16[128,2048]{1,0:T(8,128)(2,1)S(1)}, u32[]{:S(2)}, u32[]{:S(2)}) collective-permute-start(bf16[128,2048]{1,0:T(8,128)(2,1)S(1)} %fusion.8), channel_id=1, source_target_pairs={{0,8},{8,0},{16,24},{24,16},{1,9},{9,1},{17,25},{25,17},{2,10},{10... | collective-permute-start | bytes 1572872 | tf_op jit(solution)/shard_map/ppermute | solution.py:561
  264.3 15.4 %collective-permute-start.53 = (bf16[128,2048]{1,0:T(8,128)(2,1)S(1)}, bf16[128,2048]{1,0:T(8,128)(2,1)S(1)}, u32[]{:S(2)}, u32[]{:S(2)}) collective-permute-start(bf16[128,2048]{1,0:T(8,128)(2,1)S(1)} %add_convert_fusion.1), channel_id=1, source_target_pairs={{8,16},{16,8},{9,17},{17,9},{10,18},{18,10},{11,19},{19,11},{12,20... | collective-permute-start | bytes 1572872 | tf_op jit(solution)/shard_map/ppermute | solution.py:560
  (52 other events, 268.0 us)
Sparse Core Ops, SparseCore 0:
  27.6 53.0 all-gather.2
